TPU v7x, 32 devices: a whole 2x2x4 slice. The times are simulated.
32 devices in a mesh: seq: 2 (over core), dp: 16 (over z, y, x).
Axes of the slice: x: 2, y: 2, z: 4, core: 2. Of those that a mesh axis runs over, the one named last changes fastest.
Arguments:
- tokens: bfloat16 [16, 1536, 768], P('dp', 'seq'), may hold values from -6 to 6
- time_embed: float32 [16, 768], P('dp'), may hold values from -4 to 4
- segments: int32 [16, 1536], P('dp'), may hold values from 0 to 3, never falling along the last dimension, each value on 1 to 768 neighbouring positions
- input_weight: bfloat16 [768, 2304], P('dp'), may hold values from -0.3125 to 0.3125
- query_bias: bfloat16 [768], P('dp'), may hold values from -3 to 3
- value_bias: bfloat16 [768], P('dp'), may hold values from -2 to 2
- output_weight: bfloat16 [768, 768], P('dp'), may hold values from -0.875 to 0.875
- output_bias: bfloat16 [768], P('dp'), may hold values from -2 to 2
- first_gain: bfloat16 [768], P('dp'), may hold values from 0.5 to 1.5
- first_shift: bfloat16 [768], P('dp'), may hold values from -2 to 2
- expand_weight: bfloat16 [768, 3072], P('dp'), may hold values from -0.21875 to 0.21875
- expand_bias: bfloat16 [3072], P('dp'), may hold values from -3 to 3
- contract_weight: bfloat16 [3072, 768], P('dp'), may hold values from -0.15625 to 0.15625
- contract_bias: bfloat16 [768], P('dp'), may hold values from -2 to 2
- second_gain: bfloat16 [768], P('dp'), may hold values from 0.5 to 1.5
- second_shift: bfloat16 [768], P('dp'), may hold values from -2 to 2
- cotangent: bfloat16 [16, 1536, 768], P('dp', 'seq'), may hold values from -6 to 6
Outputs:
- layer_output: bfloat16 [16, 1536, 768], P('dp', 'seq')
- input_grad: float32 [16, 1536, 768], P('dp', 'seq')
- grad_input_weight: float32 [768, 2304], P('dp')
- grad_query_bias: float32 [768], P('dp')
- grad_value_bias: float32 [768], P('dp')
- grad_output_weight: float32 [768, 768], P('dp')
- grad_output_bias: float32 [768], P('dp')
- grad_first_gain: float32 [768], P('dp')
- grad_first_shift: float32 [768], P('dp')
- grad_expand_weight: float32 [768, 3072], P('dp')
- grad_expand_bias: float32 [3072], P('dp')
- grad_contract_weight: float32 [3072, 768], P('dp')
- grad_contract_bias: float32 [768], P('dp')
- grad_second_gain: float32 [768], P('dp')
- grad_second_shift: float32 [768], P('dp')
Inputs may be any that keep to these rules, and one draw needn't show every extreme that they name: `segments`: within each sequence segment numbers start at 0 and never fall; each of the 4 documents has 1 to 768 tokens and one has exactly 768.
All inputs are finite; a program needn't handle non-finite values.
Results may differ from a plain program's by a relative error of at most 0.017.
The roundings to bfloat16 on the way count: a program that leaves them out, or rounds other values in their place, can miss the bound.
Values may be sent and summed in bfloat16 or wider, within the bound.
A program may use at most 192 MiB of HBM per device.

v0:
```python
import math

import jax
import jax.numpy as jnp
from jax import lax
from jax.sharding import PartitionSpec as P

HD = 64


epsilon = 1e-05
masked_score = -1e30


def matmul(left, right):
    return jnp.dot(left, right, preferred_element_type=jnp.float32)


def product_tn(left, right):
    return lax.dot_general(
        left, right, (((0,), (0,)), ((), ())), preferred_element_type=jnp.float32
    )


def product_nt(left, right):
    return lax.dot_general(
        left, right, (((1,), (1,)), ((), ())), preferred_element_type=jnp.float32
    )


def normalize(values):
    mean = jnp.mean(values, axis=-1, keepdims=True)
    centred = values - mean
    scale = lax.rsqrt(jnp.mean(centred * centred, axis=-1, keepdims=True) + epsilon)
    return (centred * scale, scale)


def norm_back(grad, normed, scale, gain):
    scaled = grad * gain
    return scale * (
        scaled
        - jnp.mean(scaled, axis=-1, keepdims=True)
        - normed * jnp.mean(scaled * normed, axis=-1, keepdims=True)
    )


def gelu_value(values):
    return 0.5 * values * (1.0 + lax.erf(values * math.sqrt(0.5)))


def gelu_slope(values):
    return 0.5 * (1.0 + lax.erf(values * math.sqrt(0.5))) + values * jnp.exp(
        -0.5 * values * values
    ) / math.sqrt(2.0 * math.pi)


def attend_forward(item):
    query, key, value, segment_row = item
    length, depth = query.shape
    block = min(512, length)
    blocks = length // block
    scale = depth ** (-0.5)

    def one_block(part):
        query_block, segment_block = part
        scores = product_nt(query_block, key) * scale
        scores = jnp.where(segment_block[:, None] == segment_row[None, :], scores, masked_score)
        top = jnp.max(scores, axis=-1, keepdims=True)
        expo = jnp.exp(scores - top)
        total = jnp.sum(expo, axis=-1, keepdims=True)
        probs_low = (expo / total).astype(jnp.bfloat16)
        return (matmul(probs_low, value).astype(jnp.bfloat16), (top + jnp.log(total))[:, 0])

    outputs, logsum = lax.map(
        one_block, (query.reshape(blocks, block, depth), segment_row.reshape(blocks, block))
    )
    return (outputs.reshape(length, depth), logsum.reshape(length))


def attend_backward(item):
    query, key, value, segment_row, logsum, out_grad = item
    length, depth = query.shape
    block = min(512, length)
    blocks = length // block
    scale = depth ** (-0.5)

    def one_block(carry, part):
        key_grad, value_grad = carry
        query_block, segment_block, logsum_block, grad_block = part
        scores = product_nt(query_block, key) * scale
        scores = jnp.where(segment_block[:, None] == segment_row[None, :], scores, masked_score)
        probs = jnp.exp(scores - logsum_block[:, None])
        probs_low = probs.astype(jnp.bfloat16)
        prob_grad = product_nt(grad_block, value)
        row_total = jnp.sum(probs * prob_grad, axis=-1, keepdims=True)
        score_grad = (probs * (prob_grad - row_total)).astype(jnp.bfloat16)
        query_grad = matmul(score_grad, key) * scale
        key_grad = key_grad + product_tn(score_grad, query_block) * scale
        value_grad = value_grad + product_tn(probs_low, grad_block)
        return ((key_grad, value_grad), query_grad.astype(jnp.bfloat16))

    zeros = jnp.zeros((length, depth), jnp.float32)
    parts = (
        query.reshape(blocks, block, depth),
        segment_row.reshape(blocks, block),
        logsum.reshape(blocks, block),
        out_grad.reshape(blocks, block, depth),
    )
    (key_grad, value_grad), query_grad = lax.scan(one_block, (zeros, zeros), parts)
    return (
        query_grad.reshape(length, depth),
        key_grad.astype(jnp.bfloat16),
        value_grad.astype(jnp.bfloat16),
    )


def body(
    tokens,
    time_embed,
    segments,
    input_weight,
    query_bias,
    value_bias,
    output_weight,
    output_bias,
    first_gain,
    first_shift,
    expand_weight,
    expand_bias,
    contract_weight,
    contract_bias,
    second_gain,
    second_shift,
    cotangent,
):
    pairs = lax.axis_size("seq")
    seqs, half, width = tokens.shape
    length = half * pairs
    rows = seqs * half
    group = width // pairs
    heads_here = group // HD
    start = (tokens.astype(jnp.float32) + time_embed[:, None, :]).reshape(rows, width)
    start_low = start.astype(jnp.bfloat16)
    attention_set = (
        lax.all_gather(input_weight, "dp", axis=0, tiled=True),
        lax.all_gather(output_weight, "dp", axis=0, tiled=True),
        lax.all_gather(query_bias, "dp", axis=0, tiled=True),
        lax.all_gather(value_bias, "dp", axis=0, tiled=True),
        lax.all_gather(output_bias, "dp", axis=0, tiled=True),
        lax.all_gather(first_gain, "dp", axis=0, tiled=True),
        lax.all_gather(first_shift, "dp", axis=0, tiled=True),
    )
    (
        full_input,
        full_output,
        full_query_bias,
        full_value_bias,
        full_output_bias,
        full_first_gain,
        full_first_shift,
    ) = attention_set
    bias_row = jnp.concatenate(
        [
            full_query_bias.astype(jnp.float32),
            jnp.zeros((width,), jnp.float32),
            full_value_bias.astype(jnp.float32),
        ]
    )
    projected_low = (matmul(start_low, full_input) + bias_row).astype(jnp.bfloat16)
    regrouped = lax.all_to_all(
        projected_low.reshape(seqs, half, 3, pairs, group),
        "seq",
        split_axis=3,
        concat_axis=1,
        tiled=True,
    )
    split = regrouped.reshape(seqs, length, 3, heads_here, HD).transpose(2, 0, 3, 1, 4)
    split = split.reshape(3, seqs * heads_here, length, HD)
    query_heads, key_heads, value_heads = (split[0], split[1], split[2])
    segment_heads = jnp.repeat(segments, heads_here, axis=0)
    heads_out, logsum = lax.map(
        attend_forward, (query_heads, key_heads, value_heads, segment_heads)
    )
    heads_tokens = (
        heads_out.reshape(seqs, heads_here, length, HD)
        .transpose(0, 2, 1, 3)
        .reshape(seqs, length, 1, group)
    )
    heads_low = lax.all_to_all(
        heads_tokens, "seq", split_axis=1, concat_axis=2, tiled=True
    ).reshape(rows, width)
    attention = matmul(heads_low, full_output) + full_output_bias.astype(jnp.float32)
    normed_one, scale_one = normalize(start + attention)
    gain_one = full_first_gain.astype(jnp.float32)
    first = normed_one * gain_one + full_first_shift.astype(jnp.float32)
    first_low = first.astype(jnp.bfloat16)
    network_set = (
        lax.all_gather(expand_weight, "dp", axis=0, tiled=True),
        lax.all_gather(contract_weight, "dp", axis=0, tiled=True),
        lax.all_gather(expand_bias, "dp", axis=0, tiled=True),
        lax.all_gather(contract_bias, "dp", axis=0, tiled=True),
        lax.all_gather(second_gain, "dp", axis=0, tiled=True),
        lax.all_gather(second_shift, "dp", axis=0, tiled=True),
    )
    (
        full_expand,
        full_contract,
        full_expand_bias,
        full_contract_bias,
        full_second_gain,
        full_second_shift,
    ) = network_set
    expand = matmul(first_low, full_expand) + full_expand_bias.astype(jnp.float32)
    hidden = gelu_value(expand).astype(jnp.bfloat16)
    second_sum = first + matmul(hidden, full_contract) + full_contract_bias.astype(jnp.float32)
    normed_two, scale_two = normalize(second_sum)
    gain_two = full_second_gain.astype(jnp.float32)
    layer_output = (normed_two * gain_two + full_second_shift.astype(jnp.float32)).astype(
        jnp.bfloat16
    )
    network_set = (
        lax.all_gather(expand_weight, "dp", axis=0, tiled=True),
        lax.all_gather(contract_weight, "dp", axis=0, tiled=True),
        lax.all_gather(expand_bias, "dp", axis=0, tiled=True),
        lax.all_gather(contract_bias, "dp", axis=0, tiled=True),
        lax.all_gather(second_gain, "dp", axis=0, tiled=True),
        lax.all_gather(second_shift, "dp", axis=0, tiled=True),
    )
    full_expand, full_contract = (network_set[0], network_set[1])
    out_grad = cotangent.astype(jnp.float32).reshape(rows, width)
    grad_second_gain = jnp.sum(out_grad * normed_two, axis=0)
    grad_second_shift = jnp.sum(out_grad, axis=0)
    second_grad = norm_back(out_grad, normed_two, scale_two, gain_two)
    branch_grad = second_grad.astype(jnp.bfloat16)
    grad_contract_bias = jnp.sum(branch_grad.astype(jnp.float32), axis=0)
    grad_contract_weight = product_tn(hidden, branch_grad)
    expand_grad = (product_nt(branch_grad, full_contract) * gelu_slope(expand)).astype(jnp.bfloat16)
    grad_expand_bias = jnp.sum(expand_grad.astype(jnp.float32), axis=0)
    grad_expand_weight = product_tn(first_low, expand_grad)
    first_grad = second_grad + product_nt(expand_grad, full_expand)
    grad_first_gain = jnp.sum(first_grad * normed_one, axis=0)
    grad_first_shift = jnp.sum(first_grad, axis=0)
    start_grad = norm_back(first_grad, normed_one, scale_one, gain_one)
    attention_set = (
        lax.all_gather(input_weight, "dp", axis=0, tiled=True),
        lax.all_gather(output_weight, "dp", axis=0, tiled=True),
        lax.all_gather(query_bias, "dp", axis=0, tiled=True),
        lax.all_gather(value_bias, "dp", axis=0, tiled=True),
        lax.all_gather(output_bias, "dp", axis=0, tiled=True),
        lax.all_gather(first_gain, "dp", axis=0, tiled=True),
        lax.all_gather(first_shift, "dp", axis=0, tiled=True),
    )
    full_input, full_output = (attention_set[0], attention_set[1])
    attention_grad = start_grad.astype(jnp.bfloat16)
    grad_output_bias = jnp.sum(attention_grad.astype(jnp.float32), axis=0)
    grad_output_weight = product_tn(heads_low, attention_grad)
    heads_grad = product_nt(attention_grad, full_output).astype(jnp.bfloat16)
    grad_heads = lax.all_to_all(
        heads_grad.reshape(seqs, half, pairs, group), "seq", split_axis=2, concat_axis=1, tiled=True
    )
    grad_heads = (
        grad_heads.reshape(seqs, length, heads_here, HD)
        .transpose(0, 2, 1, 3)
        .reshape(seqs * heads_here, length, HD)
    )
    query_grad, key_grad, value_grad = lax.map(
        attend_backward, (query_heads, key_heads, value_heads, segment_heads, logsum, grad_heads)
    )
    stacked = jnp.stack([query_grad, key_grad, value_grad]).reshape(3, seqs, heads_here, length, HD)
    stacked = stacked.transpose(1, 3, 0, 2, 4).reshape(seqs, length, 3, 1, group)
    projected_grad = lax.all_to_all(
        stacked, "seq", split_axis=1, concat_axis=3, tiled=True
    ).reshape(rows, 3 * width)
    grad_query_bias = jnp.sum(projected_grad[:, :width].astype(jnp.float32), axis=0)
    grad_value_bias = jnp.sum(projected_grad[:, 2 * width :].astype(jnp.float32), axis=0)
    grad_input_weight = product_tn(start_low, projected_grad)
    input_grad = (start_grad + product_nt(projected_grad, full_input)).reshape(seqs, half, width)
    grads = (
        grad_input_weight,
        grad_query_bias,
        grad_value_bias,
        grad_output_weight,
        grad_output_bias,
        grad_first_gain,
        grad_first_shift,
        grad_expand_weight,
        grad_expand_bias,
        grad_contract_weight,
        grad_contract_bias,
        grad_second_gain,
        grad_second_shift,
    )
    owned = (
        lax.psum_scatter(grads[0], "dp", scatter_dimension=0, tiled=True),
        lax.psum_scatter(grads[1], "dp", scatter_dimension=0, tiled=True),
        lax.psum_scatter(grads[2], "dp", scatter_dimension=0, tiled=True),
        lax.psum_scatter(grads[3], "dp", scatter_dimension=0, tiled=True),
        lax.psum_scatter(grads[4], "dp", scatter_dimension=0, tiled=True),
        lax.psum_scatter(grads[5], "dp", scatter_dimension=0, tiled=True),
        lax.psum_scatter(grads[6], "dp", scatter_dimension=0, tiled=True),
        lax.psum_scatter(grads[7], "dp", scatter_dimension=0, tiled=True),
        lax.psum_scatter(grads[8], "dp", scatter_dimension=0, tiled=True),
        lax.psum_scatter(grads[9], "dp", scatter_dimension=0, tiled=True),
        lax.psum_scatter(grads[10], "dp", scatter_dimension=0, tiled=True),
        lax.psum_scatter(grads[11], "dp", scatter_dimension=0, tiled=True),
        lax.psum_scatter(grads[12], "dp", scatter_dimension=0, tiled=True),
    )
    summed = (
        lax.psum(owned[0].astype(jnp.bfloat16), "seq").astype(jnp.float32),
        lax.psum(owned[1].astype(jnp.bfloat16), "seq").astype(jnp.float32),
        lax.psum(owned[2].astype(jnp.bfloat16), "seq").astype(jnp.float32),
        lax.psum(owned[3].astype(jnp.bfloat16), "seq").astype(jnp.float32),
        lax.psum(owned[4].astype(jnp.bfloat16), "seq").astype(jnp.float32),
        lax.psum(owned[5].astype(jnp.bfloat16), "seq").astype(jnp.float32),
        lax.psum(owned[6].astype(jnp.bfloat16), "seq").astype(jnp.float32),
        lax.psum(owned[7].astype(jnp.bfloat16), "seq").astype(jnp.float32),
        lax.psum(owned[8].astype(jnp.bfloat16), "seq").astype(jnp.float32),
        lax.psum(owned[9].astype(jnp.bfloat16), "seq").astype(jnp.float32),
        lax.psum(owned[10].astype(jnp.bfloat16), "seq").astype(jnp.float32),
        lax.psum(owned[11].astype(jnp.bfloat16), "seq").astype(jnp.float32),
        lax.psum(owned[12].astype(jnp.bfloat16), "seq").astype(jnp.float32),
    )
    return (layer_output.reshape(seqs, half, width), input_grad) + tuple(summed)


def solution(mesh):
    return jax.shard_map(
        body,
        mesh=mesh,
        in_specs=(
            P("dp", "seq", None),
            P("dp", None),
            P("dp", None),
            P("dp", None),
            P("dp"),
            P("dp"),
            P("dp", None),
            P("dp"),
            P("dp"),
            P("dp"),
            P("dp", None),
            P("dp"),
            P("dp", None),
            P("dp"),
            P("dp"),
            P("dp"),
            P("dp", "seq", None),
        ),
        out_specs=(
            P("dp", "seq", None),
            P("dp", "seq", None),
            P("dp", None),
            P("dp"),
            P("dp"),
            P("dp", None),
            P("dp"),
            P("dp"),
            P("dp"),
            P("dp", None),
            P("dp"),
            P("dp", None),
            P("dp"),
            P("dp"),
            P("dp"),
        ),
        check_vma=False,
    )
```

profile of v0, /device:TPU:0, one launch (start us, length us, event | category | flops | bytes accessed | tf_op | source)
XLA Modules:
  0.0 1275.7 jit_solution(2705987269619123851)
XLA Ops:
  16.6 79.2 %all-reduce.19 = (bf16[768]{0:T(1024)(128)(2,1)S(1)}, bf16[768]{0:T(1024)(128)(2,1)S(1)}, bf16[768]{0:T(1024)(128)(2,1)S(1)}, bf16[768]{0:T(1024)(128)(2,1)S(1)}...) all-reduce(bf16[768]{0:T(1024)(128)(2,1)S(1)} %dynamic-update-slice, ...), channel_id=1, replica_groups=mesh['seq'=2,'dp'=16] {'dp'}, use_global_device_ids=true, to_apply=%add.1 | all-reduce | flops 9216 | bytes 36864
  101.4 6.6 add_convert_fusion
  107.9 6.5 reshape.205
  114.4 9.3 copy.123
  123.7 8.4 all_to_all.60
  132.1 5.4 copy.124
  137.5 7.5 reshape.206
  146.8 3.8 copy.125
  156.1 70.1 %while.54 = (s32[]{:T(128)}, bf16[6,1536,64]{1,2,0:T(8,128)(2,1)S(1)}, f32[6,1536]{1,0:T(8,128)}, bf16[6,1536,64]{2,1,0:T(8,128)(2,1)}, s32[6,1536]{1,0:T(8,128)...) while((s32[]{:T(128)}, ...), condition=%wide.region_5.6_spmd, body=%wide.region_0.5_spmd.sunk | while | flops 208436736 | bytes 12863838 | solution.py:181
  159.2 6.7 while.57
  170.9 6.7 while.57
  182.6 6.7 while.57
  194.2 6.7 while.57
  205.9 6.7 while.57
  217.6 6.7 while.57
  226.2 3.3 copy.129
  230.0 9.1 reduce.11
  239.5 4.8 all_to_all.61
  247.0 3.2 fusion.64
  251.1 10.3 multiply_convert_fusion.1
  261.4 45.7 %all-gather.11.cloned.1.call-done = bf16[3072,768]{1,0:T(8,128)(2,1)} async-done(((bf16[192,768]{1,0:T(8,128)(2,1)}), bf16[3072,768]{1,0:T(8,128)(2,1)}) %all-gather.11.cloned.1.call-update) | async-done | bytes 4718608 | tf_op jit(solution)/shard_map/all_gather | solution.py:199
  307.1 7.6 fusion.65
  317.6 2.6 convert_reduce_fusion.2
  320.3 10.7 convert_reduce_fusion
  331.0 5.6 multiply_reduce_fusion.1
  342.1 2.7 convolution_convert_fusion
  344.9 4.7 all_to_all.62
  355.1 279.2 %while.56 = (s32[]{:T(128)}, bf16[6,1536,64]{1,2,0:T(8,128)(2,1)}, bf16[6,1536,64]{1,2,0:T(8,128)(2,1)}, bf16[6,1536,64]{1,2,0:T(8,128)(2,1)}, bf16[6,1536,64]{2...) while((s32[]{:T(128)}, bf16[6,1536,64]{1,2,0:T(8,128)(2,1)}, ...), condition=%wide.region_18.19_spmd, body=%wide.region_14.18_spmd.sunk | while | flops 511933952 | bytes 51386988 | solution.py:266
  362.3 35.1 %while.58 = (s32[]{:T(128)}, f32[1536,64]{0,1:T(8,128)}, f32[1536,64]{0,1:T(8,128)}, bf16[3,512,64]{1,2,0:T(8,128)(2,1)}, s32[3,512]{1,0:T(4,128)S(1)}, /*index=...) while((s32[]{:T(128)}, f32[1536,64]{0,1:T(8,128)}, ...), condition=%wide.region_17.17_spmd.clone, body=%wide.region_15.16_spmd.clone.sunk | while | flops 511737344 | bytes 36002044 | solution.py:109
  368.5 2.6 fusion.119
  380.1 2.8 fusion.119
  391.8 2.8 fusion.119
  408.9 35.0 %while.58 = (s32[]{:T(128)}, f32[1536,64]{0,1:T(8,128)}, f32[1536,64]{0,1:T(8,128)}, bf16[3,512,64]{1,2,0:T(8,128)(2,1)}, s32[3,512]{1,0:T(4,128)S(1)}, /*index=...) while((s32[]{:T(128)}, f32[1536,64]{0,1:T(8,128)}, ...), condition=%wide.region_17.17_spmd.clone, body=%wide.region_15.16_spmd.clone.sunk | while | flops 511737344 | bytes 36002044 | solution.py:109
  415.1 2.6 fusion.119
  426.7 2.7 fusion.119
  438.4 2.7 fusion.119
  455.4 35.0 %while.58 = (s32[]{:T(128)}, f32[1536,64]{0,1:T(8,128)}, f32[1536,64]{0,1:T(8,128)}, bf16[3,512,64]{1,2,0:T(8,128)(2,1)}, s32[3,512]{1,0:T(4,128)S(1)}, /*index=...) while((s32[]{:T(128)}, f32[1536,64]{0,1:T(8,128)}, ...), condition=%wide.region_17.17_spmd.clone, body=%wide.region_15.16_spmd.clone.sunk | while | flops 511737344 | bytes 36002044 | solution.py:109
  461.6 2.6 fusion.119
  473.2 2.8 fusion.119
  484.9 2.7 fusion.119
  501.9 35.0 %while.58 = (s32[]{:T(128)}, f32[1536,64]{0,1:T(8,128)}, f32[1536,64]{0,1:T(8,128)}, bf16[3,512,64]{1,2,0:T(8,128)(2,1)}, s32[3,512]{1,0:T(4,128)S(1)}, /*index=...) while((s32[]{:T(128)}, f32[1536,64]{0,1:T(8,128)}, ...), condition=%wide.region_17.17_spmd.clone, body=%wide.region_15.16_spmd.clone.sunk | while | flops 511737344 | bytes 36002044 | solution.py:109
  508.1 2.6 fusion.119
  519.7 2.7 fusion.119
  531.4 2.7 fusion.119
  548.3 35.0 %while.58 = (s32[]{:T(128)}, f32[1536,64]{0,1:T(8,128)}, f32[1536,64]{0,1:T(8,128)}, bf16[3,512,64]{1,2,0:T(8,128)(2,1)}, s32[3,512]{1,0:T(4,128)S(1)}, /*index=...) while((s32[]{:T(128)}, f32[1536,64]{0,1:T(8,128)}, ...), condition=%wide.region_17.17_spmd.clone, body=%wide.region_15.16_spmd.clone.sunk | while | flops 511737344 | bytes 36002044 | solution.py:109
  554.5 2.6 fusion.119
  566.1 2.7 fusion.119
  577.8 2.7 fusion.119
  594.8 35.0 %while.58 = (s32[]{:T(128)}, f32[1536,64]{0,1:T(8,128)}, f32[1536,64]{0,1:T(8,128)}, bf16[3,512,64]{1,2,0:T(8,128)(2,1)}, s32[3,512]{1,0:T(4,128)S(1)}, /*index=...) while((s32[]{:T(128)}, f32[1536,64]{0,1:T(8,128)}, ...), condition=%wide.region_17.17_spmd.clone, body=%wide.region_15.16_spmd.clone.sunk | while | flops 511737344 | bytes 36002044 | solution.py:109
  601.0 2.6 fusion.119
  612.6 2.7 fusion.119
  624.3 2.7 fusion.119
  636.5 5.7 copy.143
  642.2 8.9 all_to_all.63
  651.6 3.8 copy.145
  655.4 8.2 fusion.48
  665.3 8.9 fusion.57
  675.5 8.7 fusion.66
  689.4 124.4 %reduce-scatter.5.cloned.1.call-done = f32[48,2304]{1,0:T(8,128)} async-done(((f32[768,2304]{1,0:T(8,128)}), f32[48,2304]{1,0:T(8,128)}) %reduce-scatter.5.cloned.1.call-update) | async-done | bytes 442384 | tf_op jit(solution)/shard_map/reduce_scatter | solution.py:294
  815.6 174.8 %reduce-scatter.9.cloned.1.call-done = f32[48,3072]{1,0:T(8,128)} async-done(((f32[768,3072]{1,0:T(8,128)}), f32[48,3072]{1,0:T(8,128)}) %reduce-scatter.9.cloned.1.call-update) | async-done | bytes 589840 | tf_op jit(solution)/shard_map/reduce_scatter | solution.py:301
  992.2 174.0 %reduce-scatter.11.cloned.1.call-done = f32[192,768]{1,0:T(8,128)} async-done(((f32[3072,768]{1,0:T(8,128)}), f32[192,768]{1,0:T(8,128)}) %reduce-scatter.11.cloned.1.call-update) | async-done | bytes 589840 | tf_op jit(solution)/shard_map/reduce_scatter | solution.py:303
  1168.0 7.0 add_bitcast_fusion
  1175.1 3.0 copy.148
  1179.1 74.8 %all-reduce.18 = (bf16[768]{0:T(1024)(128)(2,1)S(1)}, bf16[768]{0:T(1024)(128)(2,1)S(1)}, bf16[768]{0:T(1024)(128)(2,1)S(1)}, bf16[768]{0:T(1024)(128)(2,1)S(1)}...) all-reduce(f32[768]{0:T(1024)} %get-tuple-element.408, ...), channel_id=3, replica_groups=mesh['seq'=2,'dp'=16] {'dp'}, use_global_device_ids=true, to_apply=%region_22.23.clone | all-reduce | flops 9216 | bytes 55296
  (758 shorter events, 367.6 us)
Async XLA Ops:
  7.2 5.4 copy-start.41
  7.2 7.3 copy-start.44
  7.2 7.5 copy-start.45
  7.2 7.7 copy-start.46
  7.2 8.0 copy-start.47
  7.2 8.2 copy-start.48
  7.2 8.4 copy-start.49
  7.3 8.6 copy-start.50
  7.3 8.9 copy-start.51
  7.3 9.1 copy-start.52
  7.3 90.3 %copy-start.18 = (bf16[1,768,768]{2,1,0:T(8,128)(2,1)S(1)}, bf16[1,768,768]{2,1,0:T(8,128)(2,1)}, u32[]{:S(2)}) copy-start(bf16[1,768,768]{2,1,0:T(8,128)(2,1)} %param.25) | copy-start | bytes 3538948
  7.3 93.5 %all-gather.5.cloned.1.call-start = ((), (), s32[]{:S(2)}) async-start(), calls=%async_computation.8 | async-start | bytes 3760128 | tf_op jit(solution)/shard_map/all_gather | solution.py:145
  8.0 239.0 %all-gather.7.cloned.1.call-start = ((), (), s32[]{:S(2)}) async-start(), calls=%async_computation.9 | async-start | bytes 1253376 | tf_op jit(solution)/shard_map/all_gather | solution.py:146
  8.8 241.9 %all-gather.9.cloned.1.call-start = ((), (), s32[]{:S(2)}) async-start(), calls=%async_computation.10 | async-start | bytes 5013504 | tf_op jit(solution)/shard_map/all_gather | solution.py:198
  9.5 297.6 %all-gather.11.cloned.1.call-start = ((), (), s32[]{:S(2)}) async-start(), calls=%async_computation.11 | async-start | bytes 5013504 | tf_op jit(solution)/shard_map/all_gather | solution.py:199
  10.1 677.6 %reduce-scatter.7.cloned.1.call-start = ((), (), s32[]{:S(2)}) async-start(), calls=%async_computation.13 | async-start | bytes 2506752 | tf_op jit(solution)/shard_map/reduce_scatter | solution.py:297
  10.2 88.1 %copy-start.32 = (s32[1,1536]{1,0:T(1,128)S(1)}, s32[1,1536]{1,0:T(1,128)}, u32[]{:S(2)}) copy-start(s32[1,1536]{1,0:T(1,128)} %param.27) | copy-start | bytes 18436
  10.2 90.6 %copy-start.40 = (f32[1,768]{1,0:T(1,128)S(1)}, f32[1,768]{1,0:T(1,128)}, u32[]{:S(2)}) copy-start(f32[1,768]{1,0:T(1,128)} %param.26) | copy-start | bytes 9220
  146.8 3.8 copy-start.11
  250.3 86.4 %copy-start.7 = (f32[768,768]{0,1:T(8,128)}, f32[768,768]{0,1:T(8,128)S(1)}, u32[]{:S(2)}) copy-start(f32[768,768]{0,1:T(8,128)S(1)} %get-tuple-element.534) | copy-start | bytes 7077892
  250.3 86.3 %copy-start.20 = (f32[768]{0:T(1024)}, f32[768]{0:T(1024)S(1)}, u32[]{:S(2)}) copy-start(f32[768]{0:T(1024)S(1)} %broadcast_multiply_fusion.5) | copy-start | bytes 9220
  250.6 86.0 %copy-start.25 = (f32[768]{0:T(1024)}, f32[768]{0:T(1024)S(1)}, u32[]{:S(2)}) copy-start(f32[768]{0:T(1024)S(1)} %add_rsqrt_fusion.1) | copy-start | bytes 9220
  250.6 56.5 %copy-start.35 = (f32[768]{0:T(1024)S(1)}, f32[768]{0:T(1024)}, u32[]{:S(2)}) copy-start(f32[768]{0:T(1024)} %convert_element_type.190) | copy-start | bytes 9220
  316.0 4.3 copy-start.42
  317.6 13.4 %slice-start = ((s8[4718592]{0:T(1024)(128)(4,1)}), s8[4194304]{0:T(1024)(128)(4,1)S(1)}, s32[]{:S(2)}) async-start(s8[4718592]{0:T(1024)(128)(4,1)} %bitcast.246), calls=%async_computation.17 | async-start | bytes 8388608
  320.3 10.7 copy-start.16
  320.3 10.7 slice-start.1
  331.0 5.7 copy-start.53
  336.7 2.9 copy-start.13
  351.6 462.3 %reduce-scatter.5.cloned.1.call-start = ((), (), s32[]{:S(2)}) async-start(), calls=%async_computation.12 | async-start | bytes 7520256 | tf_op jit(solution)/shard_map/reduce_scatter | solution.py:294
  355.3 7.0 copy-start.14
  380.1 2.8 copy-start.1
  391.8 2.8 copy-start.1
  397.4 3.8 copy-start.3
  397.4 4.6 copy-start.15
  401.9 7.0 copy-start.14
  426.7 2.8 copy-start.1
  438.4 2.7 copy-start.1
  443.9 3.8 copy-start.3
  443.9 4.5 copy-start.15
  448.4 6.9 copy-start.14
  473.2 2.8 copy-start.1
  490.4 3.9 copy-start.3
  490.4 4.6 copy-start.15
  495.0 6.9 copy-start.14
  519.7 2.7 copy-start.1
  531.4 2.7 copy-start.1
  536.9 3.8 copy-start.3
  536.9 4.5 copy-start.15
  541.4 6.9 copy-start.14
  566.1 2.7 copy-start.1
  577.8 2.7 copy-start.1
  583.3 3.9 copy-start.3
  583.3 4.5 copy-start.15
  587.8 6.9 copy-start.14
  612.6 2.7 copy-start.1
  624.3 2.7 copy-start.1
  629.7 3.9 copy-start.3
  629.7 4.6 copy-start.15
  651.6 3.8 copy-start.39
  663.7 326.7 %reduce-scatter.9.cloned.1.call-start = ((), (), s32[]{:S(2)}) async-start(), calls=%async_computation.14 | async-start | bytes 10027008 | tf_op jit(solution)/shard_map/reduce_scatter | solution.py:301
  674.2 492.0 %reduce-scatter.11.cloned.1.call-start = ((), (), s32[]{:S(2)}) async-start(), calls=%async_computation.15 | async-start | bytes 10027008 | tf_op jit(solution)/shard_map/reduce_scatter | solution.py:303
  684.2 577.5 %all-reduce.24.cloned.1.call-start = ((), (), s32[]{:S(2)}) async-start(), calls=%async_computation.16 | async-start | bytes 1769472 | tf_op jit(solution)/shard_map/psum | solution.py:309
  687.7 480.3 %copy-start.6 = (bf16[1,768,3,2,1,384]{1,5,3,2,4,0:T(8,128)(2,1)S(1)}, bf16[1,768,3,2,1,384]{1,5,3,2,4,0:T(8,128)(2,1)}, u32[]{:S(2)}) copy-start(bf16[1,768,3,2,1,384]{1,5,3,2,4,0:T(8,128)(2,1)} %copy.145) | copy-start | bytes 10616836
  (67 other events, 104.5 us)
Sparse Core Ops, SparseCore 0:
  10.9 74.4 all-gather.4
  88.2 54.8 all-gather.6
  145.9 79.4 all-gather.8
  228.0 79.0 all-gather.10
  351.7 127.1 reduce-scatter.6
  663.8 150.0 reduce-scatter.4
  820.5 169.8 reduce-scatter.8
  996.0 170.1 reduce-scatter.10
  1170.1 18.3 all-reduce.23
where the time goes:
time: 1290 us; the launch traced here: 1280 us
  waiting for transfers between devices  522 us (40%)
  matrix products  275 us (21%)
  blocking collectives  183 us (14%)
  local copies, waits for them, and re-layouts  177 us (14%)
  other arithmetic  97.9 us (8%)
  between operations  17.7 us (1%)
    reduce_scatter x1, waiting for transfers between devices, body(): lax.psum_scatter(grads[7], 'dp', scatter_dimension=0, tiled=True)  175 us
    reduce_scatter x1, waiting for transfers between devices, body(): lax.psum_scatter(grads[9], 'dp', scatter_dimension=0, tiled=True)  174 us
    unnamed x2, blocking collectives  154 us
    reduce_scatter x1, waiting for transfers between devices, body(): lax.psum_scatter(grads[0], 'dp', scatter_dimension=0, tiled=True)  124 us
    dot_general x58, matrix products, product_nt(): lax.dot_general(left, right, (((1,), (1,)), ((), ())), preferred_element_...  106 us
    dot_general x40, matrix products, product_tn(): lax.dot_general(left, right, (((0,), (0,)), ((), ())), preferred_element_...  104 us
    dot_general x40, matrix products, matmul(): return jnp.dot(left, right, preferred_element_type=jnp.float32)  65.2 us
    all_gather x1, waiting for transfers between devices, body(): lax.all_gather(contract_weight, 'dp', axis=0, tiled=True)  45.7 us
  transfers between devices with their start and end apart: 9, of which 4 were waited for; matrix products, arithmetic and copies ran while one was open for 39% of the time, Pallas kernels for 0%

commit v1 on v0

--- a/solution.py
+++ b/solution.py
@@ -1,11 +1,765 @@
+import functools
 import math
 
 import jax
 import jax.numpy as jnp
 from jax import lax
+from jax.experimental import pallas as pl
+from jax.experimental.pallas import tpu as pltpu
 from jax.sharding import PartitionSpec as P
 
 HD = 64
+DOCS = 4
+BF = jnp.bfloat16
+F32 = jnp.float32
+MESH = pl.DeviceIdType.MESH
+VM = pltpu.VMEM
+DMA = pltpu.SemaphoreType.DMA
+
+
+def nn(a, b):
+    return jnp.dot(a, b, preferred_element_type=F32)
+
+
+def nt(a, b):
+    return lax.dot_general(a, b, (((1,), (1,)), ((), ())), preferred_element_type=F32)
+
+
+def tn(a, b):
+    return lax.dot_general(a, b, (((0,), (0,)), ((), ())), preferred_element_type=F32)
+
+
+def fused_kernel(
+    tokens, cot, te, seg, win_s, wout_s, wexp_s, wcon_s, small_s,
+    lo_o, ig_o, gin_o, gout_o, gexp_o, gcon_o, gvec_o, spill,
+    win, wout, wexp, wcon, tok, tokr, cotn, cotr, vec, fullv, fulle, proj, xl, n1, bias,
+    sc1, heads, fl, hidden, slope, pslot, lonew, lor, sg, bg,
+    gin, con_r, gv, ge, vout, vsum, vr, fin, fout, fexp, fcon,
+    swap_sem, ls, gs, gr, ps, rs, rr, pd,
+):
+    T, D = tok.shape
+    FF = wexp.shape[1]
+    me = lax.axis_index("dp")
+    c = lax.axis_index("seq")
+    x = lax.rem(me, 2)
+    y = lax.rem(me // 2, 2)
+    xy = lax.rem(me, 4)
+    z = me // 4
+    flip_x = me + 1 - 2 * x
+    flip_y = me + 2 - 4 * y
+    near = (1 - c) * flip_x + c * flip_y
+    far = (1 - c) * flip_y + c * flip_x
+    other = 1 - c
+    zs = [lax.rem(z + k, 4) * 4 + xy for k in (1, 2, 3)]
+
+    def send(src, dst, s, r, dp, seq):
+        return pltpu.make_async_remote_copy(
+            src_ref=src, dst_ref=dst, send_sem=s, recv_sem=r,
+            device_id={"dp": dp, "seq": seq}, device_id_type=MESH,
+        )
+
+    barrier = pltpu.get_barrier_semaphore()
+    for dp, seq in [(me, other), (near, c), (far, c)] + [(q, c) for q in zs]:
+        pl.semaphore_signal(
+            barrier, inc=1, device_id={"dp": dp, "seq": seq}, device_id_type=MESH
+        )
+    pl.semaphore_wait(barrier, 6)
+
+    def al(v, m):
+        return pl.multiple_of(v, m)
+
+    class Piece:
+        def __init__(self, n, shard, buf, rows, col, half):
+            self.n, self.shard, self.buf, self.rows, self.col, self.half = n, shard, buf, rows, col, half
+
+        def cols(self, core):
+            return pl.ds(al(self.col + core * self.half, 128), self.half)
+
+        def block(self, o):
+            return self.buf.at[pl.ds(al(o * self.rows, 16), self.rows), self.cols(c)]
+
+        def many(self, k):
+            return self.buf.at[pl.ds(0, k * self.rows), self.cols(c)]
+
+        def recv(self, stage, k):
+            send(self.many(k), self.many(k), gs.at[self.n, stage], gr.at[self.n, stage], me, other).wait_recv()
+
+        def sent(self, stage, k):
+            send(self.many(k), self.many(k), gs.at[self.n, stage], gr.at[self.n, stage], me, other).wait_send()
+
+        def local(self):
+            return pltpu.make_async_copy(
+                self.shard.at[:, self.cols(c)], self.block(me), ls.at[self.n]
+            )
+
+        def s1(self):
+            self.local().start()
+            for q in zs:
+                send(self.shard.at[:, self.cols(c)], self.block(me), gs.at[self.n, 0], gr.at[self.n, 0], q, c).start()
+
+        def s2(self):
+            self.local().wait()
+            self.recv(0, 3)
+
+            def one(k, _):
+                b = self.block(k * 4 + xy)
+                send(b, b, gs.at[self.n, 1], gr.at[self.n, 1], near, c).start()
+                return 0
+
+            lax.fori_loop(0, 4, one, 0)
+
+        def s3(self):
+            self.recv(1, 4)
+
+            def one(k, _):
+                b = self.block((k // 2) * 4 + (1 - c) * 2 * y + c * x + lax.rem(k, 2) * (1 + c))
+                send(b, b, gs.at[self.n, 2], gr.at[self.n, 2], far, c).start()
+                return 0
+
+            lax.fori_loop(0, 8, one, 0)
+
+        def s4(self):
+            self.recv(2, 8)
+            m = self.many(16)
+            send(m, m, gs.at[self.n, 3], gr.at[self.n, 3], me, other).start()
+
+        def done(self):
+            n = self.buf.at[pl.ds(0, 16 * self.rows), self.cols(other)]
+            send(n, n, gs.at[self.n, 3], gr.at[self.n, 3], me, other).wait_recv()
+
+        def drain(self):
+            for stage, k in ((0, 3), (1, 4), (2, 8), (3, 16)):
+                self.sent(stage, k)
+
+    w_in = Piece(0, win_s, win, 48, 0, 1152)
+    w_out = Piece(1, wout_s, wout, 48, 0, 384)
+    w_exp = [Piece(2 + k, wexp_s, wexp, 48, 1536 * k, 768) for k in range(2)]
+    w_con = [Piece(4 + k, wcon_s, wcon, 192, 256 * k, 128) for k in range(3)]
+    SM = 7
+
+    def small(stage, k, recv):
+        d = send(vec.at[pl.ds(0, k)], vec.at[pl.ds(0, k)], gs.at[SM, stage], gr.at[SM, stage], me, other)
+        d.wait_recv() if recv else d.wait_send()
+
+    swap_tok = send(tokens, tokr, swap_sem.at[0, 0], swap_sem.at[0, 1], me, other)
+    swap_cot = send(cot, cotr, swap_sem.at[1, 0], swap_sem.at[1, 1], me, other)
+    own_tok = pltpu.make_async_copy(tokens, tok, ls.at[8])
+    own_cot = pltpu.make_async_copy(cot, cotn, ls.at[9])
+    own_vec = pltpu.make_async_copy(small_s, vec.at[me], ls.at[10])
+
+    own_tok.start()
+    own_vec.start()
+    w_in.s1()
+    for q in zs:
+        send(small_s, vec.at[me], gs.at[SM, 0], gr.at[SM, 0], q, c).start()
+    swap_tok.start()
+    w_out.s1()
+    for p in w_exp + w_con:
+        p.s1()
+    swap_cot.start()
+    own_cot.start()
+
+    row = seg[...].astype(F32)
+    first_row = jnp.zeros((1, 1), F32)
+    for d in range(DOCS):
+        size = jnp.sum(jnp.where(row == d, 1.0, 0.0), axis=1, keepdims=True)
+        before = jnp.sum(jnp.where(row < d, 1.0, 0.0), axis=1, keepdims=True)
+        first_row = first_row + jnp.where(size == T, before, 0.0)
+    keep_row = lax.broadcasted_iota(jnp.int32, (1, T), 1).astype(F32) >= first_row
+    mine = seg[:, pl.ds(al(c * T, 128), T)].astype(F32)
+    theirs = seg[:, pl.ds(al(other * T, 128), T)].astype(F32)
+    seg_row = jnp.where(keep_row, mine, theirs)
+    seg_col = jnp.broadcast_to(seg_row, (128, T)).T[:, :1]
+    keep_col = lax.broadcasted_iota(jnp.int32, (T, 1), 0).astype(F32) >= first_row
+    keep_col = jnp.where(keep_col, 1.0, 0.0)
+    sc1[...] = jnp.concatenate([keep_col, seg_col], axis=1)
+
+    def mask_rows(i, _):
+        r = pl.ds(al(i * 128, 128), 128)
+        bias[r, :] = jnp.where(sc1[r, 1:2] == seg_row, 0.0, -1e30)
+        return 0
+
+    lax.fori_loop(0, T // 128, mask_rows, 0)
+    own_tok.wait()
+    swap_tok.wait_recv()
+
+    def start_rows(i, _):
+        r = pl.ds(al(i * 128, 128), 128)
+        t = jnp.where(sc1[r, 0:1] > 0.5, tok[r, :].astype(F32), tokr[r, :].astype(F32)) + te[...]
+        n1[r, :] = t
+        xl[r, :] = t.astype(BF)
+        return 0
+
+    lax.fori_loop(0, T // 128, start_rows, 0)
+
+    w_in.s2()
+    own_vec.wait()
+    small(0, 3, True)
+
+    def small2(k, _):
+        b = vec.at[k * 4 + xy]
+        send(b, b, gs.at[SM, 1], gr.at[SM, 1], near, c).start()
+        return 0
+
+    lax.fori_loop(0, 4, small2, 0)
+    w_in.s3()
+    small(1, 4, True)
+
+    def small3(k, _):
+        b = vec.at[(k // 2) * 4 + (1 - c) * 2 * y + c * x + lax.rem(k, 2) * (1 + c)]
+        send(b, b, gs.at[SM, 2], gr.at[SM, 2], far, c).start()
+        return 0
+
+    lax.fori_loop(0, 8, small3, 0)
+    w_out.s2()
+    w_in.s4()
+    small(2, 8, True)
+    for o in range(16):
+        fullv[:, o * 48 : (o + 1) * 48] = vec[o][:, :48].astype(F32)
+        for k in range(4):
+            fulle[:, o * 192 + k * 48 : o * 192 + (k + 1) * 48] = vec[o][k : k + 1, 64:112].astype(F32)
+    w_in.done()
+
+    for j in range(3):
+        v = nn(xl[...], win[:, j * D : (j + 1) * D])
+        if j == 0:
+            v = (v + fullv[0:1, :]).astype(BF) * jnp.asarray(HD**-0.5, BF)
+        elif j == 1:
+            v = v.astype(BF)
+        else:
+            v = (v + fullv[1:2, :]).astype(BF)
+        proj[:, j * D : (j + 1) * D] = v
+
+    lane = lax.broadcasted_iota(jnp.int32, (1, 128), 1)
+    halves = (lane < HD, lane >= HD)
+    pairs = D // 128
+
+    def keep(h, a):
+        return pltpu.make_async_copy(pslot.at[a], spill.at[h * 2 + a], ps.at[a])
+
+    tasks = [
+        [w_out.s3, w_exp[0].s2],
+        [w_out.s4, w_exp[0].s3],
+        [w_exp[0].s4, w_exp[1].s2],
+        [w_exp[1].s3, w_con[0].s2],
+        [w_exp[1].s4, w_con[0].s3, w_con[1].s2],
+        [w_con[0].s4, w_con[1].s3],
+    ]
+
+    def attend(h, _):
+        cs = al(h * 128, 128)
+        q2 = proj[:, pl.ds(cs, 128)]
+        k2 = proj[:, pl.ds(D + cs, 128)]
+        v2 = proj[:, pl.ds(2 * D + cs, 128)]
+        outs = []
+        for a in range(2):
+            s = nt(jnp.where(halves[a], q2, jnp.zeros_like(q2)), k2) + bias[...]
+            e = jnp.exp(s - jnp.max(s, axis=-1, keepdims=True))
+            p = (e * (1.0 / jnp.sum(e, axis=-1, keepdims=True))).astype(BF)
+
+            @pl.when(h > 0)
+            def _():
+                keep(h - 1, a).wait()
+
+            pslot[a] = p
+            keep(h, a).start()
+            outs.append(nn(p, v2))
+        heads[:, pl.ds(cs, 128)] = jnp.where(halves[0], outs[0], outs[1]).astype(BF)
+        for k in range(pairs):
+
+            @pl.when(h == k)
+            def _():
+                for t in tasks[k]:
+                    t()
+
+        return 0
+
+    lax.fori_loop(0, pairs, attend, 0)
+    w_out.done()
+
+    def load(h, a):
+        return pltpu.make_async_copy(spill.at[h * 2 + a], pslot.at[a], pd.at[a])
+
+    for a in range(2):
+        keep(pairs - 1, a).wait()
+        load(0, a).start()
+
+    def normalize(v):
+        centred = v - jnp.mean(v, axis=-1, keepdims=True)
+        scale = lax.rsqrt(jnp.mean(centred * centred, axis=-1, keepdims=True) + 1e-5)
+        return centred * scale, scale
+
+    def first_rows(i, _):
+        r = pl.ds(al(i * 256, 256), 256)
+        v = n1[r, :] + (nn(heads[r, :], wout[...]) + fullv[2:3, :])
+        n, s = normalize(v)
+        n1[r, :] = n
+        sc1[r, 1:2] = s
+        fl[r, :] = (n * fullv[3:4, :] + fullv[4:5, :]).astype(BF)
+        return 0
+
+    lax.fori_loop(0, T // 256, first_rows, 0)
+    w_con[2].s2()
+    w_exp[0].done()
+    w_exp[1].done()
+    w_con[1].s4()
+    w_con[2].s3()
+
+    def expand(i, _):
+        cs = pl.ds(al(i * 512, 512), 512)
+        u = nn(fl[...], wexp[:, cs]) + fulle[:, cs]
+        cdf = 0.5 * (1.0 + lax.erf(u * math.sqrt(0.5)))
+        hidden[:, cs] = (u * cdf).astype(BF)
+        slope[:, cs] = (cdf + u * jnp.exp(-0.5 * u * u) * (1.0 / math.sqrt(2.0 * math.pi))).astype(BF)
+        return 0
+
+    lax.fori_loop(0, FF // 512, expand, 0)
+    w_con[2].s4()
+    for p in w_con:
+        p.done()
+    own_cot.wait()
+    swap_cot.wait_recv()
+
+    gv[...] = jnp.zeros_like(gv)
+
+    def second_rows(i, _):
+        r = pl.ds(al(i * 256, 256), 256)
+        v = n1[r, :] * fullv[3:4, :] + fullv[4:5, :] + (nn(hidden[r, :], wcon[...]) + fullv[5:6, :])
+        n, s = normalize(v)
+        lonew[r, :] = (n * fullv[6:7, :] + fullv[7:8, :]).astype(BF)
+        og = jnp.where(sc1[r, 0:1] > 0.5, cotn[r, :].astype(F32), cotr[r, :].astype(F32))
+        gv[6:7, :] += jnp.sum(og * n, axis=0, keepdims=True)
+        gv[7:8, :] += jnp.sum(og, axis=0, keepdims=True)
+        w = og * fullv[6:7, :]
+        g = s * (w - jnp.mean(w, axis=-1, keepdims=True) - n * jnp.mean(w * n, axis=-1, keepdims=True))
+        sg[r, :] = g
+        low = g.astype(BF)
+        bg[r, :] = low
+        gv[5:6, :] += jnp.sum(low.astype(F32), axis=0, keepdims=True)
+        return 0
+
+    lax.fori_loop(0, T // 256, second_rows, 0)
+    swap_lo = send(lonew, lor, swap_sem.at[2, 0], swap_sem.at[2, 1], me, other)
+    swap_lo.start()
+
+    S = 384
+    my_k = (1 - c) * x + c * y
+    far_base = (1 - c) * (2 - 2 * y) + c * (1 - x)
+    own_base = (1 - c) * 2 * y + c * x
+    near_xy = xy + (1 - c) * (1 - 2 * x) + c * (2 - 4 * y)
+    step_k = 1 + c
+
+    def total(*refs):
+        t = refs[0][...].astype(F32)
+        for ref in refs[1:]:
+            t = t + ref[...].astype(F32)
+        return t
+
+    class Red:
+        def __init__(self, n, g, col, rows, recv, rcol, fsum, plane=None):
+            self.n, self.g, self.col, self.rows, self.recv, self.rcol, self.fsum = n, g, col, rows, recv, rcol, fsum
+            self.plane = plane
+
+        def cols(self, core):
+            return pl.ds(al(self.col + core * S, 128), S)
+
+        def part(self, base, i, k=1, second=False):
+            if self.plane is None:
+                cs = pl.ds(self.rcol + (S if second else 0), S)
+            else:
+                cs = pl.ds(0, S)
+                base = base + self.rcol
+            return self.recv.at[pl.ds(al(base + i * self.rows, 16), k * self.rows), cs]
+
+        def mine(self, o):
+            base = 0 if self.plane is None else self.plane * 4
+            return self.g.at[pl.ds(al((base + o) * self.rows, 16), self.rows), self.cols(c)]
+
+        def planes(self):
+            return 4 if self.plane is None else 1
+
+        def rp(self, o, k=1):
+            return self.part(0, o, k)
+
+        def ra(self, i, k=1):
+            return self.part(0 if self.plane is None else 768, i, k, True)
+
+        def rb(self, i, k=1):
+            return self.part(384 if self.plane is None else 1152, i, k, True)
+
+        def rz(self, i, k=1):
+            if self.plane is None:
+                return self.part(576, i, k, True)
+            return self.recv.at[pl.ds(al(5376 + i * self.rows, 16), k * self.rows), pl.ds(0, S)]
+
+        def sem(self, stage):
+            return rs.at[self.n, stage], rr.at[self.n, stage]
+
+        def got(self, stage, ref):
+            s, r = self.sem(stage)
+            send(ref, ref, s, r, me, other).wait_recv()
+
+        def gone(self, stage, ref):
+            s, r = self.sem(stage)
+            send(ref, ref, s, r, me, other).wait_send()
+
+        def P(self):
+            base = 0 if self.plane is None else self.plane * 4 * self.rows
+            n = 4 * self.planes() * self.rows
+            src = self.g.at[pl.ds(al(base, 16), n), self.cols(other)]
+            s, r = self.sem(0)
+            send(src, self.rp(0, 4 * self.planes()), s, r, me, other).start()
+
+        def A(self):
+            self.got(0, self.rp(0, 4 * self.planes()))
+            s, r = self.sem(1)
+
+            def one(i, _):
+                o = (i // 2) * 4 + far_base + lax.rem(i, 2) * step_k
+                b = self.mine(o)
+                b[...] = total(b, self.rp(o)).astype(BF)
+                send(b, self.ra(i), s, r, far, c).start()
+                return 0
+
+            lax.fori_loop(0, 2 * self.planes(), one, 0)
+
+        def B(self):
+            self.got(1, self.ra(0, 2 * self.planes()))
+            s, r = self.sem(2)
+
+            def one(i, _):
+                o = i * 4 + near_xy
+                b = self.mine(o)
+                b[...] = total(b, self.rp(o), self.ra(i * 2 + 1 - my_k)).astype(BF)
+                send(b, self.rb(i), s, r, near, c).start()
+                return 0
+
+            lax.fori_loop(0, self.planes(), one, 0)
+
+        def Z(self, j=None):
+            self.got(2, self.rb(0, self.planes()))
+            if self.plane is None:
+                for k in range(3):
+                    s, r = self.sem(3)
+                    p = lax.rem(z + k + 1, 4)
+                    b = self.mine(p * 4 + xy)
+                    b[...] = total(b, self.rp(p * 4 + xy), self.ra(p * 2 + my_k), self.rb(p)).astype(BF)
+                    send(b, self.rz(k), s, r, zs[k], c).start()
+            elif j > 0:
+                s, r = rs.at[self.n, 3], rr.at[0, 3]
+                b = self.mine(xy)
+                b[...] = total(b, self.rp(xy), self.ra(my_k), self.rb(0)).astype(BF)
+                send(b, self.rz(j - 1), s, r, zs[j - 1], c).start()
+
+        def F(self):
+            if self.plane is None:
+                self.got(3, self.rz(0, 3))
+                t = total(self.mine(z * 4 + xy), self.rp(z * 4 + xy), self.ra(z * 2 + my_k), self.rb(z),
+                          self.rz(0), self.rz(1), self.rz(2))
+            else:
+                ref = self.rz(0, 3)
+                send(ref, ref, rs.at[0, 3], rr.at[0, 3], me, other).wait_recv()
+                t = total(self.mine(xy), self.rp(xy), self.ra(my_k), self.rb(0), self.rz(0), self.rz(1), self.rz(2))
+            s, r = self.sem(4)
+            if self.n >= 9:
+                for k in range(3):
+                    b = self.fsum.at[:, pl.ds(al(k * D + (self.n - 9) * 256 + c * 128, 128), 128)]
+                    b[...] = t[:, k * 128 : (k + 1) * 128]
+                    send(b, b, s, r, me, other).start()
+            else:
+                b = self.fsum.at[:, self.cols(c)]
+                b[...] = t
+                send(b, b, s, r, me, other).start()
+
+        def end(self):
+            p = self.planes()
+            self.gone(0, self.rp(0, 4 * p))
+            self.gone(1, self.ra(0, 2 * p))
+            self.gone(2, self.rb(0, p))
+            if self.plane is None:
+                self.gone(3, self.rz(0, 3))
+            elif self.n > 0:
+                self.gone(3, self.rz(0, 1))
+            if self.plane is None or self.n == 0:
+                half = self.fsum.at[:, pl.ds(0, S)]
+                self.gone(4, half)
+                self.got(4, half)
+
+    con = {j: Red(j, wcon, 0, 192, con_r, j * 1344, fcon, plane=lax.rem(z + j, 4)) for j in range(4)}
+    exp = [Red(4 + k, wexp, k * 768, 48, hidden, k * 768, fexp) for k in range(4)]
+    out = Red(8, wout, 0, 48, slope, 2304, fout)
+    ins = [Red(9 + k, gin, k * 768, 48, slope, k * 768, fin) for k in range(3)]
+
+    def expand_back(i, _):
+        cs = pl.ds(al(i * 512, 512), 512)
+        g = (nt(bg[...], wcon[cs, :]) * slope[:, cs].astype(F32)).astype(BF)
+        slope[:, cs] = g
+        ge[:, cs] = jnp.sum(g.astype(F32), axis=0, keepdims=True)
+        return 0
+
+    lax.fori_loop(0, FF // 512, expand_back, 0)
+    for p in w_con:
+        p.drain()
+
+    def grad_con(i, _):
+        p = al(lax.rem(z + i + 1, 4) * 768, 768)
+        wcon[pl.ds(p, 768), :] = tn(hidden[:, pl.ds(p, 768)], bg[...]).astype(BF)
+        for k, t in enumerate([
+            [con[1].P],
+            [con[2].P, con[1].A],
+            [con[3].P, con[2].A],
+            [con[0].P, con[3].A],
+        ]):
+
+            @pl.when(i == k)
+            def _():
+                for u in t:
+                    u()
+
+        return 0
+
+    lax.fori_loop(0, 4, grad_con, 0)
+
+    def first_back(i, _):
+        r = pl.ds(al(i * 256, 256), 256)
+        g = sg[r, :] + nt(slope[r, :], wexp[...])
+        n = n1[r, :]
+        gv[3:4, :] += jnp.sum(g * n, axis=0, keepdims=True)
+        gv[4:5, :] += jnp.sum(g, axis=0, keepdims=True)
+        w = g * fullv[3:4, :]
+        g = sc1[r, 1:2] * (w - jnp.mean(w, axis=-1, keepdims=True) - n * jnp.mean(w * n, axis=-1, keepdims=True))
+        sg[r, :] = g
+        low = g.astype(BF)
+        bg[r, :] = low
+        gv[2:3, :] += jnp.sum(low.astype(F32), axis=0, keepdims=True)
+        for k, t in enumerate([[con[0].A, con[1].B], [con[2].B], [con[3].B]]):
+
+            @pl.when(i == k)
+            def _():
+                for u in t:
+                    u()
+
+        return 0
+
+    lax.fori_loop(0, T // 256, first_back, 0)
+    for p in w_exp:
+        p.drain()
+    con[0].B()
+
+    def grad_exp(i, _):
+        cs = pl.ds(al(i * 768, 768), 768)
+        wexp[:, cs] = tn(fl[...], slope[:, cs]).astype(BF)
+        for k, t in enumerate([
+            [exp[0].P, lambda: con[1].Z(1)],
+            [exp[1].P, exp[0].A, lambda: con[2].Z(2)],
+            [exp[2].P, exp[1].A, lambda: con[3].Z(3)],
+            [exp[3].P, exp[2].A, lambda: con[0].Z(0), exp[0].B],
+        ]):
+
+            @pl.when(i == k)
+            def _():
+                for u in t:
+                    u()
+
+        return 0
+
+    lax.fori_loop(0, 4, grad_exp, 0)
+    hg = cotr
+    hg[...] = nt(bg[...], wout[...]).astype(BF)
+    exp[3].A()
+    exp[1].B()
+    w_out.drain()
+    wout[...] = tn(heads[...], bg[...]).astype(BF)
+    out.P()
+    con[0].F()
+
+    tasks = [
+        [exp[2].B, exp[0].Z],
+        [exp[3].B, exp[1].Z],
+        [out.A, exp[2].Z, exp[0].F],
+        [exp[3].Z, ins[0].A, exp[1].F],
+        [out.B, exp[2].F, exp[3].F],
+        [ins[0].B, out.Z, ins[1].A],
+    ]
+
+    def attend_back(h, _):
+        cs = al(h * 128, 128)
+        q2 = proj[:, pl.ds(cs, 128)]
+        k2 = proj[:, pl.ds(D + cs, 128)]
+        v2 = proj[:, pl.ds(2 * D + cs, 128)]
+        g2 = hg[:, pl.ds(cs, 128)]
+        prod = g2.astype(F32) * heads[:, pl.ds(cs, 128)].astype(F32)
+        qt = q2.astype(F32).T.astype(BF)
+        gt = g2.astype(F32).T.astype(BF)
+        dq, dk, dv = [], [], []
+        for a in range(2):
+            load(h, a).wait()
+            rowdot = jnp.sum(jnp.where(halves[a], prod, 0.0), axis=-1, keepdims=True)
+            p = pslot[a]
+            dp = nt(jnp.where(halves[a], g2, jnp.zeros_like(g2)), v2)
+            ds = (p.astype(F32) * (dp - rowdot)).astype(BF)
+            dq.append(nn(ds, k2))
+            dk.append(nn(qt[a * HD : (a + 1) * HD], ds))
+            dv.append(nn(gt[a * HD : (a + 1) * HD], p))
+
+            @pl.when(h + 1 < pairs)
+            def _():
+                load(h + 1, a).start()
+
+        dq = (jnp.where(halves[0], dq[0], dq[1]) * HD**-0.5).astype(BF)
+        dk = jnp.concatenate(dk, axis=0).T.astype(BF)
+        dv = jnp.concatenate(dv, axis=0).T.astype(BF)
+        proj[:, pl.ds(cs, 128)] = dq
+        proj[:, pl.ds(D + cs, 128)] = dk
+        proj[:, pl.ds(2 * D + cs, 128)] = dv
+        gv[0:1, pl.ds(cs, 128)] = jnp.sum(dq.astype(F32), axis=0, keepdims=True)
+        gv[1:2, pl.ds(cs, 128)] = jnp.sum(dv.astype(F32), axis=0, keepdims=True)
+
+        @pl.when(lax.rem(h, 2) == 1)
+        def _():
+            g = al((h // 2) * 256, 256)
+            cols = jnp.concatenate(
+                [proj[:, pl.ds(al(k * D + g + e * 128, 128), 128)] for e in range(2) for k in range(3)], axis=1
+            )
+            gin[:, pl.ds(al((h // 2) * 768, 768), 768)] = tn(xl[...], cols).astype(BF)
+
+        for k in range(pairs):
+
+            @pl.when(h == k)
+            def _():
+                if k % 2 == 1:
+                    ins[k // 2].P()
+                for t in tasks[k]:
+                    t()
+
+        return 0
+
+    lax.fori_loop(0, pairs, attend_back, 0)
+
+    vout[...] = jnp.zeros_like(vout)
+    for o in range(16):
+        vout[o, :, 0:48] = gv[0:8, o * 48 : (o + 1) * 48]
+        for k in range(4):
+            vout[o, k : k + 1, 64:112] = ge[:, o * 192 + k * 48 : o * 192 + (k + 1) * 48]
+    VN = 12
+
+    def vsend(stage, src, dst, dp, seq):
+        return send(src, dst, rs.at[VN, stage], rr.at[VN, stage], dp, seq)
+
+    vsend(0, vout, vr.at[pl.ds(0, 16)], me, other).start()
+    ins[2].A()
+
+    def input_rows(i, _):
+        r = pl.ds(al(i * 256, 256), 256)
+        sg[r, :] = sg[r, :] + nt(proj[r, :], win[...])
+        for k, t in enumerate([[ins[1].B], [ins[0].Z], [ins[2].B]]):
+
+            @pl.when(i == k)
+            def _():
+                for u in t:
+                    u()
+
+        return 0
+
+    lax.fori_loop(0, T // 256, input_rows, 0)
+    swap_ig = send(sg, n1, swap_sem.at[3, 0], swap_sem.at[3, 1], me, other)
+    swap_ig.start()
+    vsend(0, vout, vr.at[pl.ds(0, 16)], me, other).wait_recv()
+    vsum[...] = vout[...] + vr[pl.ds(0, 16)]
+    for i in range(8):
+        b = vsum.at[(i // 2) * 4 + 2 - 2 * y + i % 2]
+        vsend(1, b, vr.at[16 + i], flip_y, c).start()
+    ins[1].Z()
+    vsend(1, vr.at[pl.ds(16, 8)], vr.at[pl.ds(16, 8)], me, other).wait_recv()
+    for i in range(8):
+        o = (i // 2) * 4 + 2 * y + i % 2
+        vsum[o] = vsum[o] + vr[16 + i]
+    for i in range(4):
+        b = vsum.at[i * 4 + 2 * y + 1 - x]
+        vsend(2, b, vr.at[24 + i], flip_x, c).start()
+    ins[2].Z()
+    vsend(2, vr.at[pl.ds(24, 4)], vr.at[pl.ds(24, 4)], me, other).wait_recv()
+    for i in range(4):
+        vsum[i * 4 + xy] = vsum[i * 4 + xy] + vr[24 + i]
+    for k in range(3):
+        b = vsum.at[lax.rem(z + k + 1, 4) * 4 + xy]
+        vsend(3, b, vr.at[28 + k], zs[k], c).start()
+    out.F()
+    for p in ins:
+        p.F()
+
+    swap_lo.wait()
+
+    def out_rows(i, _):
+        r = pl.ds(al(i * 128, 128), 128)
+        lonew[r, :] = jnp.where(sc1[r, 0:1] > 0.5, lonew[r, :].astype(F32), lor[r, :].astype(F32)).astype(BF)
+        return 0
+
+    lax.fori_loop(0, T // 128, out_rows, 0)
+    lo_done = pltpu.make_async_copy(lonew, lo_o, ls.at[11])
+    lo_done.start()
+    swap_ig.wait()
+
+    def grad_rows(i, _):
+        r = pl.ds(al(i * 128, 128), 128)
+        sg[r, :] = jnp.where(sc1[r, 0:1] > 0.5, sg[r, :], n1[r, :])
+        return 0
+
+    lax.fori_loop(0, T // 128, grad_rows, 0)
+    outs = [lo_done, pltpu.make_async_copy(sg, ig_o, ls.at[12])]
+    outs[1].start()
+    vsend(3, vr.at[pl.ds(28, 3)], vr.at[pl.ds(28, 3)], me, other).wait_recv()
+    vfin = vr.at[31]
+    vfin[...] = vsum[z * 4 + xy] + vr[28] + vr[29] + vr[30]
+    outs.append(pltpu.make_async_copy(vfin, gvec_o, ls.at[13]))
+    outs[2].start()
+    swap_tok.wait_send()
+    swap_cot.wait_send()
+    w_in.drain()
+    for stage, k in ((0, 3), (1, 4), (2, 8)):
+        small(stage, k, False)
+        vsend(stage + 1, vr.at[pl.ds(0, (8, 4, 3)[stage])], vr.at[pl.ds(0, (8, 4, 3)[stage])], me, other).wait_send()
+    vsend(0, vout, vr.at[pl.ds(0, 16)], me, other).wait_send()
+    for p in list(con.values()) + exp + [out] + ins:
+        p.end()
+    for k, (v, o) in enumerate([(fin, gin_o), (fout, gout_o), (fexp, gexp_o), (fcon, gcon_o)]):
+        outs.append(pltpu.make_async_copy(v, o, ls.at[14 + k]))
+        outs[-1].start()
+    for o in outs:
+        o.wait()
+
+
+def fused_layer(tokens, time_embed, segments, iw, ow, ew, cw, small, cot):
+    T, D = tokens.shape
+    FF = ew.shape[1]
+    sh = jax.ShapeDtypeStruct
+    anyspec = pl.BlockSpec(memory_space=pl.ANY)
+    vspec = pl.BlockSpec(memory_space=VM)
+    scratch = [
+        VM((D, 3 * D), BF), VM((D, D), BF), VM((D, FF), BF), VM((FF, D), BF),
+        VM((T, D), BF), VM((T, D), BF), VM((T, D), BF), VM((T, D), BF),
+        VM((16, 16, 128), BF), VM((16, D), F32), VM((1, FF), F32),
+        VM((T, 3 * D), BF), VM((T, D), BF), VM((T, D), F32), VM((T, T), F32),
+        VM((T, 2), F32), VM((T, D), BF), VM((T, D), BF), VM((T, FF), BF), VM((T, FF), BF),
+        VM((2, T, T), BF), VM((T, D), BF), VM((T, D), BF), VM((T, D), F32), VM((T, D), BF),
+        VM((D, 3 * D), BF), VM((5952, 384), BF), VM((8, D), F32), VM((1, FF), F32),
+        VM((16, 8, 128), F32), VM((16, 8, 128), F32), VM((32, 8, 128), F32),
+        VM(iw.shape, F32), VM(ow.shape, F32), VM(ew.shape, F32), VM(cw.shape, F32),
+        DMA((4, 2)), DMA((18,)), DMA((8, 4)), DMA((8, 4)), DMA((2,)), DMA((13, 5)), DMA((13, 5)), DMA((2,)),
+    ]
+    return pl.pallas_call(
+        fused_kernel,
+        out_shape=(
+            sh((T, D), BF), sh((T, D), F32), sh(iw.shape, F32), sh(ow.shape, F32), sh(ew.shape, F32),
+            sh(cw.shape, F32), sh((8, 128), F32), sh((D // HD, T, T), BF),
+        ),
+        in_specs=[anyspec, anyspec, vspec, vspec, anyspec, anyspec, anyspec, anyspec, anyspec],
+        out_specs=(anyspec,) * 8,
+        scratch_shapes=scratch,
+        compiler_params=pltpu.CompilerParams(
+            collective_id=0, has_side_effects=True, vmem_limit_bytes=67043328
+        ),
+    )(tokens, cot, time_embed, segments, iw, ow, ew, cw, small)
 
 
 epsilon = 1e-05
@@ -114,7 +868,7 @@
     )
 
 
-def body(
+def plain_body(
     tokens,
     time_embed,
     segments,
@@ -323,6 +1077,35 @@
     return (layer_output.reshape(seqs, half, width), input_grad) + tuple(summed)
 
 
+def fused_body(
+    tokens, time_embed, segments, input_weight, query_bias, value_bias, output_weight, output_bias, first_gain,
+    first_shift, expand_weight, expand_bias, contract_weight, contract_bias, second_gain, second_shift, cotangent,
+):
+    vectors = [
+        query_bias, value_bias, output_bias, first_gain, first_shift, contract_bias, second_gain, second_shift,
+    ]
+    own = query_bias.shape[0]
+    small = jnp.pad(jnp.stack(vectors), ((0, 8), (0, 64 - own)))
+    wide = jnp.pad(expand_bias.reshape(4, own), ((0, 12), (0, 64 - own)))
+    small = jnp.concatenate([small, wide], axis=1)
+    layer_output, input_grad, g_in, g_out, g_exp, g_con, vec = fused_layer(
+        tokens[0], time_embed, segments, input_weight, output_weight, expand_weight, contract_weight, small,
+        cotangent[0],
+    )[:7]
+    row = [vec[k, :own] for k in range(8)]
+    g_eb = vec[0:4, 64 : 64 + own].reshape(4 * own)
+    return (
+        layer_output[None], input_grad[None], g_in, row[0], row[1], g_out, row[2], row[3], row[4],
+        g_exp, g_eb, g_con, row[5], row[6], row[7],
+    )
+
+
+def body(*args):
+    if lax.axis_size("dp") == 16 and lax.axis_size("seq") == 2:
+        return fused_body(*args)
+    return plain_body(*args)
+
+
 def solution(mesh):
     return jax.shard_map(
         body,

time: 1290 us -> 224 us (0.17); the launches traced: 1280 us -> 223 us
  waiting for transfers between devices: 522 us -> 0 us
  matrix products: 275 us -> 0 us
  Pallas kernels: 0 us -> 211 us
  blocking collectives: 183 us -> 0 us
  local copies, waits for them, and re-layouts: 177 us -> 11.4 us
  other arithmetic: 97.9 us -> 0.67 us
  between operations: 17.7 us -> 0.67 us
    reduce_scatter x4 -> x0, waiting for transfers between devices: 473 us -> none  [the longest x1 175 us: body(): lax.psum_scatter(grads[7], 'dp', scatter_dimension=0, tiled=True)]
    dot_general x138 -> x0, matrix products: 275 us -> none  [the longest x58 106 us: product_nt(): lax.dot_general(left, right, (((1,), (1,)), ((), ())), preferred_element_...]
    pallas_call x0 -> x1, Pallas kernels: none -> 211 us  [fused_layer(): pl.pallas_call(fused_kernel, out_shape=(sh((T, D), BF), sh((T, D), F32),...]
    unnamed x2 -> x0, blocking collectives: 154 us -> none
    convert_element_type x44 -> x0, other arithmetic: 54.2 us -> none  [the longest x18 31.4 us: one_block(): score_grad = (probs * (prob_grad - row_total)).astype(jnp.bfloat16)]
    dynamic_slice x96 -> x0, local copies, waits for them, and re-layouts: 50.4 us -> none  [the longest x36 32.5 us: body(): lax.map(attend_forward, (query_heads, key_heads, value_heads, segment_hea...]
    all_gather x4 -> x0, waiting for transfers between devices: 45.8 us -> none  [the longest x1 45.7 us: body(): lax.all_gather(contract_weight, 'dp', axis=0, tiled=True)]
    reshape x25 -> x2, local copies, waits for them, and re-layouts: 37.3 us -> 1.39 us  [the longest x1 0.74 us: fused_body(): wide = jnp.pad(expand_bias.reshape(4, own), ((0, 12), (0, 64 - own)))]
  transfers between devices with their start and end apart: 9 -> 0, of which waited for: 4 -> 0; matrix products, arithmetic and copies ran while one was open for 39% -> 0% of each run, Pallas kernels for 0% -> 0%
where the time goes in v1:
time: 224 us; the launch traced here: 223 us
  Pallas kernels  211 us (94%)
  local copies, waits for them, and re-layouts  11.4 us (5%)
    pallas_call x1, Pallas kernels, fused_layer(): pl.pallas_call(fused_kernel, out_shape=(sh((T, D), BF), sh((T, D), F32),...  211 us
    unnamed x16, local copies, waits for them, and re-layouts  6.99 us

profile of v1, /device:TPU:0, one launch (start us, length us, event | category | flops | bytes accessed | tf_op | source)
XLA Modules:
  0.0 223.5 jit_solution(7813201969381222045)
XLA Ops:
  0.6 0.7 reshape.36
  1.4 0.8 stack.35
  2.2 0.7 fusion.2.small_s
  2.9 210.7 %shard_map.280 = (bf16[768,768]{1,0:T(8,128)(2,1)}, f32[768,768]{1,0:T(8,128)}, f32[48,2304]{1,0:T(8,128)}, f32[48,768]{1,0:T(8,128)}, f32[48,3072]{1,0:T(8,128)...) custom-call(bf16[768,768]{1,0:T(8,128)(2,1)} %bitcast.30, bf16[768,768]{1,0:T(8,128)(2,1)} %bitcast.31, ...), custom_call_target="tpu_custom_call" | custom-call | tf_op jit(solution)/shard_map/pallas_call | solution.py:750
  213.6 0.8 slice.32
  214.3 0.6 reshape.37
  215.0 1.5 slice_bitcast_fusion
  216.5 0.0 copy-start
  216.5 2.5 %copy.38 = bf16[1,768,768]{2,1,0:T(8,128)(2,1)} copy(bf16[1,768,768]{2,1,0:T(8,128)(2,1)} %bitcast.29) | data formatting | bytes 2359296
  219.0 0.0 copy-done
  219.0 0.0 copy-start.3
  219.0 0.0 copy-start.4
  219.0 1.4 copy.39
  220.4 0.0 copy-done.3
  220.4 0.0 copy-start.2
  220.4 0.0 copy-start.1
  220.4 0.8 copy.40
  221.2 0.0 copy-done.4
  221.2 0.7 copy.41
  221.8 0.0 copy-done.2
  221.8 0.8 copy.42
  222.7 0.0 copy-done.1
  222.7 0.8 copy.43
Async XLA Ops:
  216.5 2.5 %copy-start = (f32[768,768]{1,0:T(8,128)S(1)}, f32[768,768]{1,0:T(8,128)}, u32[]{:S(2)}) copy-start(f32[768,768]{1,0:T(8,128)} %get-tuple-element.23) | copy-start | bytes 7077892
  219.0 1.4 copy-start.3
  219.0 2.2 copy-start.4
  220.4 1.4 copy-start.2
  220.4 2.2 %copy-start.1 = (f32[192,768]{1,0:T(8,128)S(1)}, f32[192,768]{1,0:T(8,128)}, u32[]{:S(2)}) copy-start(f32[192,768]{1,0:T(8,128)} %get-tuple-element.63) | copy-start | bytes 1769476

commit v2 on v1

--- a/solution.py
+++ b/solution.py
@@ -32,13 +32,15 @@
 def fused_kernel(
     tokens, cot, te, seg, win_s, wout_s, wexp_s, wcon_s, small_s,
     lo_o, ig_o, gin_o, gout_o, gexp_o, gcon_o, gvec_o, spill,
-    win, wout, wexp, wcon, tok, tokr, cotn, cotr, vec, fullv, fulle, proj, xl, n1, bias,
-    sc1, heads, fl, hidden, slope, pslot, lonew, lor, sg, bg,
-    gin, con_r, gv, ge, vout, vsum, vr, fin, fout, fexp, fcon,
+    wide, wcon, tok, tokr, cotn, cotr, vec, fullv, fulle, fullp, proj, xl, n1, sg,
+    sc1, heads, fl, hidden, slope, pslot, bg,
+    gin, gcon, con_r, gv, ge, vout, vsum, vr, fin, fout, fexp, fcon,
     swap_sem, ls, gs, gr, ps, rs, rr, pd,
 ):
     T, D = tok.shape
-    FF = wexp.shape[1]
+    FF = wcon.shape[0]
+    IN, OUT, EXP = 0, 3 * D, 4 * D
+    bias, lonew, lor = sg, tok, tokr
     me = lax.axis_index("dp")
     c = lax.axis_index("seq")
     x = lax.rem(me, 2)
@@ -69,8 +71,8 @@
         return pl.multiple_of(v, m)
 
     class Piece:
-        def __init__(self, n, shard, buf, rows, col, half):
-            self.n, self.shard, self.buf, self.rows, self.col, self.half = n, shard, buf, rows, col, half
+        def __init__(self, n, buf, rows, col, half, shards):
+            self.n, self.buf, self.rows, self.col, self.half, self.shards = n, buf, rows, col, half, shards
 
         def cols(self, core):
             return pl.ds(al(self.col + core * self.half, 128), self.half)
@@ -78,64 +80,85 @@
         def block(self, o):
             return self.buf.at[pl.ds(al(o * self.rows, 16), self.rows), self.cols(c)]
 
-        def many(self, k):
-            return self.buf.at[pl.ds(0, k * self.rows), self.cols(c)]
-
-        def recv(self, stage, k):
-            send(self.many(k), self.many(k), gs.at[self.n, stage], gr.at[self.n, stage], me, other).wait_recv()
-
-        def sent(self, stage, k):
-            send(self.many(k), self.many(k), gs.at[self.n, stage], gr.at[self.n, stage], me, other).wait_send()
-
-        def local(self):
-            return pltpu.make_async_copy(
-                self.shard.at[:, self.cols(c)], self.block(me), ls.at[self.n]
-            )
-
-        def s1(self):
-            self.local().start()
-            for q in zs:
-                send(self.shard.at[:, self.cols(c)], self.block(me), gs.at[self.n, 0], gr.at[self.n, 0], q, c).start()
-
-        def s2(self):
-            self.local().wait()
-            self.recv(0, 3)
-
-            def one(k, _):
-                b = self.block(k * 4 + xy)
-                send(b, b, gs.at[self.n, 1], gr.at[self.n, 1], near, c).start()
-                return 0
-
-            lax.fori_loop(0, 4, one, 0)
+        def region(self, k, core=c):
+            return self.buf.at[pl.ds(0, k * self.rows), self.cols(core)]
+
+        def push(self, src, dst, stage, k, dp):
+            send(src, dst, gs.at[self.n, stage], gr.at[self.n, stage * 4 + k], dp, c).start()
+
+        def got(self, stage, k, blocks):
+            m = self.region(blocks)
+            send(m, m, gs.at[self.n, stage], gr.at[self.n, stage * 4 + k], me, other).wait_recv()
+
+        def own(self):
+            base = pl.ds(al(me * self.rows, 16), self.rows)
+            for i, (ref, first, width) in enumerate(self.shards):
+                yield (
+                    ref.at[:, pl.ds(al(first + c * width, 128), width)],
+                    self.buf.at[base, pl.ds(al(self.col + c * self.half + i * width, 128), width)],
+                )
+
+        def s1(self, early):
+            for k in range(3):
+                for a, b in self.own():
+                    self.push(a, b, 0, k + 1, zs[k])
+            if early:
+                for a, b in self.own():
+                    self.push(a, b, 1, 0, near)
+                    self.push(a, b, 2, 0, far)
+            for a, b in self.own():
+                pltpu.make_async_copy(a, b, ls.at[self.n]).start()
+
+        def s2(self, early):
+            m = self.block(me)
+            pltpu.make_async_copy(m, m, ls.at[self.n]).wait()
+            for k in range(1 if early else 0, 4):
+                if k > 0:
+                    self.got(0, k, 1)
+                b = self.block(lax.rem(z + 4 - k, 4) * 4 + xy)
+                self.push(b, b, 1, k, near)
+                self.push(b, b, 2, k, far)
 
         def s3(self):
-            self.recv(1, 4)
-
-            def one(k, _):
-                b = self.block((k // 2) * 4 + (1 - c) * 2 * y + c * x + lax.rem(k, 2) * (1 + c))
-                send(b, b, gs.at[self.n, 2], gr.at[self.n, 2], far, c).start()
-                return 0
-
-            lax.fori_loop(0, 8, one, 0)
+            for k in range(4):
+                self.got(1, k, 1)
+                b = self.block(lax.rem(z + 4 - k, 4) * 4 + near_xy)
+                self.push(b, b, 2, k, far)
 
         def s4(self):
-            self.recv(2, 8)
-            m = self.many(16)
-            send(m, m, gs.at[self.n, 3], gr.at[self.n, 3], me, other).start()
+            for k in range(4):
+                self.got(2, k, 2)
+                p = self.buf.at[pl.ds(al(lax.rem(z + 4 - k, 4) * 4 * self.rows, 16), 4 * self.rows), self.cols(c)]
+                send(p, p, gs.at[self.n, 3], gr.at[self.n, 12], me, other).start()
 
         def done(self):
-            n = self.buf.at[pl.ds(0, 16 * self.rows), self.cols(other)]
-            send(n, n, gs.at[self.n, 3], gr.at[self.n, 3], me, other).wait_recv()
+            m = self.region(16, other)
+            send(m, m, gs.at[self.n, 3], gr.at[self.n, 12], me, other).wait_recv()
 
         def drain(self):
             for stage, k in ((0, 3), (1, 4), (2, 8), (3, 16)):
-                self.sent(stage, k)
-
-    w_in = Piece(0, win_s, win, 48, 0, 1152)
-    w_out = Piece(1, wout_s, wout, 48, 0, 384)
-    w_exp = [Piece(2 + k, wexp_s, wexp, 48, 1536 * k, 768) for k in range(2)]
-    w_con = [Piece(4 + k, wcon_s, wcon, 192, 256 * k, 128) for k in range(3)]
-    SM = 7
+                m = self.region(k)
+                send(m, m, gs.at[self.n, stage], gr.at[self.n, 12], me, other).wait_send()
+
+    near_xy = xy + (1 - c) * (1 - 2 * x) + c * (2 - 4 * y)
+    pieces = [
+        Piece(g, wide, 48, g * 768, 384, [(win_s, k * D + g * 256, 128) for k in range(3)]) for g in range(3)
+    ]
+    pieces += [Piece(3, wide, 48, OUT, 384, [(wout_s, 0, 384)])]
+    pieces += [Piece(4 + k, wide, 48, EXP + k * 768, 384, [(wexp_s, k * 768, 384)]) for k in range(4)]
+    pieces += [Piece(8 + k, wcon, 192, k * 256, 128, [(wcon_s, k * 256, 128)]) for k in range(3)]
+    EARLY = 3
+
+    def s2(t):
+        pieces[t].s2(t < EARLY)
+
+    def s3(t):
+        pieces[t].s3()
+
+    def s4(t):
+        pieces[t].s4()
+
+    SM = 11
 
     def small(stage, k, recv):
         d = send(vec.at[pl.ds(0, k)], vec.at[pl.ds(0, k)], gs.at[SM, stage], gr.at[SM, stage], me, other)
@@ -143,19 +166,18 @@
 
     swap_tok = send(tokens, tokr, swap_sem.at[0, 0], swap_sem.at[0, 1], me, other)
     swap_cot = send(cot, cotr, swap_sem.at[1, 0], swap_sem.at[1, 1], me, other)
-    own_tok = pltpu.make_async_copy(tokens, tok, ls.at[8])
-    own_cot = pltpu.make_async_copy(cot, cotn, ls.at[9])
-    own_vec = pltpu.make_async_copy(small_s, vec.at[me], ls.at[10])
-
+    own_tok = pltpu.make_async_copy(tokens, tok, ls.at[11])
+    own_cot = pltpu.make_async_copy(cot, cotn, ls.at[12])
+    own_vec = pltpu.make_async_copy(small_s, vec.at[me], ls.at[13])
+
+    pieces[0].s1(True)
     own_tok.start()
     own_vec.start()
-    w_in.s1()
+    swap_tok.start()
     for q in zs:
         send(small_s, vec.at[me], gs.at[SM, 0], gr.at[SM, 0], q, c).start()
-    swap_tok.start()
-    w_out.s1()
-    for p in w_exp + w_con:
-        p.s1()
+    for t, p in enumerate(pieces[1:]):
+        p.s1(t + 1 < EARLY)
     swap_cot.start()
     own_cot.start()
 
@@ -180,6 +202,17 @@
         return 0
 
     lax.fori_loop(0, T // 128, mask_rows, 0)
+    s2(0)
+    own_vec.wait()
+    small(0, 3, True)
+
+    def small2(k, _):
+        b = vec.at[k * 4 + xy]
+        send(b, b, gs.at[SM, 1], gr.at[SM, 1], near, c).start()
+        return 0
+
+    lax.fori_loop(0, 4, small2, 0)
+    s3(0)
     own_tok.wait()
     swap_tok.wait_recv()
 
@@ -191,18 +224,8 @@
         return 0
 
     lax.fori_loop(0, T // 128, start_rows, 0)
-
-    w_in.s2()
-    own_vec.wait()
-    small(0, 3, True)
-
-    def small2(k, _):
-        b = vec.at[k * 4 + xy]
-        send(b, b, gs.at[SM, 1], gr.at[SM, 1], near, c).start()
-        return 0
-
-    lax.fori_loop(0, 4, small2, 0)
-    w_in.s3()
+    s2(1)
+    s4(0)
     small(1, 4, True)
 
     def small3(k, _):
@@ -211,24 +234,21 @@
         return 0
 
     lax.fori_loop(0, 8, small3, 0)
-    w_out.s2()
-    w_in.s4()
+    s3(1)
     small(2, 8, True)
     for o in range(16):
         fullv[:, o * 48 : (o + 1) * 48] = vec[o][:, :48].astype(F32)
         for k in range(4):
             fulle[:, o * 192 + k * 48 : o * 192 + (k + 1) * 48] = vec[o][k : k + 1, 64:112].astype(F32)
-    w_in.done()
-
-    for j in range(3):
-        v = nn(xl[...], win[:, j * D : (j + 1) * D])
-        if j == 0:
-            v = (v + fullv[0:1, :]).astype(BF) * jnp.asarray(HD**-0.5, BF)
-        elif j == 1:
-            v = v.astype(BF)
-        else:
-            v = (v + fullv[1:2, :]).astype(BF)
-        proj[:, j * D : (j + 1) * D] = v
+    fullp[...] = jnp.concatenate([jnp.zeros_like(fullp[0:1, :]), jnp.ones_like(fullp[0:1, :])], axis=0)
+    for h in range(D // 128):
+        fullp[0:1, h * 384 : h * 384 + 128] = fullv[0:1, h * 128 : (h + 1) * 128]
+        fullp[0:1, h * 384 + 256 : h * 384 + 384] = fullv[1:2, h * 128 : (h + 1) * 128]
+        fullp[1:2, h * 384 : h * 384 + 128] = jnp.full((1, 128), HD**-0.5, F32)
+
+    def project(g):
+        cs = pl.ds(al(g * 768, 768), 768)
+        proj[:, cs] = ((nn(xl[...], wide[:, cs]) + fullp[0:1, cs]) * fullp[1:2, cs]).astype(BF)
 
     lane = lax.broadcasted_iota(jnp.int32, (1, 128), 1)
     halves = (lane < HD, lane >= HD)
@@ -238,19 +258,29 @@
         return pltpu.make_async_copy(pslot.at[a], spill.at[h * 2 + a], ps.at[a])
 
     tasks = [
-        [w_out.s3, w_exp[0].s2],
-        [w_out.s4, w_exp[0].s3],
-        [w_exp[0].s4, w_exp[1].s2],
-        [w_exp[1].s3, w_con[0].s2],
-        [w_exp[1].s4, w_con[0].s3, w_con[1].s2],
-        [w_con[0].s4, w_con[1].s3],
+        lambda: (s2(2), s4(1)),
+        lambda: (s2(3), s3(2)),
+        lambda: (s4(2), s2(4), s3(3)),
+        lambda: (s2(5),),
+        lambda: (s4(3), s3(4)),
+        lambda: (s2(6), s4(4), s3(5)),
     ]
 
     def attend(h, _):
-        cs = al(h * 128, 128)
+        for g in range(3):
+
+            @pl.when(h == 2 * g)
+            def _():
+                pieces[g].done()
+
+        @pl.when(lax.rem(h, 2) == 0)
+        def _():
+            project(h // 2)
+
+        cs = al(h * 384, 128)
         q2 = proj[:, pl.ds(cs, 128)]
-        k2 = proj[:, pl.ds(D + cs, 128)]
-        v2 = proj[:, pl.ds(2 * D + cs, 128)]
+        k2 = proj[:, pl.ds(cs + 128, 128)]
+        v2 = proj[:, pl.ds(cs + 256, 128)]
         outs = []
         for a in range(2):
             s = nt(jnp.where(halves[a], q2, jnp.zeros_like(q2)), k2) + bias[...]
@@ -264,18 +294,17 @@
             pslot[a] = p
             keep(h, a).start()
             outs.append(nn(p, v2))
-        heads[:, pl.ds(cs, 128)] = jnp.where(halves[0], outs[0], outs[1]).astype(BF)
+        heads[:, pl.ds(al(h * 128, 128), 128)] = jnp.where(halves[0], outs[0], outs[1]).astype(BF)
         for k in range(pairs):
 
             @pl.when(h == k)
             def _():
-                for t in tasks[k]:
-                    t()
+                tasks[k]()
 
         return 0
 
     lax.fori_loop(0, pairs, attend, 0)
-    w_out.done()
+    pieces[3].done()
 
     def load(h, a):
         return pltpu.make_async_copy(spill.at[h * 2 + a], pslot.at[a], pd.at[a])
@@ -291,7 +320,7 @@
 
     def first_rows(i, _):
         r = pl.ds(al(i * 256, 256), 256)
-        v = n1[r, :] + (nn(heads[r, :], wout[...]) + fullv[2:3, :])
+        v = n1[r, :] + (nn(heads[r, :], wide[:, OUT:EXP]) + fullv[2:3, :])
         n, s = normalize(v)
         n1[r, :] = n
         sc1[r, 1:2] = s
@@ -299,24 +328,52 @@
         return 0
 
     lax.fori_loop(0, T // 256, first_rows, 0)
-    w_con[2].s2()
-    w_exp[0].done()
-    w_exp[1].done()
-    w_con[1].s4()
-    w_con[2].s3()
+    s2(7)
+    s4(5)
+    s3(6)
+    after = [
+        lambda: (s2(8), s4(6), s3(7)),
+        lambda: (s2(9), s4(7), s3(8)),
+        lambda: (s2(10), s4(8), s3(9)),
+        lambda: (s4(9), s3(10)),
+    ]
 
     def expand(i, _):
-        cs = pl.ds(al(i * 512, 512), 512)
-        u = nn(fl[...], wexp[:, cs]) + fulle[:, cs]
+        for k in range(4):
+
+            @pl.when(i == k)
+            def _():
+                pieces[4 + k].done()
+
+        cs = pl.ds(al(i * 768, 768), 768)
+        u = nn(fl[...], wide[:, pl.ds(al(EXP + i * 768, 768), 768)]) + fulle[:, cs]
         cdf = 0.5 * (1.0 + lax.erf(u * math.sqrt(0.5)))
         hidden[:, cs] = (u * cdf).astype(BF)
         slope[:, cs] = (cdf + u * jnp.exp(-0.5 * u * u) * (1.0 / math.sqrt(2.0 * math.pi))).astype(BF)
-        return 0
-
-    lax.fori_loop(0, FF // 512, expand, 0)
-    w_con[2].s4()
-    for p in w_con:
-        p.done()
+        for k in range(4):
+
+            @pl.when(i == k)
+            def _():
+                after[k]()
+
+        return 0
+
+    lax.fori_loop(0, FF // 768, expand, 0)
+
+    def contract(i, _):
+        for k in range(3):
+
+            @pl.when(i == k)
+            def _():
+                if k == 1:
+                    s4(10)
+                pieces[8 + k].done()
+
+        cs = pl.ds(al(i * 256, 256), 256)
+        sg[:, cs] = nn(hidden[...], wcon[:, cs]) + fullv[5:6, cs]
+        return 0
+
+    lax.fori_loop(0, D // 256, contract, 0)
     own_cot.wait()
     swap_cot.wait_recv()
 
@@ -324,7 +381,7 @@
 
     def second_rows(i, _):
         r = pl.ds(al(i * 256, 256), 256)
-        v = n1[r, :] * fullv[3:4, :] + fullv[4:5, :] + (nn(hidden[r, :], wcon[...]) + fullv[5:6, :])
+        v = n1[r, :] * fullv[3:4, :] + fullv[4:5, :] + sg[r, :]
         n, s = normalize(v)
         lonew[r, :] = (n * fullv[6:7, :] + fullv[7:8, :]).astype(BF)
         og = jnp.where(sc1[r, 0:1] > 0.5, cotn[r, :].astype(F32), cotr[r, :].astype(F32))
@@ -346,7 +403,6 @@
     my_k = (1 - c) * x + c * y
     far_base = (1 - c) * (2 - 2 * y) + c * (1 - x)
     own_base = (1 - c) * 2 * y + c * x
-    near_xy = xy + (1 - c) * (1 - 2 * x) + c * (2 - 4 * y)
     step_k = 1 + c
 
     def total(*refs):
@@ -359,6 +415,7 @@
         def __init__(self, n, g, col, rows, recv, rcol, fsum, plane=None):
             self.n, self.g, self.col, self.rows, self.recv, self.rcol, self.fsum = n, g, col, rows, recv, rcol, fsum
             self.plane = plane
+            self.fcol = (n - 4) * 768 if 4 <= n < 8 else 0
 
         def cols(self, core):
             return pl.ds(al(self.col + core * S, 128), S)
@@ -467,7 +524,7 @@
                     b[...] = t[:, k * 128 : (k + 1) * 128]
                     send(b, b, s, r, me, other).start()
             else:
-                b = self.fsum.at[:, self.cols(c)]
+                b = self.fsum.at[:, pl.ds(al(self.fcol + c * S, 128), S)]
                 b[...] = t
                 send(b, b, s, r, me, other).start()
 
@@ -485,44 +542,45 @@
                 self.gone(4, half)
                 self.got(4, half)
 
-    con = {j: Red(j, wcon, 0, 192, con_r, j * 1344, fcon, plane=lax.rem(z + j, 4)) for j in range(4)}
-    exp = [Red(4 + k, wexp, k * 768, 48, hidden, k * 768, fexp) for k in range(4)]
-    out = Red(8, wout, 0, 48, slope, 2304, fout)
+    con = {j: Red(j, gcon, 0, 192, con_r, j * 1344, fcon, plane=lax.rem(z + j, 4)) for j in range(4)}
+    exp = [Red(4 + k, wide, EXP + k * 768, 48, hidden, k * 768, fexp) for k in range(4)]
+    out = Red(8, wide, OUT, 48, cotn, 0, fout)
     ins = [Red(9 + k, gin, k * 768, 48, slope, k * 768, fin) for k in range(3)]
 
-    def expand_back(i, _):
-        cs = pl.ds(al(i * 512, 512), 512)
-        g = (nt(bg[...], wcon[cs, :]) * slope[:, cs].astype(F32)).astype(BF)
-        slope[:, cs] = g
-        ge[:, cs] = jnp.sum(g.astype(F32), axis=0, keepdims=True)
-        return 0
-
-    lax.fori_loop(0, FF // 512, expand_back, 0)
-    for p in w_con:
-        p.drain()
-
-    def grad_con(i, _):
-        p = al(lax.rem(z + i + 1, 4) * 768, 768)
-        wcon[pl.ds(p, 768), :] = tn(hidden[:, pl.ds(p, 768)], bg[...]).astype(BF)
-        for k, t in enumerate([
-            [con[1].P],
-            [con[2].P, con[1].A],
-            [con[3].P, con[2].A],
-            [con[0].P, con[3].A],
-        ]):
+    def run_at(i, lists):
+        for k, t in lists.items():
 
             @pl.when(i == k)
             def _():
                 for u in t:
                     u()
 
+    def grad_con(i, _):
+        p = al(lax.rem(z + i + 1, 4) * 768, 768)
+        gcon[pl.ds(p, 768), :] = tn(hidden[:, pl.ds(p, 768)], bg[...]).astype(BF)
+        run_at(i, {
+            0: [con[1].P],
+            1: [con[2].P, con[1].A],
+            2: [con[3].P, con[2].A],
+            3: [con[0].P, con[3].A],
+        })
         return 0
 
     lax.fori_loop(0, 4, grad_con, 0)
+
+    def expand_back(i, _):
+        cs = pl.ds(al(i * 768, 768), 768)
+        g = (nt(bg[...], wcon[cs, :]) * slope[:, cs].astype(F32)).astype(BF)
+        slope[:, cs] = g
+        ge[:, cs] = jnp.sum(g.astype(F32), axis=0, keepdims=True)
+        run_at(i, {0: [con[0].A], 1: [con[1].B], 3: [con[2].B]})
+        return 0
+
+    lax.fori_loop(0, FF // 768, expand_back, 0)
 
     def first_back(i, _):
         r = pl.ds(al(i * 256, 256), 256)
-        g = sg[r, :] + nt(slope[r, :], wexp[...])
+        g = sg[r, :] + nt(slope[r, :], wide[:, EXP:])
         n = n1[r, :]
         gv[3:4, :] += jnp.sum(g * n, axis=0, keepdims=True)
         gv[4:5, :] += jnp.sum(g, axis=0, keepdims=True)
@@ -532,63 +590,49 @@
         low = g.astype(BF)
         bg[r, :] = low
         gv[2:3, :] += jnp.sum(low.astype(F32), axis=0, keepdims=True)
-        for k, t in enumerate([[con[0].A, con[1].B], [con[2].B], [con[3].B]]):
-
-            @pl.when(i == k)
-            def _():
-                for u in t:
-                    u()
-
+        run_at(i, {0: [con[3].B], 1: [lambda: con[1].Z(1)], 2: [con[0].B, lambda: con[2].Z(2)]})
         return 0
 
     lax.fori_loop(0, T // 256, first_back, 0)
-    for p in w_exp:
+    for p in pieces[4:8]:
         p.drain()
-    con[0].B()
 
     def grad_exp(i, _):
         cs = pl.ds(al(i * 768, 768), 768)
-        wexp[:, cs] = tn(fl[...], slope[:, cs]).astype(BF)
-        for k, t in enumerate([
-            [exp[0].P, lambda: con[1].Z(1)],
-            [exp[1].P, exp[0].A, lambda: con[2].Z(2)],
-            [exp[2].P, exp[1].A, lambda: con[3].Z(3)],
-            [exp[3].P, exp[2].A, lambda: con[0].Z(0), exp[0].B],
-        ]):
-
-            @pl.when(i == k)
-            def _():
-                for u in t:
-                    u()
-
+        wide[:, pl.ds(al(EXP + i * 768, 768), 768)] = tn(fl[...], slope[:, cs]).astype(BF)
+        run_at(i, {
+            0: [exp[0].P, lambda: con[3].Z(3)],
+            1: [exp[1].P, exp[0].A, lambda: con[0].Z(0)],
+            2: [exp[2].P, exp[1].A],
+            3: [exp[3].P, exp[2].A, con[0].F],
+        })
         return 0
 
     lax.fori_loop(0, 4, grad_exp, 0)
     hg = cotr
-    hg[...] = nt(bg[...], wout[...]).astype(BF)
+    hg[...] = nt(bg[...], wide[:, OUT:EXP]).astype(BF)
     exp[3].A()
-    exp[1].B()
-    w_out.drain()
-    wout[...] = tn(heads[...], bg[...]).astype(BF)
+    pieces[3].drain()
+    wide[:, OUT:EXP] = tn(heads[...], bg[...]).astype(BF)
     out.P()
-    con[0].F()
 
     tasks = [
-        [exp[2].B, exp[0].Z],
-        [exp[3].B, exp[1].Z],
-        [out.A, exp[2].Z, exp[0].F],
-        [exp[3].Z, ins[0].A, exp[1].F],
-        [out.B, exp[2].F, exp[3].F],
-        [ins[0].B, out.Z, ins[1].A],
+        [exp[0].B],
+        [exp[1].B, exp[0].Z],
+        [out.A],
+        [exp[2].B, ins[0].A, exp[1].Z],
+        [exp[3].B, exp[2].Z, exp[0].F, ins[1].A],
+        [exp[3].Z, out.B, exp[1].F],
     ]
 
     def attend_back(h, _):
-        cs = al(h * 128, 128)
+        cs = al(h * 384, 128)
+        hs = pl.ds(al(h * 128, 128), 128)
         q2 = proj[:, pl.ds(cs, 128)]
-        k2 = proj[:, pl.ds(D + cs, 128)]
-        v2 = proj[:, pl.ds(2 * D + cs, 128)]
-        g2 = hg[:, pl.ds(cs, 128)]
-        prod = g2.astype(F32) * heads[:, pl.ds(cs, 128)].astype(F32)
+        k2 = proj[:, pl.ds(cs + 128, 128)]
+        v2 = proj[:, pl.ds(cs + 256, 128)]
+        g2 = hg[:, hs]
+        prod = g2.astype(F32) * heads[:, hs].astype(F32)
         qt = q2.astype(F32).T.astype(BF)
         gt = g2.astype(F32).T.astype(BF)
         dq, dk, dv = [], [], []
@@ -610,18 +654,15 @@
         dk = jnp.concatenate(dk, axis=0).T.astype(BF)
         dv = jnp.concatenate(dv, axis=0).T.astype(BF)
         proj[:, pl.ds(cs, 128)] = dq
-        proj[:, pl.ds(D + cs, 128)] = dk
-        proj[:, pl.ds(2 * D + cs, 128)] = dv
-        gv[0:1, pl.ds(cs, 128)] = jnp.sum(dq.astype(F32), axis=0, keepdims=True)
-        gv[1:2, pl.ds(cs, 128)] = jnp.sum(dv.astype(F32), axis=0, keepdims=True)
+        proj[:, pl.ds(cs + 128, 128)] = dk
+        proj[:, pl.ds(cs + 256, 128)] = dv
+        gv[0:1, hs] = jnp.sum(dq.astype(F32), axis=0, keepdims=True)
+        gv[1:2, hs] = jnp.sum(dv.astype(F32), axis=0, keepdims=True)
 
         @pl.when(lax.rem(h, 2) == 1)
         def _():
-            g = al((h // 2) * 256, 256)
-            cols = jnp.concatenate(
-                [proj[:, pl.ds(al(k * D + g + e * 128, 128), 128)] for e in range(2) for k in range(3)], axis=1
-            )
-            gin[:, pl.ds(al((h // 2) * 768, 768), 768)] = tn(xl[...], cols).astype(BF)
+            cols = pl.ds(al((h // 2) * 768, 768), 768)
+            gin[:, cols] = tn(xl[...], proj[:, cols]).astype(BF)
 
         for k in range(pairs):
 
@@ -651,14 +692,8 @@
 
     def input_rows(i, _):
         r = pl.ds(al(i * 256, 256), 256)
-        sg[r, :] = sg[r, :] + nt(proj[r, :], win[...])
-        for k, t in enumerate([[ins[1].B], [ins[0].Z], [ins[2].B]]):
-
-            @pl.when(i == k)
-            def _():
-                for u in t:
-                    u()
-
+        sg[r, :] = sg[r, :] + nt(proj[r, :], wide[:, IN:OUT])
+        run_at(i, {0: [exp[2].F, ins[0].B], 1: [exp[3].F, out.Z], 2: [ins[1].B]})
         return 0
 
     lax.fori_loop(0, T // 256, input_rows, 0)
@@ -669,7 +704,8 @@
     for i in range(8):
         b = vsum.at[(i // 2) * 4 + 2 - 2 * y + i % 2]
         vsend(1, b, vr.at[16 + i], flip_y, c).start()
-    ins[1].Z()
+    ins[0].Z()
+    ins[2].B()
     vsend(1, vr.at[pl.ds(16, 8)], vr.at[pl.ds(16, 8)], me, other).wait_recv()
     for i in range(8):
         o = (i // 2) * 4 + 2 * y + i % 2
@@ -677,16 +713,18 @@
     for i in range(4):
         b = vsum.at[i * 4 + 2 * y + 1 - x]
         vsend(2, b, vr.at[24 + i], flip_x, c).start()
-    ins[2].Z()
+    ins[1].Z()
+    out.F()
     vsend(2, vr.at[pl.ds(24, 4)], vr.at[pl.ds(24, 4)], me, other).wait_recv()
     for i in range(4):
         vsum[i * 4 + xy] = vsum[i * 4 + xy] + vr[24 + i]
     for k in range(3):
         b = vsum.at[lax.rem(z + k + 1, 4) * 4 + xy]
         vsend(3, b, vr.at[28 + k], zs[k], c).start()
-    out.F()
-    for p in ins:
-        p.F()
+    ins[0].F()
+    ins[2].Z()
+    ins[1].F()
+    ins[2].F()
 
     swap_lo.wait()
 
@@ -696,7 +734,7 @@
         return 0
 
     lax.fori_loop(0, T // 128, out_rows, 0)
-    lo_done = pltpu.make_async_copy(lonew, lo_o, ls.at[11])
+    lo_done = pltpu.make_async_copy(lonew, lo_o, ls.at[14])
     lo_done.start()
     swap_ig.wait()
 
@@ -706,16 +744,17 @@
         return 0
 
     lax.fori_loop(0, T // 128, grad_rows, 0)
-    outs = [lo_done, pltpu.make_async_copy(sg, ig_o, ls.at[12])]
+    outs = [lo_done, pltpu.make_async_copy(sg, ig_o, ls.at[15])]
     outs[1].start()
     vsend(3, vr.at[pl.ds(28, 3)], vr.at[pl.ds(28, 3)], me, other).wait_recv()
     vfin = vr.at[31]
     vfin[...] = vsum[z * 4 + xy] + vr[28] + vr[29] + vr[30]
-    outs.append(pltpu.make_async_copy(vfin, gvec_o, ls.at[13]))
+    outs.append(pltpu.make_async_copy(vfin, gvec_o, ls.at[16]))
     outs[2].start()
     swap_tok.wait_send()
     swap_cot.wait_send()
-    w_in.drain()
+    for p in pieces[0:3] + pieces[8:]:
+        p.drain()
     for stage, k in ((0, 3), (1, 4), (2, 8)):
         small(stage, k, False)
         vsend(stage + 1, vr.at[pl.ds(0, (8, 4, 3)[stage])], vr.at[pl.ds(0, (8, 4, 3)[stage])], me, other).wait_send()
@@ -723,7 +762,7 @@
     for p in list(con.values()) + exp + [out] + ins:
         p.end()
     for k, (v, o) in enumerate([(fin, gin_o), (fout, gout_o), (fexp, gexp_o), (fcon, gcon_o)]):
-        outs.append(pltpu.make_async_copy(v, o, ls.at[14 + k]))
+        outs.append(pltpu.make_async_copy(v, o, ls.at[17 + k]))
         outs[-1].start()
     for o in outs:
         o.wait()
@@ -736,16 +775,16 @@
     anyspec = pl.BlockSpec(memory_space=pl.ANY)
     vspec = pl.BlockSpec(memory_space=VM)
     scratch = [
-        VM((D, 3 * D), BF), VM((D, D), BF), VM((D, FF), BF), VM((FF, D), BF),
+        VM((D, 4 * D + FF), BF), VM((FF, D), BF),
         VM((T, D), BF), VM((T, D), BF), VM((T, D), BF), VM((T, D), BF),
-        VM((16, 16, 128), BF), VM((16, D), F32), VM((1, FF), F32),
+        VM((16, 16, 128), BF), VM((16, D), F32), VM((1, FF), F32), VM((2, 3 * D), F32),
         VM((T, 3 * D), BF), VM((T, D), BF), VM((T, D), F32), VM((T, T), F32),
         VM((T, 2), F32), VM((T, D), BF), VM((T, D), BF), VM((T, FF), BF), VM((T, FF), BF),
-        VM((2, T, T), BF), VM((T, D), BF), VM((T, D), BF), VM((T, D), F32), VM((T, D), BF),
-        VM((D, 3 * D), BF), VM((5952, 384), BF), VM((8, D), F32), VM((1, FF), F32),
+        VM((2, T, T), BF), VM((T, D), BF),
+        VM((D, 3 * D), BF), VM((FF, D), BF), VM((5952, 384), BF), VM((8, D), F32), VM((1, FF), F32),
         VM((16, 8, 128), F32), VM((16, 8, 128), F32), VM((32, 8, 128), F32),
         VM(iw.shape, F32), VM(ow.shape, F32), VM(ew.shape, F32), VM(cw.shape, F32),
-        DMA((4, 2)), DMA((18,)), DMA((8, 4)), DMA((8, 4)), DMA((2,)), DMA((13, 5)), DMA((13, 5)), DMA((2,)),
+        DMA((4, 2)), DMA((21,)), DMA((12, 4)), DMA((12, 13)), DMA((2,)), DMA((13, 5)), DMA((13, 5)), DMA((2,)),
     ]
     return pl.pallas_call(
         fused_kernel,

time: 224 us -> 189 us (0.84)
  Pallas kernels: 211 us -> 176 us
    pallas_call x1, Pallas kernels: 211 us -> 176 us  [fused_layer(): pl.pallas_call(fused_kernel, out_shape=(sh((T, D), BF), sh((T, D), F32),...]
where the time goes in v2:
time: 189 us
  Pallas kernels  176 us (93%)
  local copies, waits for them, and re-layouts  11.4 us (6%)
    pallas_call x1, Pallas kernels, fused_layer(): pl.pallas_call(fused_kernel, out_shape=(sh((T, D), BF), sh((T, D), F32),...  176 us
    unnamed x16, local copies, waits for them, and re-layouts  6.99 us

profile of v2, /device:TPU:0, one launch (start us, length us, event | category | flops | bytes accessed | tf_op | source)
XLA Modules:
  0.0 188.6 jit_solution(7841881329023282572)
XLA Ops:
  0.6 0.7 reshape.36
  1.4 0.8 stack.35
  2.2 0.7 fusion.2.small_s
  2.9 175.9 %shard_map.280 = (bf16[768,768]{1,0:T(8,128)(2,1)}, f32[768,768]{1,0:T(8,128)}, f32[48,2304]{1,0:T(8,128)}, f32[48,768]{1,0:T(8,128)}, f32[48,3072]{1,0:T(8,128)...) custom-call(bf16[768,768]{1,0:T(8,128)(2,1)} %bitcast.30, bf16[768,768]{1,0:T(8,128)(2,1)} %bitcast.31, ...), custom_call_target="tpu_custom_call" | custom-call | tf_op jit(solution)/shard_map/pallas_call | solution.py:789
  178.7 0.8 slice.32
  179.5 0.6 reshape.37
  180.1 1.5 slice_bitcast_fusion
  181.6 0.0 copy-start
  181.6 2.5 %copy.38 = bf16[1,768,768]{2,1,0:T(8,128)(2,1)} copy(bf16[1,768,768]{2,1,0:T(8,128)(2,1)} %bitcast.29) | data formatting | bytes 2359296
  184.2 0.0 copy-done
  184.2 0.0 copy-start.3
  184.2 0.0 copy-start.4
  184.2 1.4 copy.39
  185.6 0.0 copy-done.3
  185.6 0.0 copy-start.2
  185.6 0.0 copy-start.1
  185.6 0.8 copy.40
  186.3 0.0 copy-done.4
  186.3 0.7 copy.41
  187.0 0.0 copy-done.2
  187.0 0.8 copy.42
  187.8 0.0 copy-done.1
  187.8 0.8 copy.43
Async XLA Ops:
  181.6 2.5 %copy-start = (f32[768,768]{1,0:T(8,128)S(1)}, f32[768,768]{1,0:T(8,128)}, u32[]{:S(2)}) copy-start(f32[768,768]{1,0:T(8,128)} %get-tuple-element.23) | copy-start | bytes 7077892
  184.2 1.4 copy-start.3
  184.2 2.2 %copy-start.4 = (f32[48,768]{1,0:T(8,128)S(1)}, f32[48,768]{1,0:T(8,128)}, u32[]{:S(2)}) copy-start(f32[48,768]{1,0:T(8,128)} %get-tuple-element.57) | copy-start | bytes 442372
  185.6 1.4 copy-start.2
  185.6 2.2 %copy-start.1 = (f32[192,768]{1,0:T(8,128)S(1)}, f32[192,768]{1,0:T(8,128)}, u32[]{:S(2)}) copy-start(f32[192,768]{1,0:T(8,128)} %get-tuple-element.63) | copy-start | bytes 1769476

commit v3 on v2

--- a/solution.py
+++ b/solution.py
@@ -35,7 +35,7 @@
     wide, wcon, tok, tokr, cotn, cotr, vec, fullv, fulle, fullp, proj, xl, n1, sg,
     sc1, heads, fl, hidden, slope, pslot, bg,
     gin, gcon, con_r, gv, ge, vout, vsum, vr, fin, fout, fexp, fcon,
-    swap_sem, ls, gs, gr, ps, rs, rr, pd,
+    swap_sem, sw3, ls, gs, gr, vs, ps, rs, rr, pd,
 ):
     T, D = tok.shape
     FF = wcon.shape[0]
@@ -83,12 +83,15 @@
         def region(self, k, core=c):
             return self.buf.at[pl.ds(0, k * self.rows), self.cols(core)]
 
+        def arrival(self, stage, k):
+            return gr.at[stage * 4 + k] if self.n == 0 and stage < 3 else gr.at[12 + self.n * 4 + stage]
+
         def push(self, src, dst, stage, k, dp):
-            send(src, dst, gs.at[self.n, stage], gr.at[self.n, stage * 4 + k], dp, c).start()
+            send(src, dst, gs.at[self.n], self.arrival(stage, k), dp, c).start()
 
         def got(self, stage, k, blocks):
             m = self.region(blocks)
-            send(m, m, gs.at[self.n, stage], gr.at[self.n, stage * 4 + k], me, other).wait_recv()
+            send(m, m, gs.at[self.n], self.arrival(stage, k), me, other).wait_recv()
 
         def own(self):
             base = pl.ds(al(me * self.rows, 16), self.rows)
@@ -98,47 +101,72 @@
                     self.buf.at[base, pl.ds(al(self.col + c * self.half + i * width, 128), width)],
                 )
 
-        def s1(self, early):
+        def s1(self):
             for k in range(3):
                 for a, b in self.own():
                     self.push(a, b, 0, k + 1, zs[k])
-            if early:
-                for a, b in self.own():
-                    self.push(a, b, 1, 0, near)
-                    self.push(a, b, 2, 0, far)
             for a, b in self.own():
                 pltpu.make_async_copy(a, b, ls.at[self.n]).start()
 
-        def s2(self, early):
-            m = self.block(me)
-            pltpu.make_async_copy(m, m, ls.at[self.n]).wait()
-            for k in range(1 if early else 0, 4):
-                if k > 0:
-                    self.got(0, k, 1)
-                b = self.block(lax.rem(z + 4 - k, 4) * 4 + xy)
-                self.push(b, b, 1, k, near)
-                self.push(b, b, 2, k, far)
-
-        def s3(self):
-            for k in range(4):
+        def s2o(self):
+            for a, b in self.own():
+                self.push(a, b, 1, 0, near)
+                self.push(a, b, 2, 0, far)
+
+        def s2(self, k=None):
+            if k is None:
+                self.got(0, 0, 3)
+            else:
+                self.got(0, k, 1)
+
+            def one(i, _):
+                b = self.block(lax.rem(z + 4 - i, 4) * 4 + xy)
+                self.push(b, b, 1, i, near)
+                self.push(b, b, 2, i, far)
+                return 0
+
+            if k is None:
+                lax.fori_loop(1, 4, one, 0)
+            else:
+                one(k, 0)
+
+        def s3(self, k=None):
+            if k is None:
+                self.got(1, 0, 4)
+            else:
                 self.got(1, k, 1)
-                b = self.block(lax.rem(z + 4 - k, 4) * 4 + near_xy)
-                self.push(b, b, 2, k, far)
-
-        def s4(self):
-            for k in range(4):
+
+            def one(i, _):
+                b = self.block(lax.rem(z + 4 - i, 4) * 4 + near_xy)
+                self.push(b, b, 2, i, far)
+                return 0
+
+            if k is None:
+                lax.fori_loop(0, 4, one, 0)
+            else:
+                one(k, 0)
+
+        def s4(self, k=None):
+            if k is None:
+                self.got(2, 0, 8)
+            else:
                 self.got(2, k, 2)
+            if not k:
+                m = self.block(me)
+                pltpu.make_async_copy(m, m, ls.at[self.n]).wait()
+            if k is None:
+                p = self.region(16)
+            else:
                 p = self.buf.at[pl.ds(al(lax.rem(z + 4 - k, 4) * 4 * self.rows, 16), 4 * self.rows), self.cols(c)]
-                send(p, p, gs.at[self.n, 3], gr.at[self.n, 12], me, other).start()
+            send(p, p, gs.at[self.n], self.arrival(3, 0), me, other).start()
 
         def done(self):
             m = self.region(16, other)
-            send(m, m, gs.at[self.n, 3], gr.at[self.n, 12], me, other).wait_recv()
+            send(m, m, gs.at[self.n], self.arrival(3, 0), me, other).wait_recv()
 
         def drain(self):
-            for stage, k in ((0, 3), (1, 4), (2, 8), (3, 16)):
-                m = self.region(k)
-                send(m, m, gs.at[self.n, stage], gr.at[self.n, 12], me, other).wait_send()
+            m = wide.at[pl.ds(0, 496), pl.ds(0, self.rows * self.half // 16)]
+            send(m, m, gs.at[self.n], self.arrival(3, 0), me, other).wait_send()
 
     near_xy = xy + (1 - c) * (1 - 2 * x) + c * (2 - 4 * y)
     pieces = [
@@ -147,21 +175,22 @@
     pieces += [Piece(3, wide, 48, OUT, 384, [(wout_s, 0, 384)])]
     pieces += [Piece(4 + k, wide, 48, EXP + k * 768, 384, [(wexp_s, k * 768, 384)]) for k in range(4)]
     pieces += [Piece(8 + k, wcon, 192, k * 256, 128, [(wcon_s, k * 256, 128)]) for k in range(3)]
-    EARLY = 3
-
-    def s2(t):
-        pieces[t].s2(t < EARLY)
-
-    def s3(t):
-        pieces[t].s3()
-
-    def s4(t):
-        pieces[t].s4()
-
-    SM = 11
+    loose = {}
+
+    def run(ops):
+        for op in ops:
+            name, _, rest = op.partition(":")
+            if op in loose:
+                loose[op]()
+            elif "." in rest:
+                p, k = rest.split(".")
+                getattr(pieces[int(p)], name)(int(k))
+            else:
+                getattr(pieces[int(rest)], name)()
+
 
     def small(stage, k, recv):
-        d = send(vec.at[pl.ds(0, k)], vec.at[pl.ds(0, k)], gs.at[SM, stage], gr.at[SM, stage], me, other)
+        d = send(vec.at[pl.ds(0, k)], vec.at[pl.ds(0, k)], vs.at[stage], vs.at[3 + stage], me, other)
         d.wait_recv() if recv else d.wait_send()
 
     swap_tok = send(tokens, tokr, swap_sem.at[0, 0], swap_sem.at[0, 1], me, other)
@@ -170,16 +199,17 @@
     own_cot = pltpu.make_async_copy(cot, cotn, ls.at[12])
     own_vec = pltpu.make_async_copy(small_s, vec.at[me], ls.at[13])
 
-    pieces[0].s1(True)
     own_tok.start()
     own_vec.start()
-    swap_tok.start()
     for q in zs:
-        send(small_s, vec.at[me], gs.at[SM, 0], gr.at[SM, 0], q, c).start()
-    for t, p in enumerate(pieces[1:]):
-        p.s1(t + 1 < EARLY)
-    swap_cot.start()
-    own_cot.start()
+        send(small_s, vec.at[me], vs.at[0], vs.at[3], q, c).start()
+    loose["swap"] = swap_tok.start
+
+    def swap_cotangent():
+        swap_cot.start()
+        own_cot.start()
+
+    loose["swc"] = swap_cotangent
 
     row = seg[...].astype(F32)
     first_row = jnp.zeros((1, 1), F32)
@@ -196,55 +226,62 @@
     keep_col = jnp.where(keep_col, 1.0, 0.0)
     sc1[...] = jnp.concatenate([keep_col, seg_col], axis=1)
 
-    def mask_rows(i, _):
-        r = pl.ds(al(i * 128, 128), 128)
-        bias[r, :] = jnp.where(sc1[r, 1:2] == seg_row, 0.0, -1e30)
-        return 0
-
-    lax.fori_loop(0, T // 128, mask_rows, 0)
-    s2(0)
-    own_vec.wait()
-    small(0, 3, True)
-
-    def small2(k, _):
-        b = vec.at[k * 4 + xy]
-        send(b, b, gs.at[SM, 1], gr.at[SM, 1], near, c).start()
-        return 0
-
-    lax.fori_loop(0, 4, small2, 0)
-    s3(0)
-    own_tok.wait()
-    swap_tok.wait_recv()
-
-    def start_rows(i, _):
-        r = pl.ds(al(i * 128, 128), 128)
-        t = jnp.where(sc1[r, 0:1] > 0.5, tok[r, :].astype(F32), tokr[r, :].astype(F32)) + te[...]
-        n1[r, :] = t
-        xl[r, :] = t.astype(BF)
-        return 0
-
-    lax.fori_loop(0, T // 128, start_rows, 0)
-    s2(1)
-    s4(0)
-    small(1, 4, True)
-
-    def small3(k, _):
-        b = vec.at[(k // 2) * 4 + (1 - c) * 2 * y + c * x + lax.rem(k, 2) * (1 + c)]
-        send(b, b, gs.at[SM, 2], gr.at[SM, 2], far, c).start()
-        return 0
-
-    lax.fori_loop(0, 8, small3, 0)
-    s3(1)
-    small(2, 8, True)
-    for o in range(16):
-        fullv[:, o * 48 : (o + 1) * 48] = vec[o][:, :48].astype(F32)
-        for k in range(4):
-            fulle[:, o * 192 + k * 48 : o * 192 + (k + 1) * 48] = vec[o][k : k + 1, 64:112].astype(F32)
-    fullp[...] = jnp.concatenate([jnp.zeros_like(fullp[0:1, :]), jnp.ones_like(fullp[0:1, :])], axis=0)
-    for h in range(D // 128):
-        fullp[0:1, h * 384 : h * 384 + 128] = fullv[0:1, h * 128 : (h + 1) * 128]
-        fullp[0:1, h * 384 + 256 : h * 384 + 384] = fullv[1:2, h * 128 : (h + 1) * 128]
-        fullp[1:2, h * 384 : h * 384 + 128] = jnp.full((1, 128), HD**-0.5, F32)
+    def fill_mask():
+        def mask_rows(i, _):
+            r = pl.ds(al(i * 128, 128), 128)
+            bias[r, :] = jnp.where(sc1[r, 1:2] == seg_row, 0.0, -1e30)
+            return 0
+
+        lax.fori_loop(0, T // 128, mask_rows, 0)
+
+    def fill_start():
+        own_tok.wait()
+        swap_tok.wait_recv()
+
+        def start_rows(i, _):
+            r = pl.ds(al(i * 128, 128), 128)
+            t = jnp.where(sc1[r, 0:1] > 0.5, tok[r, :].astype(F32), tokr[r, :].astype(F32)) + te[...]
+            n1[r, :] = t
+            xl[r, :] = t.astype(BF)
+            return 0
+
+        lax.fori_loop(0, T // 128, start_rows, 0)
+
+    def small_near():
+        own_vec.wait()
+        small(0, 3, True)
+
+        def one(k, _):
+            b = vec.at[k * 4 + xy]
+            send(b, b, vs.at[1], vs.at[4], near, c).start()
+            return 0
+
+        lax.fori_loop(0, 4, one, 0)
+
+    def small_far():
+        small(1, 4, True)
+
+        def one(k, _):
+            b = vec.at[(k // 2) * 4 + (1 - c) * 2 * y + c * x + lax.rem(k, 2) * (1 + c)]
+            send(b, b, vs.at[2], vs.at[5], far, c).start()
+            return 0
+
+        lax.fori_loop(0, 8, one, 0)
+
+    def fill_vectors():
+        small(2, 8, True)
+        for o in range(16):
+            fullv[:, o * 48 : (o + 1) * 48] = vec[o][:, :48].astype(F32)
+            for k in range(4):
+                fulle[:, o * 192 + k * 48 : o * 192 + (k + 1) * 48] = vec[o][k : k + 1, 64:112].astype(F32)
+        fullp[...] = jnp.concatenate([jnp.zeros_like(fullp[0:1, :]), jnp.ones_like(fullp[0:1, :])], axis=0)
+        for h in range(D // 128):
+            fullp[0:1, h * 384 : h * 384 + 128] = fullv[0:1, h * 128 : (h + 1) * 128]
+            fullp[0:1, h * 384 + 256 : h * 384 + 384] = fullv[1:2, h * 128 : (h + 1) * 128]
+            fullp[1:2, h * 384 : h * 384 + 128] = jnp.full((1, 128), HD**-0.5, F32)
+
+    loose.update({"mask": fill_mask, "start": fill_start, "vec": fill_vectors, "vn": small_near, "vf": small_far})
+    run(['s1:0', 's2o:0', 's1:1', 'swap', 's1:2', 's2o:2', 's1:3', 's1:4', 's2o:4', 's2o:3', 's3:0.0', 's2o:1', 's2:0.1', 's2:0.2', 's1:6', 's2:0.3', 'vn', 's1:5', 's3:0.1', 's1:8', 's2o:8', 's2o:5', 's4:0.0', 's3:0.2', 's3:0.3', 'vf', 's4:0.1', 's2:1', 's4:0.2', 's2:2', 's1:7', 's4:0.3', 'start', 'mask', 's3:1', 'vec'])
 
     def project(g):
         cs = pl.ds(al(g * 768, 768), 768)
@@ -258,13 +295,14 @@
         return pltpu.make_async_copy(pslot.at[a], spill.at[h * 2 + a], ps.at[a])
 
     tasks = [
-        lambda: (s2(2), s4(1)),
-        lambda: (s2(3), s3(2)),
-        lambda: (s4(2), s2(4), s3(3)),
-        lambda: (s2(5),),
-        lambda: (s4(3), s3(4)),
-        lambda: (s2(6), s4(4), s3(5)),
+        ['s3:2', 's2:4', 's1:10', 's4:1'],
+        [],
+        ['s2:5', 's4:2'],
+        ['s1:9', 'swc'],
+        ['s2:7'],
+        ['s4:4'],
     ]
+    between = [['s2o:6', 's2:3'], ['s3:3', 's2:6', 's3:4'], ['s3:6', 's3:5', 's2o:7', 's2:8', 's4:3']]
 
     def attend(h, _):
         for g in range(3):
@@ -276,6 +314,13 @@
         @pl.when(lax.rem(h, 2) == 0)
         def _():
             project(h // 2)
+
+        for g in range(3):
+            if between[g]:
+
+                @pl.when(h == 2 * g)
+                def _():
+                    run(between[g])
 
         cs = al(h * 384, 128)
         q2 = proj[:, pl.ds(cs, 128)]
@@ -299,7 +344,7 @@
 
             @pl.when(h == k)
             def _():
-                tasks[k]()
+                run(tasks[k])
 
         return 0
 
@@ -328,15 +373,14 @@
         return 0
 
     lax.fori_loop(0, T // 256, first_rows, 0)
-    s2(7)
-    s4(5)
-    s3(6)
+    run(['s4:6', 's2o:10', 's3:7', 's3:8', 's4:5', 's2o:9'])
     after = [
-        lambda: (s2(8), s4(6), s3(7)),
-        lambda: (s2(9), s4(7), s3(8)),
-        lambda: (s2(10), s4(8), s3(9)),
-        lambda: (s4(9), s3(10)),
+        [],
+        [],
+        ['s4:7', 's2:9', 's2:10', 's4:8'],
+        ['s3:9'],
     ]
+    then = [['s3:10', 's4:9', 's4:10'], [], []]
 
     def expand(i, _):
         for k in range(4):
@@ -354,7 +398,7 @@
 
             @pl.when(i == k)
             def _():
-                after[k]()
+                run(after[k])
 
         return 0
 
@@ -365,12 +409,17 @@
 
             @pl.when(i == k)
             def _():
-                if k == 1:
-                    s4(10)
                 pieces[8 + k].done()
 
         cs = pl.ds(al(i * 256, 256), 256)
         sg[:, cs] = nn(hidden[...], wcon[:, cs]) + fullv[5:6, cs]
+        for k in range(3):
+            if then[k]:
+
+                @pl.when(i == k)
+                def _():
+                    run(then[k])
+
         return 0
 
     lax.fori_loop(0, D // 256, contract, 0)
@@ -412,17 +461,16 @@
         return t
 
     class Red:
-        def __init__(self, n, g, col, rows, recv, rcol, fsum, plane=None):
+        def __init__(self, n, g, col, rows, recv, rcol, fsum, plane=None, width=384, parts=()):
             self.n, self.g, self.col, self.rows, self.recv, self.rcol, self.fsum = n, g, col, rows, recv, rcol, fsum
-            self.plane = plane
-            self.fcol = (n - 4) * 768 if 4 <= n < 8 else 0
+            self.plane, self.width, self.parts = plane, width, parts
 
         def cols(self, core):
-            return pl.ds(al(self.col + core * S, 128), S)
+            return pl.ds(al(self.col + core * S, 128), self.width)
 
         def part(self, base, i, k=1, second=False):
             if self.plane is None:
-                cs = pl.ds(self.rcol + (S if second else 0), S)
+                cs = pl.ds(self.rcol + (self.width if second else 0), self.width)
             else:
                 cs = pl.ds(0, S)
                 base = base + self.rcol
@@ -450,15 +498,12 @@
             return self.recv.at[pl.ds(al(5376 + i * self.rows, 16), k * self.rows), pl.ds(0, S)]
 
         def sem(self, stage):
-            return rs.at[self.n, stage], rr.at[self.n, stage]
+            n = 0 if self.plane is not None and stage == 3 else self.n
+            return rs.at[self.n], rr.at[n * 5 + stage]
 
         def got(self, stage, ref):
             s, r = self.sem(stage)
             send(ref, ref, s, r, me, other).wait_recv()
-
-        def gone(self, stage, ref):
-            s, r = self.sem(stage)
-            send(ref, ref, s, r, me, other).wait_send()
 
         def P(self):
             base = 0 if self.plane is None else self.plane * 4 * self.rows
@@ -493,77 +538,153 @@
 
             lax.fori_loop(0, self.planes(), one, 0)
 
-        def Z(self, j=None):
+        def Z(self):
             self.got(2, self.rb(0, self.planes()))
+            s, r = self.sem(3)
             if self.plane is None:
                 for k in range(3):
-                    s, r = self.sem(3)
                     p = lax.rem(z + k + 1, 4)
                     b = self.mine(p * 4 + xy)
                     b[...] = total(b, self.rp(p * 4 + xy), self.ra(p * 2 + my_k), self.rb(p)).astype(BF)
                     send(b, self.rz(k), s, r, zs[k], c).start()
-            elif j > 0:
-                s, r = rs.at[self.n, 3], rr.at[0, 3]
+            elif self.n > 0:
                 b = self.mine(xy)
                 b[...] = total(b, self.rp(xy), self.ra(my_k), self.rb(0)).astype(BF)
-                send(b, self.rz(j - 1), s, r, zs[j - 1], c).start()
+                send(b, self.rz(self.n - 1), s, r, zs[self.n - 1], c).start()
 
         def F(self):
-            if self.plane is None:
-                self.got(3, self.rz(0, 3))
-                t = total(self.mine(z * 4 + xy), self.rp(z * 4 + xy), self.ra(z * 2 + my_k), self.rb(z),
-                          self.rz(0), self.rz(1), self.rz(2))
-            else:
-                ref = self.rz(0, 3)
-                send(ref, ref, rs.at[0, 3], rr.at[0, 3], me, other).wait_recv()
-                t = total(self.mine(xy), self.rp(xy), self.ra(my_k), self.rb(0), self.rz(0), self.rz(1), self.rz(2))
+            self.got(3, self.rz(0, 3))
+            o, p = (z * 4 + xy, z) if self.plane is None else (xy, 0)
+            t = total(self.mine(o), self.rp(o), self.ra(p * 2 + my_k), self.rb(p), self.rz(0), self.rz(1), self.rz(2))
             s, r = self.sem(4)
-            if self.n >= 9:
-                for k in range(3):
-                    b = self.fsum.at[:, pl.ds(al(k * D + (self.n - 9) * 256 + c * 128, 128), 128)]
-                    b[...] = t[:, k * 128 : (k + 1) * 128]
+            if self.parts:
+                for i, k in enumerate(self.parts):
+                    b = self.fsum.at[:, pl.ds(al(k + c * 128, 128), 128)]
+                    b[...] = t[:, i * 128 : (i + 1) * 128]
                     send(b, b, s, r, me, other).start()
             else:
-                b = self.fsum.at[:, pl.ds(al(self.fcol + c * S, 128), S)]
+                b = self.fsum.at[:, pl.ds(al((self.n - 4 if 4 <= self.n < 8 else 0) * 768 + c * S, 128), S)]
                 b[...] = t
                 send(b, b, s, r, me, other).start()
 
         def end(self):
-            p = self.planes()
-            self.gone(0, self.rp(0, 4 * p))
-            self.gone(1, self.ra(0, 2 * p))
-            self.gone(2, self.rb(0, p))
             if self.plane is None:
-                self.gone(3, self.rz(0, 3))
-            elif self.n > 0:
-                self.gone(3, self.rz(0, 1))
+                m = wide.at[pl.ds(0, 528), pl.ds(0, 3 * self.width)]
+            else:
+                m = wide.at[pl.ds(0, 576 if self.n == 0 else 512), pl.ds(0, 1152)]
+            send(m, m, rs.at[self.n], rr.at[self.n], me, other).wait_send()
             if self.plane is None or self.n == 0:
-                half = self.fsum.at[:, pl.ds(0, S)]
-                self.gone(4, half)
-                self.got(4, half)
+                self.got(4, self.fsum.at[:, pl.ds(0, self.width)])
 
     con = {j: Red(j, gcon, 0, 192, con_r, j * 1344, fcon, plane=lax.rem(z + j, 4)) for j in range(4)}
     exp = [Red(4 + k, wide, EXP + k * 768, 48, hidden, k * 768, fexp) for k in range(4)]
     out = Red(8, wide, OUT, 48, cotn, 0, fout)
-    ins = [Red(9 + k, gin, k * 768, 48, slope, k * 768, fin) for k in range(3)]
-
-    def run_at(i, lists):
-        for k, t in lists.items():
-
-            @pl.when(i == k)
-            def _():
-                for u in t:
-                    u()
+    ins = [
+        Red(9 + k, gin, k * 768, 48, slope, k * 768, fin, parts=[q * D + k * 256 for q in range(3)]) for k in range(2)
+    ]
+    ins.append(Red(11, gin, 1536, 48, slope, 1536, fin, width=256, parts=[512, D + 512]))
+    ins.append(Red(12, gin, 1792, 48, slope, 2048, fin, width=128, parts=[2 * D + 512]))
+    sums = {f"C{k}": con[k] for k in range(4)}
+    sums.update({f"E{k}": exp[k] for k in range(4)})
+    sums.update({f"I{k}": ins[k] for k in range(4)})
+    sums["O"] = out
+
+    def reduce(ops):
+        for op in ops:
+            name, _, rest = op.partition(":")
+            if op in loose:
+                loose[op]()
+            else:
+                getattr(sums[rest], name)()
+
+    def steps(i, lists):
+        for k, ops in enumerate(lists):
+            if ops:
+
+                @pl.when(i == k)
+                def _():
+                    reduce(ops)
+
+    def send_back():
+        def out_rows(i, _):
+            r = pl.ds(al(i * 128, 128), 128)
+            lonew[r, :] = jnp.where(sc1[r, 0:1] > 0.5, lonew[r, :].astype(F32), lor[r, :].astype(F32)).astype(BF)
+            return 0
+
+        swap_lo.wait()
+        lax.fori_loop(0, T // 128, out_rows, 0)
+        lo_done.start()
+
+    lo_done = pltpu.make_async_copy(lonew, lo_o, ls.at[14])
+    loose["lo"] = send_back
+
+    def vsend(stage, src, dst, dp, seq):
+        return send(src, dst, rs.at[13 + stage], rr.at[65 + stage], dp, seq)
+
+    def v_partner():
+        vout[...] = jnp.zeros_like(vout)
+        for o in range(16):
+            vout[o, :, 0:48] = gv[0:8, o * 48 : (o + 1) * 48]
+            for k in range(4):
+                vout[o, k : k + 1, 64:112] = ge[:, o * 192 + k * 48 : o * 192 + (k + 1) * 48]
+        vsend(0, vout, vr.at[pl.ds(0, 16)], me, other).start()
+
+    def v_flip_y():
+        vsend(0, vout, vr.at[pl.ds(0, 16)], me, other).wait_recv()
+        vsum[...] = vout[...] + vr[pl.ds(0, 16)]
+        for i in range(8):
+            vsend(1, vsum.at[(i // 2) * 4 + 2 - 2 * y + i % 2], vr.at[16 + i], flip_y, c).start()
+
+    def v_flip_x():
+        vsend(1, vr.at[pl.ds(16, 8)], vr.at[pl.ds(16, 8)], me, other).wait_recv()
+        for i in range(8):
+            o = (i // 2) * 4 + 2 * y + i % 2
+            vsum[o] = vsum[o] + vr[16 + i]
+        for i in range(4):
+            vsend(2, vsum.at[i * 4 + 2 * y + 1 - x], vr.at[24 + i], flip_x, c).start()
+
+    def v_planes():
+        vsend(2, vr.at[pl.ds(24, 4)], vr.at[pl.ds(24, 4)], me, other).wait_recv()
+        for i in range(4):
+            vsum[i * 4 + xy] = vsum[i * 4 + xy] + vr[24 + i]
+        for k in range(3):
+            vsend(3, vsum.at[lax.rem(z + k + 1, 4) * 4 + xy], vr.at[28 + k], zs[k], c).start()
+
+    def v_total():
+        vsend(3, vr.at[pl.ds(28, 3)], vr.at[pl.ds(28, 3)], me, other).wait_recv()
+        vr[31] = vsum[z * 4 + xy] + vr[28] + vr[29] + vr[30]
+        v_done.start()
+
+    v_done = pltpu.make_async_copy(vr.at[31], gvec_o, ls.at[16])
+    loose.update({"vP": v_partner, "vA": v_flip_y, "vB": v_flip_x, "vZ": v_planes, "vF": v_total})
+
+    ig_mine, ig_theirs = bg, fl
+    swap_ig = [
+        send(ig_mine.at[pl.ds(256 * k, 256)], ig_theirs.at[pl.ds(256 * k, 256)], sw3.at[0, k], sw3.at[1, k], me, other)
+        for k in range(3)
+    ]
+    for k in range(3):
+        loose[f"swg{k}"] = swap_ig[k].start
+    ig_done = pltpu.make_async_copy(sg, ig_o, ls.at[15])
+
+    def take_rows():
+        for d in swap_ig:
+            d.wait_recv()
+
+        def grad_rows(i, _):
+            r = pl.ds(al(i * 128, 128), 128)
+            sg[r, :] = jnp.where(sc1[r, 0:1] > 0.5, sg[r, :], ig_theirs[r, :].astype(F32))
+            return 0
+
+        lax.fori_loop(0, T // 128, grad_rows, 0)
+        ig_done.start()
+
+    loose["sel"] = take_rows
 
     def grad_con(i, _):
         p = al(lax.rem(z + i + 1, 4) * 768, 768)
         gcon[pl.ds(p, 768), :] = tn(hidden[:, pl.ds(p, 768)], bg[...]).astype(BF)
-        run_at(i, {
-            0: [con[1].P],
-            1: [con[2].P, con[1].A],
-            2: [con[3].P, con[2].A],
-            3: [con[0].P, con[3].A],
-        })
+        steps(i, [['P:C1'], ['P:C2'], ['P:C3', 'A:C1'], ['P:C0']])
         return 0
 
     lax.fori_loop(0, 4, grad_con, 0)
@@ -573,7 +694,7 @@
         g = (nt(bg[...], wcon[cs, :]) * slope[:, cs].astype(F32)).astype(BF)
         slope[:, cs] = g
         ge[:, cs] = jnp.sum(g.astype(F32), axis=0, keepdims=True)
-        run_at(i, {0: [con[0].A], 1: [con[1].B], 3: [con[2].B]})
+        steps(i, [['A:C3', 'A:C2'], [], [], []])
         return 0
 
     lax.fori_loop(0, FF // 768, expand_back, 0)
@@ -590,7 +711,7 @@
         low = g.astype(BF)
         bg[r, :] = low
         gv[2:3, :] += jnp.sum(low.astype(F32), axis=0, keepdims=True)
-        run_at(i, {0: [con[3].B], 1: [lambda: con[1].Z(1)], 2: [con[0].B, lambda: con[2].Z(2)]})
+        steps(i, [['B:C1'], ['A:C0'], []])
         return 0
 
     lax.fori_loop(0, T // 256, first_back, 0)
@@ -600,30 +721,19 @@
     def grad_exp(i, _):
         cs = pl.ds(al(i * 768, 768), 768)
         wide[:, pl.ds(al(EXP + i * 768, 768), 768)] = tn(fl[...], slope[:, cs]).astype(BF)
-        run_at(i, {
-            0: [exp[0].P, lambda: con[3].Z(3)],
-            1: [exp[1].P, exp[0].A, lambda: con[0].Z(0)],
-            2: [exp[2].P, exp[1].A],
-            3: [exp[3].P, exp[2].A, con[0].F],
-        })
+        steps(i, [['P:E0', 'B:C3'], ['P:E1', 'B:C2'], ['Z:C1', 'B:C0'], ['P:E3', 'Z:C3', 'A:E0']])
         return 0
 
     lax.fori_loop(0, 4, grad_exp, 0)
     hg = cotr
     hg[...] = nt(bg[...], wide[:, OUT:EXP]).astype(BF)
-    exp[3].A()
+    reduce([])
     pieces[3].drain()
     wide[:, OUT:EXP] = tn(heads[...], bg[...]).astype(BF)
-    out.P()
-
-    tasks = [
-        [exp[0].B],
-        [exp[1].B, exp[0].Z],
-        [out.A],
-        [exp[2].B, ins[0].A, exp[1].Z],
-        [exp[3].B, exp[2].Z, exp[0].F, ins[1].A],
-        [exp[3].Z, out.B, exp[1].F],
-    ]
+    reduce(['P:O', 'A:E1', 'Z:C2', 'P:E2'])
+
+    tasks = [['A:E3'], ['A:O'], ['P:I0', 'B:E3', 'B:E0', 'Z:C0'], ['F:C0', 'B:E1'], ['Z:E0', 'A:I1'], ['Z:E1', 'vP', 'B:E2']]
+    after = [[], ['P:I1', 'Z:E3', 'A:E2', 'lo', 'B:O'], []]
 
     def attend_back(h, _):
         cs = al(h * 384, 128)
@@ -659,111 +769,46 @@
         gv[0:1, hs] = jnp.sum(dq.astype(F32), axis=0, keepdims=True)
         gv[1:2, hs] = jnp.sum(dv.astype(F32), axis=0, keepdims=True)
 
+        steps(h, tasks)
+
         @pl.when(lax.rem(h, 2) == 1)
         def _():
             cols = pl.ds(al((h // 2) * 768, 768), 768)
             gin[:, cols] = tn(xl[...], proj[:, cols]).astype(BF)
 
-        for k in range(pairs):
-
-            @pl.when(h == k)
-            def _():
-                if k % 2 == 1:
-                    ins[k // 2].P()
-                for t in tasks[k]:
-                    t()
-
+        steps((h - 1) // 2 + 8 * (1 - lax.rem(h, 2)), after)
         return 0
 
     lax.fori_loop(0, pairs, attend_back, 0)
-
-    vout[...] = jnp.zeros_like(vout)
-    for o in range(16):
-        vout[o, :, 0:48] = gv[0:8, o * 48 : (o + 1) * 48]
-        for k in range(4):
-            vout[o, k : k + 1, 64:112] = ge[:, o * 192 + k * 48 : o * 192 + (k + 1) * 48]
-    VN = 12
-
-    def vsend(stage, src, dst, dp, seq):
-        return send(src, dst, rs.at[VN, stage], rr.at[VN, stage], dp, seq)
-
-    vsend(0, vout, vr.at[pl.ds(0, 16)], me, other).start()
-    ins[2].A()
 
     def input_rows(i, _):
         r = pl.ds(al(i * 256, 256), 256)
-        sg[r, :] = sg[r, :] + nt(proj[r, :], wide[:, IN:OUT])
-        run_at(i, {0: [exp[2].F, ins[0].B], 1: [exp[3].F, out.Z], 2: [ins[1].B]})
+        g = sg[r, :] + nt(proj[r, :], wide[:, IN:OUT])
+        sg[r, :] = g
+        ig_mine[r, :] = g.astype(BF)
+        steps(i, [['Z:O', 'A:I0', 'P:I2'], [], ['Z:E2', 'B:I1', 'P:I3', 'swg0', 'A:I3', 'swg1', 'F:E0', 'F:E3', 'F:O', 'B:I0', 'Z:I1', 'A:I2', 'vA', 'swg2', 'F:E2', 'Z:I0', 'B:I3', 'B:I2', 'Z:I3', 'vB', 'sel', 'Z:I2', 'F:I0', 'vZ', 'F:I3', 'F:E1', 'F:I1', 'F:I2', 'vF']])
         return 0
 
     lax.fori_loop(0, T // 256, input_rows, 0)
-    swap_ig = send(sg, n1, swap_sem.at[3, 0], swap_sem.at[3, 1], me, other)
-    swap_ig.start()
-    vsend(0, vout, vr.at[pl.ds(0, 16)], me, other).wait_recv()
-    vsum[...] = vout[...] + vr[pl.ds(0, 16)]
-    for i in range(8):
-        b = vsum.at[(i // 2) * 4 + 2 - 2 * y + i % 2]
-        vsend(1, b, vr.at[16 + i], flip_y, c).start()
-    ins[0].Z()
-    ins[2].B()
-    vsend(1, vr.at[pl.ds(16, 8)], vr.at[pl.ds(16, 8)], me, other).wait_recv()
-    for i in range(8):
-        o = (i // 2) * 4 + 2 * y + i % 2
-        vsum[o] = vsum[o] + vr[16 + i]
-    for i in range(4):
-        b = vsum.at[i * 4 + 2 * y + 1 - x]
-        vsend(2, b, vr.at[24 + i], flip_x, c).start()
-    ins[1].Z()
-    out.F()
-    vsend(2, vr.at[pl.ds(24, 4)], vr.at[pl.ds(24, 4)], me, other).wait_recv()
-    for i in range(4):
-        vsum[i * 4 + xy] = vsum[i * 4 + xy] + vr[24 + i]
-    for k in range(3):
-        b = vsum.at[lax.rem(z + k + 1, 4) * 4 + xy]
-        vsend(3, b, vr.at[28 + k], zs[k], c).start()
-    ins[0].F()
-    ins[2].Z()
-    ins[1].F()
-    ins[2].F()
-
-    swap_lo.wait()
-
-    def out_rows(i, _):
-        r = pl.ds(al(i * 128, 128), 128)
-        lonew[r, :] = jnp.where(sc1[r, 0:1] > 0.5, lonew[r, :].astype(F32), lor[r, :].astype(F32)).astype(BF)
-        return 0
-
-    lax.fori_loop(0, T // 128, out_rows, 0)
-    lo_done = pltpu.make_async_copy(lonew, lo_o, ls.at[14])
-    lo_done.start()
-    swap_ig.wait()
-
-    def grad_rows(i, _):
-        r = pl.ds(al(i * 128, 128), 128)
-        sg[r, :] = jnp.where(sc1[r, 0:1] > 0.5, sg[r, :], n1[r, :])
-        return 0
-
-    lax.fori_loop(0, T // 128, grad_rows, 0)
-    outs = [lo_done, pltpu.make_async_copy(sg, ig_o, ls.at[15])]
-    outs[1].start()
-    vsend(3, vr.at[pl.ds(28, 3)], vr.at[pl.ds(28, 3)], me, other).wait_recv()
-    vfin = vr.at[31]
-    vfin[...] = vsum[z * 4 + xy] + vr[28] + vr[29] + vr[30]
-    outs.append(pltpu.make_async_copy(vfin, gvec_o, ls.at[16]))
-    outs[2].start()
+    outs = [lo_done, ig_done, v_done]
+    for k, (v, o) in enumerate([(fcon, gcon_o), (fexp, gexp_o), (fout, gout_o), (fin, gin_o)]):
+        for p in [[con[0]], exp, [out], ins][k]:
+            p.end()
+        outs.append(pltpu.make_async_copy(v, o, ls.at[17 + k]))
+        outs[-1].start()
+    for k in (1, 2, 3):
+        con[k].end()
     swap_tok.wait_send()
     swap_cot.wait_send()
+    for d in swap_ig:
+        d.wait_send()
     for p in pieces[0:3] + pieces[8:]:
         p.drain()
     for stage, k in ((0, 3), (1, 4), (2, 8)):
         small(stage, k, False)
-        vsend(stage + 1, vr.at[pl.ds(0, (8, 4, 3)[stage])], vr.at[pl.ds(0, (8, 4, 3)[stage])], me, other).wait_send()
+        m = vr.at[pl.ds(0, (8, 4, 3)[stage])]
+        vsend(stage + 1, m, m, me, other).wait_send()
     vsend(0, vout, vr.at[pl.ds(0, 16)], me, other).wait_send()
-    for p in list(con.values()) + exp + [out] + ins:
-        p.end()
-    for k, (v, o) in enumerate([(fin, gin_o), (fout, gout_o), (fexp, gexp_o), (fcon, gcon_o)]):
-        outs.append(pltpu.make_async_copy(v, o, ls.at[17 + k]))
-        outs[-1].start()
     for o in outs:
         o.wait()
 
@@ -784,7 +829,7 @@
         VM((D, 3 * D), BF), VM((FF, D), BF), VM((5952, 384), BF), VM((8, D), F32), VM((1, FF), F32),
         VM((16, 8, 128), F32), VM((16, 8, 128), F32), VM((32, 8, 128), F32),
         VM(iw.shape, F32), VM(ow.shape, F32), VM(ew.shape, F32), VM(cw.shape, F32),
-        DMA((4, 2)), DMA((21,)), DMA((12, 4)), DMA((12, 13)), DMA((2,)), DMA((13, 5)), DMA((13, 5)), DMA((2,)),
+        DMA((3, 2)), DMA((2, 3)), DMA((21,)), DMA((11,)), DMA((56,)), DMA((6,)), DMA((2,)), DMA((17,)), DMA((69,)), DMA((2,)),
     ]
     return pl.pallas_call(
         fused_kernel,
@@ -1116,6 +1161,40 @@
     return (layer_output.reshape(seqs, half, width), input_grad) + tuple(summed)
 
 
+def finish_kernel(lo, ig, gi, go, ge, gc, vec, lo_o, ig_o, gi_o, go_o, ge_o, gc_o, *rest):
+    small, bufs, sems = rest[:9], rest[9:15], rest[15]
+    pairs = list(zip((ig, lo, ge, gi, gc, go), (bufs[1], bufs[0], bufs[4], bufs[2], bufs[5], bufs[3])))
+    results = (ig_o, lo_o, ge_o, gi_o, gc_o, go_o)
+    loads = [pltpu.make_async_copy(a, b, sems.at[0, k]) for k, (a, b) in enumerate(pairs)]
+    stores = [pltpu.make_async_copy(b, r, sems.at[1, k]) for k, ((_, b), r) in enumerate(zip(pairs, results))]
+    for d in loads:
+        d.start()
+    own = small[0].shape[1]
+    for k in range(8):
+        small[k][...] = vec[k : k + 1, :own]
+    for k in range(4):
+        small[8][:, k * own : (k + 1) * own] = vec[k : k + 1, 64 : 64 + own]
+    for a, b in zip(loads, stores):
+        a.wait()
+        b.start()
+    for b in stores:
+        b.wait()
+
+
+def finish(lo, ig, gi, go, ge, gc, vec, own):
+    sh = jax.ShapeDtypeStruct
+    anyspec = pl.BlockSpec(memory_space=pl.ANY)
+    vspec = pl.BlockSpec(memory_space=VM)
+    big = (lo, ig, gi, go, ge, gc)
+    return pl.pallas_call(
+        finish_kernel,
+        out_shape=[sh(v.shape, v.dtype) for v in big] + [sh((1, own), F32)] * 8 + [sh((1, 4 * own), F32)],
+        in_specs=[anyspec] * 6 + [vspec],
+        out_specs=[anyspec] * 6 + [vspec] * 9,
+        scratch_shapes=[VM(v.shape, v.dtype) for v in big] + [DMA((2, 6))],
+    )(*big, vec)
+
+
 def fused_body(
     tokens, time_embed, segments, input_weight, query_bias, value_bias, output_weight, output_bias, first_gain,
     first_shift, expand_weight, expand_bias, contract_weight, contract_bias, second_gain, second_shift, cotangent,
@@ -1127,15 +1206,15 @@
     small = jnp.pad(jnp.stack(vectors), ((0, 8), (0, 64 - own)))
     wide = jnp.pad(expand_bias.reshape(4, own), ((0, 12), (0, 64 - own)))
     small = jnp.concatenate([small, wide], axis=1)
-    layer_output, input_grad, g_in, g_out, g_exp, g_con, vec = fused_layer(
+    parts = fused_layer(
         tokens[0], time_embed, segments, input_weight, output_weight, expand_weight, contract_weight, small,
         cotangent[0],
     )[:7]
-    row = [vec[k, :own] for k in range(8)]
-    g_eb = vec[0:4, 64 : 64 + own].reshape(4 * own)
+    layer_output, input_grad, g_in, g_out, g_exp, g_con, *row = finish(*parts, own)
+    row = [v.reshape(v.shape[1]) for v in row]
     return (
         layer_output[None], input_grad[None], g_in, row[0], row[1], g_out, row[2], row[3], row[4],
-        g_exp, g_eb, g_con, row[5], row[6], row[7],
+        g_exp, row[8], g_con, row[5], row[6], row[7],
     )
 
 

time: 189 us -> 165 us (0.87)
  Pallas kernels: 176 us -> 162 us
  local copies, waits for them, and re-layouts: 11.4 us -> 1.54 us
    pallas_call x1, Pallas kernels: 176 us -> 156 us  [fused_layer(): pl.pallas_call(fused_kernel, out_shape=(sh((T, D), BF), sh((T, D), F32),...]
    unnamed x16 -> x0, local copies, waits for them, and re-layouts: 6.99 us -> none
    pallas_call x0 -> x1, Pallas kernels: none -> 5.39 us  [finish(): pl.pallas_call(finish_kernel, out_shape=[sh(v.shape, v.dtype) for v in bi...]
where the time goes in v3:
time: 165 us
  Pallas kernels  162 us (98%)
    pallas_call x1, Pallas kernels, fused_layer(): pl.pallas_call(fused_kernel, out_shape=(sh((T, D), BF), sh((T, D), F32),...  156 us
    pallas_call x1, Pallas kernels, finish(): pl.pallas_call(finish_kernel, out_shape=[sh(v.shape, v.dtype) for v in bi...  5.39 us

profile of v3, /device:TPU:0, one launch (start us, length us, event | category | flops | bytes accessed | tf_op | source)
XLA Modules:
  0.0 164.7 jit_solution(15188827534443374992)
XLA Ops:
  0.6 0.7 reshape.60
  1.4 0.8 stack.35
  2.2 0.7 fusion.2.small_s
  2.8 156.3 %shard_map.280 = (bf16[768,768]{1,0:T(8,128)(2,1)}, f32[768,768]{1,0:T(8,128)}, f32[48,2304]{1,0:T(8,128)}, f32[48,768]{1,0:T(8,128)}, f32[48,3072]{1,0:T(8,128)...) custom-call(bf16[768,768]{1,0:T(8,128)(2,1)} %bitcast.21, bf16[768,768]{1,0:T(8,128)(2,1)} %bitcast.22, ...), custom_call_target="tpu_custom_call" | custom-call | tf_op jit(solution)/shard_map/pallas_call | solution.py:834
  159.2 5.4 %shard_map.281 = (bf16[768,768]{1,0:T(8,128)(2,1)}, f32[768,768]{1,0:T(8,128)}, f32[48,2304]{1,0:T(8,128)}, f32[48,768]{1,0:T(8,128)}, f32[48,3072]{1,0:T(8,128)...) custom-call(bf16[768,768]{1,0:T(8,128)(2,1)} %get-tuple-element.37.l, ...), custom_call_target="tpu_custom_call" | custom-call | tf_op jit(solution)/shard_map/pallas_call | solution.py:1189

commit v4 on v3

--- a/solution.py
+++ b/solution.py
@@ -30,13 +30,14 @@
 
 
 def fused_kernel(
-    tokens, cot, te, seg, win_s, wout_s, wexp_s, wcon_s, small_s,
+    tokens, cot, te, seg, win_s, wout_s, wexp_s, wcon_s, v0, v1, v2, v3, v4, v5, v6, v7, v8,
     lo_o, ig_o, gin_o, gout_o, gexp_o, gcon_o, gvec_o, spill,
-    wide, wcon, tok, tokr, cotn, cotr, vec, fullv, fulle, fullp, proj, xl, n1, sg,
+    wide, wcon, tok, tokr, cotn, cotr, vec, pack, fullv, fulle, fullp, proj, xl, n1, sg,
     sc1, heads, fl, hidden, slope, pslot, bg,
     gin, gcon, con_r, gv, ge, vout, vsum, vr, fin, fout, fexp, fcon,
     swap_sem, sw3, ls, gs, gr, vs, ps, rs, rr, pd,
 ):
+    vectors = (v0, v1, v2, v3, v4, v5, v6, v7, v8)
     T, D = tok.shape
     FF = wcon.shape[0]
     IN, OUT, EXP = 0, 3 * D, 4 * D
@@ -65,14 +66,15 @@
         pl.semaphore_signal(
             barrier, inc=1, device_id={"dp": dp, "seq": seq}, device_id_type=MESH
         )
-    pl.semaphore_wait(barrier, 6)
 
     def al(v, m):
         return pl.multiple_of(v, m)
 
     class Piece:
-        def __init__(self, n, buf, rows, col, half, shards):
+        def __init__(self, n, buf, rows, col, half, shards, whole=None):
             self.n, self.buf, self.rows, self.col, self.half, self.shards = n, buf, rows, col, half, shards
+            self.whole = whole
+            self.low = 1 if whole is None else 2
 
         def cols(self, core):
             return pl.ds(al(self.col + core * self.half, 128), self.half)
@@ -84,6 +86,8 @@
             return self.buf.at[pl.ds(0, k * self.rows), self.cols(core)]
 
         def arrival(self, stage, k):
+            if stage > 3:
+                return gr.at[56 + self.whole * 3 + stage - 4]
             return gr.at[stage * 4 + k] if self.n == 0 and stage < 3 else gr.at[12 + self.n * 4 + stage]
 
         def push(self, src, dst, stage, k, dp):
@@ -102,7 +106,7 @@
                 )
 
         def s1(self):
-            for k in range(3):
+            for k in range(self.low - 1, 3):
                 for a, b in self.own():
                     self.push(a, b, 0, k + 1, zs[k])
             for a, b in self.own():
@@ -110,12 +114,24 @@
 
         def s2o(self):
             for a, b in self.own():
-                self.push(a, b, 1, 0, near)
-                self.push(a, b, 2, 0, far)
+                self.push(a, b, 1 if self.whole is None else 4, 0, near)
+                self.push(a, b, 2 if self.whole is None else 5, 0, far)
+
+        def s2n(self):
+            self.got(4, 0, 1)
+            b = self.block(z * 4 + near_xy)
+            self.push(b, b, 5, 0, far)
+
+        def s5(self):
+            self.got(5, 0, 2)
+            m = self.block(me)
+            pltpu.make_async_copy(m, m, ls.at[self.n]).wait()
+            p = self.buf.at[pl.ds(al(z * 4 * self.rows, 16), 4 * self.rows), self.cols(c)]
+            self.push(p, p, 6, 0, zs[0])
 
         def s2(self, k=None):
             if k is None:
-                self.got(0, 0, 3)
+                self.got(0, 0, 4 - self.low)
             else:
                 self.got(0, k, 1)
 
@@ -126,13 +142,13 @@
                 return 0
 
             if k is None:
-                lax.fori_loop(1, 4, one, 0)
+                lax.fori_loop(self.low, 4, one, 0)
             else:
                 one(k, 0)
 
         def s3(self, k=None):
             if k is None:
-                self.got(1, 0, 4)
+                self.got(1, 0, 4 if self.whole is None else 2)
             else:
                 self.got(1, k, 1)
 
@@ -142,16 +158,18 @@
                 return 0
 
             if k is None:
-                lax.fori_loop(0, 4, one, 0)
+                lax.fori_loop(0 if self.whole is None else 2, 4, one, 0)
             else:
                 one(k, 0)
 
         def s4(self, k=None):
             if k is None:
-                self.got(2, 0, 8)
+                self.got(2, 0, 8 if self.whole is None else 4)
             else:
                 self.got(2, k, 2)
-            if not k:
+            if self.whole is not None:
+                self.got(6, 0, 4)
+            elif not k:
                 m = self.block(me)
                 pltpu.make_async_copy(m, m, ls.at[self.n]).wait()
             if k is None:
@@ -169,12 +187,19 @@
             send(m, m, gs.at[self.n], self.arrival(3, 0), me, other).wait_send()
 
     near_xy = xy + (1 - c) * (1 - 2 * x) + c * (2 - 4 * y)
-    pieces = [
-        Piece(g, wide, 48, g * 768, 384, [(win_s, k * D + g * 256, 128) for k in range(3)]) for g in range(3)
-    ]
-    pieces += [Piece(3, wide, 48, OUT, 384, [(wout_s, 0, 384)])]
-    pieces += [Piece(4 + k, wide, 48, EXP + k * 768, 384, [(wexp_s, k * 768, 384)]) for k in range(4)]
-    pieces += [Piece(8 + k, wcon, 192, k * 256, 128, [(wcon_s, k * 256, 128)]) for k in range(3)]
+    whole = {8: 0, 9: 1, 10: 2}
+    pieces = []
+    for n in range(11):
+        if n < 3:
+            spec = (wide, 48, n * 768, 384, [(win_s, k * D + n * 256, 128) for k in range(3)])
+        elif n == 3:
+            spec = (wide, 48, OUT, 384, [(wout_s, 0, 384)])
+        elif n < 8:
+            spec = (wide, 48, EXP + (n - 4) * 768, 384, [(wexp_s, (n - 4) * 768, 384)])
+        else:
+            spec = (wcon, 192, (n - 8) * 256, 128, [(wcon_s, (n - 8) * 256, 128)])
+        pieces.append(Piece(n, *spec, whole=whole.get(n)))
+
     loose = {}
 
     def run(ops):
@@ -197,19 +222,14 @@
     swap_cot = send(cot, cotr, swap_sem.at[1, 0], swap_sem.at[1, 1], me, other)
     own_tok = pltpu.make_async_copy(tokens, tok, ls.at[11])
     own_cot = pltpu.make_async_copy(cot, cotn, ls.at[12])
-    own_vec = pltpu.make_async_copy(small_s, vec.at[me], ls.at[13])
 
     own_tok.start()
-    own_vec.start()
-    for q in zs:
-        send(small_s, vec.at[me], vs.at[0], vs.at[3], q, c).start()
-    loose["swap"] = swap_tok.start
-
-    def swap_cotangent():
-        swap_cot.start()
-        own_cot.start()
-
-    loose["swc"] = swap_cotangent
+    pack[...] = jnp.zeros_like(pack)
+    for k in range(8):
+        pack[k : k + 1, 0:48] = vectors[k][...].astype(F32)
+    for k in range(4):
+        pack[k : k + 1, 64:112] = vectors[8][:, k * 48 : (k + 1) * 48].astype(F32)
+    vec[me] = pack[...].astype(BF)
 
     row = seg[...].astype(F32)
     first_row = jnp.zeros((1, 1), F32)
@@ -226,13 +246,22 @@
     keep_col = jnp.where(keep_col, 1.0, 0.0)
     sc1[...] = jnp.concatenate([keep_col, seg_col], axis=1)
 
-    def fill_mask():
-        def mask_rows(i, _):
-            r = pl.ds(al(i * 128, 128), 128)
-            bias[r, :] = jnp.where(sc1[r, 1:2] == seg_row, 0.0, -1e30)
-            return 0
-
-        lax.fori_loop(0, T // 128, mask_rows, 0)
+    def mask_rows(i, _):
+        r = pl.ds(al(i * 128, 128), 128)
+        bias[r, :] = jnp.where(sc1[r, 1:2] == seg_row, 0.0, -1e30)
+        return 0
+
+    lax.fori_loop(0, T // 128, mask_rows, 0)
+    pl.semaphore_wait(barrier, 6)
+    for q in zs:
+        send(vec.at[me], vec.at[me], vs.at[0], vs.at[3], q, c).start()
+    loose["swap"] = swap_tok.start
+
+    def swap_cotangent():
+        swap_cot.start()
+        own_cot.start()
+
+    loose["swc"] = swap_cotangent
 
     def fill_start():
         own_tok.wait()
@@ -248,7 +277,6 @@
         lax.fori_loop(0, T // 128, start_rows, 0)
 
     def small_near():
-        own_vec.wait()
         small(0, 3, True)
 
         def one(k, _):
@@ -280,8 +308,8 @@
             fullp[0:1, h * 384 + 256 : h * 384 + 384] = fullv[1:2, h * 128 : (h + 1) * 128]
             fullp[1:2, h * 384 : h * 384 + 128] = jnp.full((1, 128), HD**-0.5, F32)
 
-    loose.update({"mask": fill_mask, "start": fill_start, "vec": fill_vectors, "vn": small_near, "vf": small_far})
-    run(['s1:0', 's2o:0', 's1:1', 'swap', 's1:2', 's2o:2', 's1:3', 's1:4', 's2o:4', 's2o:3', 's3:0.0', 's2o:1', 's2:0.1', 's2:0.2', 's1:6', 's2:0.3', 'vn', 's1:5', 's3:0.1', 's1:8', 's2o:8', 's2o:5', 's4:0.0', 's3:0.2', 's3:0.3', 'vf', 's4:0.1', 's2:1', 's4:0.2', 's2:2', 's1:7', 's4:0.3', 'start', 'mask', 's3:1', 'vec'])
+    loose.update({"start": fill_start, "vec": fill_vectors, "vn": small_near, "vf": small_far})
+    run(['s1:0', 's1:1', 's2o:9', 's1:2', 's2o:8', 'swap', 's2o:0', 's2o:10', 's2n:9', 's2o:2', 'start', 's1:3', 's2n:8', 's3:0.0', 's1:4', 's2o:1', 's2:0.1', 's2:0.2', 's2o:4', 's1:7', 's4:0.0', 's2o:7', 's2:0.3', 'vn', 'swc', 's3:0.1', 's2n:10', 's1:5', 's1:6', 's3:0.2', 's2:1', 's3:0.3', 'vf', 's4:0.1', 's2o:6', 's2o:3', 's2:2', 's4:0.2', 's3:1', 's4:0.3', 's2:3', 'vec'])
 
     def project(g):
         cs = pl.ds(al(g * 768, 768), 768)
@@ -295,14 +323,14 @@
         return pltpu.make_async_copy(pslot.at[a], spill.at[h * 2 + a], ps.at[a])
 
     tasks = [
-        ['s3:2', 's2:4', 's1:10', 's4:1'],
+        ['s4:1', 's3:3', 's2:7'],
+        ['s1:9', 's2:5', 's4:2'],
         [],
-        ['s2:5', 's4:2'],
-        ['s1:9', 'swc'],
-        ['s2:7'],
-        ['s4:4'],
+        ['s5:9', 's3:5', 's3:6', 's3:7', 's2:8'],
+        [],
+        ['s4:5', 's3:8', 's3:9', 's2:10'],
     ]
-    between = [['s2o:6', 's2:3'], ['s3:3', 's2:6', 's3:4'], ['s3:6', 's3:5', 's2o:7', 's2:8', 's4:3']]
+    between = [['s2o:5', 's3:2', 's1:8', 's2:4'], ['s1:10', 's3:4', 's2:6'], ['s4:3', 's5:8', 's4:4', 's2:9', 's5:10']]
 
     def attend(h, _):
         for g in range(3):
@@ -373,14 +401,14 @@
         return 0
 
     lax.fori_loop(0, T // 256, first_rows, 0)
-    run(['s4:6', 's2o:10', 's3:7', 's3:8', 's4:5', 's2o:9'])
+    run(['s4:7', 's4:6'])
     after = [
         [],
-        [],
-        ['s4:7', 's2:9', 's2:10', 's4:8'],
-        ['s3:9'],
+        ['s3:10', 's4:8'],
+        ['s4:9'],
+        ['s4:10'],
     ]
-    then = [['s3:10', 's4:9', 's4:10'], [], []]
+    then = [[], [], []]
 
     def expand(i, _):
         for k in range(4):
@@ -813,7 +841,7 @@
         o.wait()
 
 
-def fused_layer(tokens, time_embed, segments, iw, ow, ew, cw, small, cot):
+def fused_layer(tokens, time_embed, segments, iw, ow, ew, cw, vectors, cot):
     T, D = tokens.shape
     FF = ew.shape[1]
     sh = jax.ShapeDtypeStruct
@@ -822,14 +850,14 @@
     scratch = [
         VM((D, 4 * D + FF), BF), VM((FF, D), BF),
         VM((T, D), BF), VM((T, D), BF), VM((T, D), BF), VM((T, D), BF),
-        VM((16, 16, 128), BF), VM((16, D), F32), VM((1, FF), F32), VM((2, 3 * D), F32),
+        VM((16, 16, 128), BF), VM((16, 128), F32), VM((16, D), F32), VM((1, FF), F32), VM((2, 3 * D), F32),
         VM((T, 3 * D), BF), VM((T, D), BF), VM((T, D), F32), VM((T, T), F32),
         VM((T, 2), F32), VM((T, D), BF), VM((T, D), BF), VM((T, FF), BF), VM((T, FF), BF),
         VM((2, T, T), BF), VM((T, D), BF),
         VM((D, 3 * D), BF), VM((FF, D), BF), VM((5952, 384), BF), VM((8, D), F32), VM((1, FF), F32),
         VM((16, 8, 128), F32), VM((16, 8, 128), F32), VM((32, 8, 128), F32),
         VM(iw.shape, F32), VM(ow.shape, F32), VM(ew.shape, F32), VM(cw.shape, F32),
-        DMA((3, 2)), DMA((2, 3)), DMA((21,)), DMA((11,)), DMA((56,)), DMA((6,)), DMA((2,)), DMA((17,)), DMA((69,)), DMA((2,)),
+        DMA((3, 2)), DMA((2, 3)), DMA((21,)), DMA((11,)), DMA((65,)), DMA((6,)), DMA((2,)), DMA((17,)), DMA((69,)), DMA((2,)),
     ]
     return pl.pallas_call(
         fused_kernel,
@@ -837,13 +865,13 @@
             sh((T, D), BF), sh((T, D), F32), sh(iw.shape, F32), sh(ow.shape, F32), sh(ew.shape, F32),
             sh(cw.shape, F32), sh((8, 128), F32), sh((D // HD, T, T), BF),
         ),
-        in_specs=[anyspec, anyspec, vspec, vspec, anyspec, anyspec, anyspec, anyspec, anyspec],
+        in_specs=[anyspec, anyspec, vspec, vspec, anyspec, anyspec, anyspec, anyspec] + [vspec] * 9,
         out_specs=(anyspec,) * 8,
         scratch_shapes=scratch,
         compiler_params=pltpu.CompilerParams(
             collective_id=0, has_side_effects=True, vmem_limit_bytes=67043328
         ),
-    )(tokens, cot, time_embed, segments, iw, ow, ew, cw, small)
+    )(tokens, cot, time_embed, segments, iw, ow, ew, cw, *vectors)
 
 
 epsilon = 1e-05
@@ -1201,13 +1229,12 @@
 ):
     vectors = [
         query_bias, value_bias, output_bias, first_gain, first_shift, contract_bias, second_gain, second_shift,
+        expand_bias,
     ]
     own = query_bias.shape[0]
-    small = jnp.pad(jnp.stack(vectors), ((0, 8), (0, 64 - own)))
-    wide = jnp.pad(expand_bias.reshape(4, own), ((0, 12), (0, 64 - own)))
-    small = jnp.concatenate([small, wide], axis=1)
+    vectors = [v.reshape(1, v.shape[0]) for v in vectors]
     parts = fused_layer(
-        tokens[0], time_embed, segments, input_weight, output_weight, expand_weight, contract_weight, small,
+        tokens[0], time_embed, segments, input_weight, output_weight, expand_weight, contract_weight, vectors,
         cotangent[0],
     )[:7]
     layer_output, input_grad, g_in, g_out, g_exp, g_con, *row = finish(*parts, own)

time: 165 us -> 155 us (0.939)
  Pallas kernels: 162 us -> 152 us
    pallas_call x1, Pallas kernels: 156 us -> 147 us  [fused_layer(): pl.pallas_call(fused_kernel, out_shape=(sh((T, D), BF), sh((T, D), F32),...]
where the time goes in v4:
time: 155 us; the launch traced here: 154 us
  Pallas kernels  152 us (98%)
    pallas_call x1, Pallas kernels, fused_layer(): pl.pallas_call(fused_kernel, out_shape=(sh((T, D), BF), sh((T, D), F32),...  147 us
    pallas_call x1, Pallas kernels, finish(): pl.pallas_call(finish_kernel, out_shape=[sh(v.shape, v.dtype) for v in bi...  5.39 us

profile of v4, /device:TPU:0, one launch (start us, length us, event | category | flops | bytes accessed | tf_op | source)
XLA Modules:
  0.0 154.4 jit_solution(3320666727729633380)
XLA Ops:
  0.6 1.2 reshape.92.v8
  1.9 146.9 %shard_map.280 = (bf16[768,768]{1,0:T(8,128)(2,1)}, f32[768,768]{1,0:T(8,128)}, f32[48,2304]{1,0:T(8,128)}, f32[48,768]{1,0:T(8,128)}, f32[48,3072]{1,0:T(8,128)...) custom-call(bf16[768,768]{1,0:T(8,128)(2,1)} %bitcast.21, bf16[768,768]{1,0:T(8,128)(2,1)} %bitcast.22, ...), custom_call_target="tpu_custom_call" | custom-call | tf_op jit(solution)/shard_map/pallas_call | solution.py:862
  148.8 5.4 %shard_map.281 = (bf16[768,768]{1,0:T(8,128)(2,1)}, f32[768,768]{1,0:T(8,128)}, f32[48,2304]{1,0:T(8,128)}, f32[48,768]{1,0:T(8,128)}, f32[48,3072]{1,0:T(8,128)...) custom-call(bf16[768,768]{1,0:T(8,128)(2,1)} %get-tuple-element.37.l, ...), custom_call_target="tpu_custom_call" | custom-call | tf_op jit(solution)/shard_map/pallas_call | solution.py:1217

commit v5 on v4

--- a/solution.py
+++ b/solution.py
@@ -34,7 +34,7 @@
     lo_o, ig_o, gin_o, gout_o, gexp_o, gcon_o, gvec_o, spill,
     wide, wcon, tok, tokr, cotn, cotr, vec, pack, fullv, fulle, fullp, proj, xl, n1, sg,
     sc1, heads, fl, hidden, slope, pslot, bg,
-    gin, gcon, con_r, gv, ge, vout, vsum, vr, fin, fout, fexp, fcon,
+    gin, gcon, con_r, ry, gv, ge, vout, vsum, vr, fin, fout, fexp, fcon,
     swap_sem, sw3, ls, gs, gr, vs, ps, rs, rr, pd,
 ):
     vectors = (v0, v1, v2, v3, v4, v5, v6, v7, v8)
@@ -225,10 +225,11 @@
 
     own_tok.start()
     pack[...] = jnp.zeros_like(pack)
+    wide_bias = vectors[8][...].astype(F32).reshape(1, 192)
     for k in range(8):
         pack[k : k + 1, 0:48] = vectors[k][...].astype(F32)
     for k in range(4):
-        pack[k : k + 1, 64:112] = vectors[8][:, k * 48 : (k + 1) * 48].astype(F32)
+        pack[k : k + 1, 64:112] = wide_bias[:, k * 48 : (k + 1) * 48]
     vec[me] = pack[...].astype(BF)
 
     row = seg[...].astype(F32)
@@ -408,7 +409,6 @@
         ['s4:9'],
         ['s4:10'],
     ]
-    then = [[], [], []]
 
     def expand(i, _):
         for k in range(4):
@@ -432,25 +432,13 @@
 
     lax.fori_loop(0, FF // 768, expand, 0)
 
-    def contract(i, _):
-        for k in range(3):
-
-            @pl.when(i == k)
-            def _():
-                pieces[8 + k].done()
-
-        cs = pl.ds(al(i * 256, 256), 256)
-        sg[:, cs] = nn(hidden[...], wcon[:, cs]) + fullv[5:6, cs]
-        for k in range(3):
-            if then[k]:
-
-                @pl.when(i == k)
-                def _():
-                    run(then[k])
-
-        return 0
-
-    lax.fori_loop(0, D // 256, contract, 0)
+    pieces[8].done()
+    sg[:, :256] = nn(hidden[...], wcon[:, :256]) + fullv[5:6, :256]
+    run([])
+    pieces[9].done()
+    run([])
+    pieces[10].done()
+    run([])
     own_cot.wait()
     swap_cot.wait_recv()
 
@@ -458,7 +446,8 @@
 
     def second_rows(i, _):
         r = pl.ds(al(i * 256, 256), 256)
-        v = n1[r, :] * fullv[3:4, :] + fullv[4:5, :] + sg[r, :]
+        v = jnp.concatenate([sg[r, :256], nn(hidden[r, :], wcon[:, 256:]) + fullv[5:6, 256:]], axis=1)
+        v = v + (n1[r, :] * fullv[3:4, :] + fullv[4:5, :])
         n, s = normalize(v)
         lonew[r, :] = (n * fullv[6:7, :] + fullv[7:8, :]).astype(BF)
         og = jnp.where(sc1[r, 0:1] > 0.5, cotn[r, :].astype(F32), cotr[r, :].astype(F32))
@@ -489,9 +478,10 @@
         return t
 
     class Red:
-        def __init__(self, n, g, col, rows, recv, rcol, fsum, plane=None, width=384, parts=()):
+        def __init__(self, n, g, col, rows, recv, rcol, fsum, plane=None, width=384, parts=(), whole=None):
             self.n, self.g, self.col, self.rows, self.recv, self.rcol, self.fsum = n, g, col, rows, recv, rcol, fsum
-            self.plane, self.width, self.parts = plane, width, parts
+            self.plane, self.width, self.parts, self.whole = plane, width, parts, whole
+            self.paired = False
 
         def cols(self, core):
             return pl.ds(al(self.col + core * S, 128), self.width)
@@ -526,6 +516,8 @@
             return self.recv.at[pl.ds(al(5376 + i * self.rows, 16), k * self.rows), pl.ds(0, S)]
 
         def sem(self, stage):
+            if stage > 4:
+                return rs.at[self.n], rr.at[74 + self.whole * 3 + stage - 5]
             n = 0 if self.plane is not None and stage == 3 else self.n
             return rs.at[self.n], rr.at[n * 5 + stage]
 
@@ -540,37 +532,73 @@
             s, r = self.sem(0)
             send(src, self.rp(0, 4 * self.planes()), s, r, me, other).start()
 
+        def pair(self):
+            if not self.paired:
+                self.paired = True
+                self.got(0, self.rp(0, 4 * self.planes()))
+
+        def early(self, o, k=1):
+            return [] if self.whole is None else [ry.at[pl.ds(al(self.whole * 192 + o * 48, 16), k * 48)]]
+
+        def Y(self):
+            self.pair()
+            s, r = self.sem(5)
+            p = lax.rem(z + 1, 4) * 4
+            b = self.g.at[pl.ds(al(p * 48, 16), 192), self.cols(c)]
+            b[...] = total(b, self.rp(p, 4)).astype(BF)
+            send(b, self.early(0, 4)[0], s, r, zs[0], c).start()
+
         def A(self):
-            self.got(0, self.rp(0, 4 * self.planes()))
+            self.pair()
             s, r = self.sem(1)
 
             def one(i, _):
-                o = (i // 2) * 4 + far_base + lax.rem(i, 2) * step_k
+                p = i // 2 if self.whole is None else lax.rem(z + 2 + i // 2, 4)
+                o = p * 4 + far_base + lax.rem(i, 2) * step_k
                 b = self.mine(o)
                 b[...] = total(b, self.rp(o)).astype(BF)
-                send(b, self.ra(i), s, r, far, c).start()
+                send(b, self.ra(p * 2 + lax.rem(i, 2)), s, r, far, c).start()
                 return 0
 
-            lax.fori_loop(0, 2 * self.planes(), one, 0)
+            lax.fori_loop(0, 4 if self.whole is not None else 2 * self.planes(), one, 0)
+
+        def A0(self):
+            self.got(5, self.early(0, 4)[0])
+            s, r = self.sem(6)
+            for k in range(2):
+                o = far_base + k * step_k
+                b = self.mine(z * 4 + o)
+                b[...] = total(b, self.rp(z * 4 + o), *self.early(o)).astype(BF)
+                send(b, self.ra(z * 2 + k), s, r, far, c).start()
 
         def B(self):
-            self.got(1, self.ra(0, 2 * self.planes()))
+            n = 2 if self.whole is not None else self.planes()
+            self.got(1, self.ra(0, 2 * n))
             s, r = self.sem(2)
 
             def one(i, _):
-                o = i * 4 + near_xy
+                p = i if self.whole is None else lax.rem(z + 2 + i, 4)
+                o = p * 4 + near_xy
                 b = self.mine(o)
-                b[...] = total(b, self.rp(o), self.ra(i * 2 + 1 - my_k)).astype(BF)
-                send(b, self.rb(i), s, r, near, c).start()
+                b[...] = total(b, self.rp(o), self.ra(p * 2 + 1 - my_k)).astype(BF)
+                send(b, self.rb(p), s, r, near, c).start()
                 return 0
 
-            lax.fori_loop(0, self.planes(), one, 0)
+            lax.fori_loop(0, n, one, 0)
+
+        def B0(self):
+            self.got(6, self.ra(0, 2))
+            s, r = self.sem(7)
+            b = self.mine(z * 4 + near_xy)
+            t = total(b, self.rp(z * 4 + near_xy), self.ra(z * 2 + 1 - my_k), *self.early(near_xy))
+            b[...] = t.astype(BF)
+            send(b, self.rb(z), s, r, near, c).start()
 
         def Z(self):
-            self.got(2, self.rb(0, self.planes()))
+            self.got(2, self.rb(0, self.planes() if self.whole is None else 2))
             s, r = self.sem(3)
             if self.plane is None:
-                for k in range(3):
+                for k in range(0 if self.whole is None else 1, 3):
                     p = lax.rem(z + k + 1, 4)
                     b = self.mine(p * 4 + xy)
                     b[...] = total(b, self.rp(p * 4 + xy), self.ra(p * 2 + my_k), self.rb(p)).astype(BF)
@@ -581,9 +609,13 @@
                 send(b, self.rz(self.n - 1), s, r, zs[self.n - 1], c).start()
 
         def F(self):
-            self.got(3, self.rz(0, 3))
+            first = 0 if self.whole is None else 1
+            self.got(3, self.rz(0, 3 - first))
+            if first:
+                self.got(7, self.rb(0))
             o, p = (z * 4 + xy, z) if self.plane is None else (xy, 0)
-            t = total(self.mine(o), self.rp(o), self.ra(p * 2 + my_k), self.rb(p), self.rz(0), self.rz(1), self.rz(2))
+            last = [self.rz(k) for k in range(first, 3)] + self.early(xy)
+            t = total(self.mine(o), self.rp(o), self.ra(p * 2 + my_k), self.rb(p), *last)
             s, r = self.sem(4)
             if self.parts:
                 for i, k in enumerate(self.parts):
@@ -604,17 +636,18 @@
             if self.plane is None or self.n == 0:
                 self.got(4, self.fsum.at[:, pl.ds(0, self.width)])
 
+    early = {0: 0, 1: 1}
     con = {j: Red(j, gcon, 0, 192, con_r, j * 1344, fcon, plane=lax.rem(z + j, 4)) for j in range(4)}
-    exp = [Red(4 + k, wide, EXP + k * 768, 48, hidden, k * 768, fexp) for k in range(4)]
+    exp = [Red(4 + k, wide, EXP + k * 768, 48, hidden, k * 768, fexp, whole=early.get(k)) for k in range(4)]
     out = Red(8, wide, OUT, 48, cotn, 0, fout)
     ins = [
         Red(9 + k, gin, k * 768, 48, slope, k * 768, fin, parts=[q * D + k * 256 for q in range(3)]) for k in range(2)
     ]
-    ins.append(Red(11, gin, 1536, 48, slope, 1536, fin, width=256, parts=[512, D + 512]))
-    ins.append(Red(12, gin, 1792, 48, slope, 2048, fin, width=128, parts=[2 * D + 512]))
+    for k, first in enumerate((512, 2 * D + 512, D + 512)):
+        ins.append(Red(11 + k, gin, 1536 + (0, 256, 128)[k], 48, slope, 1536 + 256 * k, fin, width=128, parts=[first]))
     sums = {f"C{k}": con[k] for k in range(4)}
     sums.update({f"E{k}": exp[k] for k in range(4)})
-    sums.update({f"I{k}": ins[k] for k in range(4)})
+    sums.update({f"I{k}": ins[k] for k in range(5)})
     sums["O"] = out
 
     def reduce(ops):
@@ -647,7 +680,7 @@
     loose["lo"] = send_back
 
     def vsend(stage, src, dst, dp, seq):
-        return send(src, dst, rs.at[13 + stage], rr.at[65 + stage], dp, seq)
+        return send(src, dst, rs.at[14 + stage], rr.at[70 + stage], dp, seq)
 
     def v_partner():
         vout[...] = jnp.zeros_like(vout)
@@ -712,7 +745,7 @@
     def grad_con(i, _):
         p = al(lax.rem(z + i + 1, 4) * 768, 768)
         gcon[pl.ds(p, 768), :] = tn(hidden[:, pl.ds(p, 768)], bg[...]).astype(BF)
-        steps(i, [['P:C1'], ['P:C2'], ['P:C3', 'A:C1'], ['P:C0']])
+        steps(i, [['P:C1'], ['P:C2'], [], ['A:C1', 'P:C3']])
         return 0
 
     lax.fori_loop(0, 4, grad_con, 0)
@@ -722,7 +755,7 @@
         g = (nt(bg[...], wcon[cs, :]) * slope[:, cs].astype(F32)).astype(BF)
         slope[:, cs] = g
         ge[:, cs] = jnp.sum(g.astype(F32), axis=0, keepdims=True)
-        steps(i, [['A:C3', 'A:C2'], [], [], []])
+        steps(i, [[], ['A:C2'], [], ['A:C3', 'P:C0']])
         return 0
 
     lax.fori_loop(0, FF // 768, expand_back, 0)
@@ -739,7 +772,7 @@
         low = g.astype(BF)
         bg[r, :] = low
         gv[2:3, :] += jnp.sum(low.astype(F32), axis=0, keepdims=True)
-        steps(i, [['B:C1'], ['A:C0'], []])
+        steps(i, [['B:C1'], [], ['A:C0']])
         return 0
 
     lax.fori_loop(0, T // 256, first_back, 0)
@@ -749,19 +782,19 @@
     def grad_exp(i, _):
         cs = pl.ds(al(i * 768, 768), 768)
         wide[:, pl.ds(al(EXP + i * 768, 768), 768)] = tn(fl[...], slope[:, cs]).astype(BF)
-        steps(i, [['P:E0', 'B:C3'], ['P:E1', 'B:C2'], ['Z:C1', 'B:C0'], ['P:E3', 'Z:C3', 'A:E0']])
+        steps(i, [[], ['B:C2', 'P:E0'], ['P:E1', 'Z:C1', 'B:C3'], []])
         return 0
 
     lax.fori_loop(0, 4, grad_exp, 0)
     hg = cotr
     hg[...] = nt(bg[...], wide[:, OUT:EXP]).astype(BF)
-    reduce([])
+    reduce(['A:E0', 'Y:E0'])
     pieces[3].drain()
     wide[:, OUT:EXP] = tn(heads[...], bg[...]).astype(BF)
-    reduce(['P:O', 'A:E1', 'Z:C2', 'P:E2'])
-
-    tasks = [['A:E3'], ['A:O'], ['P:I0', 'B:E3', 'B:E0', 'Z:C0'], ['F:C0', 'B:E1'], ['Z:E0', 'A:I1'], ['Z:E1', 'vP', 'B:E2']]
-    after = [[], ['P:I1', 'Z:E3', 'A:E2', 'lo', 'B:O'], []]
+    reduce(['P:O', 'Y:E1', 'B:C0', 'A:E1', 'P:E2'])
+
+    tasks = [['Z:C3', 'A:O'], [], ['B:E0', 'Z:C2', 'Z:C0', 'B:O'], ['A:I0'], ['A:E3'], []]
+    after = [['A:E2', 'P:E3', 'P:I0'], ['B:E1'], ['P:I2', 'F:C0', 'Z:O', 'B:I0', 'P:I3', 'Z:E1', 'P:I4', 'P:I1']]
 
     def attend_back(h, _):
         cs = al(h * 384, 128)
@@ -814,7 +847,7 @@
         g = sg[r, :] + nt(proj[r, :], wide[:, IN:OUT])
         sg[r, :] = g
         ig_mine[r, :] = g.astype(BF)
-        steps(i, [['Z:O', 'A:I0', 'P:I2'], [], ['Z:E2', 'B:I1', 'P:I3', 'swg0', 'A:I3', 'swg1', 'F:E0', 'F:E3', 'F:O', 'B:I0', 'Z:I1', 'A:I2', 'vA', 'swg2', 'F:E2', 'Z:I0', 'B:I3', 'B:I2', 'Z:I3', 'vB', 'sel', 'Z:I2', 'F:I0', 'vZ', 'F:I3', 'F:E1', 'F:I1', 'F:I2', 'vF']])
+        steps(i, [['vP', 'A:I2', 'Z:E0', 'A:I3', 'B:E3'], ['B:E2', 'A:I4', 'A:I1'], ['A0:E1', 'Z:I0', 'Z:E3', 'Z:E2', 'swg2', 'B:I2', 'B:I3', 'B:I4', 'B:I1', 'lo', 'swg0', 'swg1', 'F:I0', 'Z:I2', 'Z:I3', 'Z:I4', 'vA', 'Z:I1', 'sel', 'F:O', 'A0:E0', 'vB', 'B0:E1', 'B0:E0', 'F:E1', 'F:E2', 'vZ', 'F:I3', 'F:E0', 'F:I4', 'F:E3', 'F:I2', 'F:I1', 'vF']])
         return 0
 
     lax.fori_loop(0, T // 256, input_rows, 0)
@@ -854,10 +887,10 @@
         VM((T, 3 * D), BF), VM((T, D), BF), VM((T, D), F32), VM((T, T), F32),
         VM((T, 2), F32), VM((T, D), BF), VM((T, D), BF), VM((T, FF), BF), VM((T, FF), BF),
         VM((2, T, T), BF), VM((T, D), BF),
-        VM((D, 3 * D), BF), VM((FF, D), BF), VM((5952, 384), BF), VM((8, D), F32), VM((1, FF), F32),
+        VM((D, 3 * D), BF), VM((FF, D), BF), VM((5952, 384), BF), VM((768, 384), BF), VM((8, D), F32), VM((1, FF), F32),
         VM((16, 8, 128), F32), VM((16, 8, 128), F32), VM((32, 8, 128), F32),
         VM(iw.shape, F32), VM(ow.shape, F32), VM(ew.shape, F32), VM(cw.shape, F32),
-        DMA((3, 2)), DMA((2, 3)), DMA((21,)), DMA((11,)), DMA((65,)), DMA((6,)), DMA((2,)), DMA((17,)), DMA((69,)), DMA((2,)),
+        DMA((3, 2)), DMA((2, 3)), DMA((21,)), DMA((11,)), DMA((65,)), DMA((6,)), DMA((2,)), DMA((18,)), DMA((80,)), DMA((2,)),
     ]
     return pl.pallas_call(
         fused_kernel,
@@ -1232,7 +1265,7 @@
         expand_bias,
     ]
     own = query_bias.shape[0]
-    vectors = [v.reshape(1, v.shape[0]) for v in vectors]
+    vectors = [v.reshape(1, own) for v in vectors[:8]] + [expand_bias]
     parts = fused_layer(
         tokens[0], time_embed, segments, input_weight, output_weight, expand_weight, contract_weight, vectors,
         cotangent[0],

time: 155 us -> 152 us (0.981)
  no operation moved by 1% of the time
where the time goes in v5:
time: 152 us
  Pallas kernels  151 us (99%)
    pallas_call x1, Pallas kernels, fused_layer(): pl.pallas_call(fused_kernel, out_shape=(sh((T, D), BF), sh((T, D), F32),...  146 us
    pallas_call x1, Pallas kernels, finish(): pl.pallas_call(finish_kernel, out_shape=[sh(v.shape, v.dtype) for v in bi...  5.39 us

profile of v5, /device:TPU:0, one launch (start us, length us, event | category | flops | bytes accessed | tf_op | source)
XLA Modules:
  0.0 152.2 jit_solution(5309027986766089750)
XLA Ops:
  0.7 145.9 %shard_map.280 = (bf16[768,768]{1,0:T(8,128)(2,1)}, f32[768,768]{1,0:T(8,128)}, f32[48,2304]{1,0:T(8,128)}, f32[48,768]{1,0:T(8,128)}, f32[48,3072]{1,0:T(8,128)...) custom-call(bf16[768,768]{1,0:T(8,128)(2,1)} %bitcast.21, bf16[768,768]{1,0:T(8,128)(2,1)} %bitcast.22, ...), custom_call_target="tpu_custom_call" | custom-call | tf_op jit(solution)/shard_map/pallas_call | solution.py:895
  146.6 5.4 %shard_map.281 = (bf16[768,768]{1,0:T(8,128)(2,1)}, f32[768,768]{1,0:T(8,128)}, f32[48,2304]{1,0:T(8,128)}, f32[48,768]{1,0:T(8,128)}, f32[48,3072]{1,0:T(8,128)...) custom-call(bf16[768,768]{1,0:T(8,128)(2,1)} %get-tuple-element.37.l, ...), custom_call_target="tpu_custom_call" | custom-call | tf_op jit(solution)/shard_map/pallas_call | solution.py:1250

commit v6 on v5

--- a/solution.py
+++ b/solution.py
@@ -842,21 +842,31 @@
 
     lax.fori_loop(0, pairs, attend_back, 0)
 
+    totals = [(fcon, gcon_o), (fexp, gexp_o), (fout, gout_o), (fin, gin_o)]
+    sum_out = [pltpu.make_async_copy(v, o, ls.at[17 + k]) for k, (v, o) in enumerate(totals)]
+
+    def first_totals():
+        for k, group in ((0, [con[0]]), (1, exp)):
+            for p in group:
+                p.end()
+            sum_out[k].start()
+
+    loose["totals"] = first_totals
+
     def input_rows(i, _):
         r = pl.ds(al(i * 256, 256), 256)
         g = sg[r, :] + nt(proj[r, :], wide[:, IN:OUT])
         sg[r, :] = g
         ig_mine[r, :] = g.astype(BF)
-        steps(i, [['vP', 'A:I2', 'Z:E0', 'A:I3', 'B:E3'], ['B:E2', 'A:I4', 'A:I1'], ['A0:E1', 'Z:I0', 'Z:E3', 'Z:E2', 'swg2', 'B:I2', 'B:I3', 'B:I4', 'B:I1', 'lo', 'swg0', 'swg1', 'F:I0', 'Z:I2', 'Z:I3', 'Z:I4', 'vA', 'Z:I1', 'sel', 'F:O', 'A0:E0', 'vB', 'B0:E1', 'B0:E0', 'F:E1', 'F:E2', 'vZ', 'F:I3', 'F:E0', 'F:I4', 'F:E3', 'F:I2', 'F:I1', 'vF']])
+        steps(i, [['vP', 'A:I2', 'Z:E0', 'A:I3', 'B:E3'], ['B:E2', 'A:I4', 'A:I1'], ['A0:E1', 'Z:I0', 'Z:E3', 'Z:E2', 'swg2', 'B:I2', 'B:I3', 'B:I4', 'B:I1', 'lo', 'swg0', 'swg1', 'F:I0', 'Z:I2', 'Z:I3', 'Z:I4', 'vA', 'Z:I1', 'sel', 'F:O', 'A0:E0', 'vB', 'B0:E1', 'B0:E0', 'F:E1', 'F:E2', 'vZ', 'F:I3', 'F:E0', 'F:I4', 'F:E3', 'F:I2', 'totals', 'F:I1', 'vF']])
         return 0
 
     lax.fori_loop(0, T // 256, input_rows, 0)
-    outs = [lo_done, ig_done, v_done]
-    for k, (v, o) in enumerate([(fcon, gcon_o), (fexp, gexp_o), (fout, gout_o), (fin, gin_o)]):
-        for p in [[con[0]], exp, [out], ins][k]:
+    outs = [lo_done, ig_done, v_done] + sum_out
+    for k, group in ((2, [out]), (3, ins)):
+        for p in group:
             p.end()
-        outs.append(pltpu.make_async_copy(v, o, ls.at[17 + k]))
-        outs[-1].start()
+        sum_out[k].start()
     for k in (1, 2, 3):
         con[k].end()
     swap_tok.wait_send()

time: 152 us -> 152 us (level)
  no operation moved by 1% of the time
where the time goes in v6:
time: 152 us
  Pallas kernels  151 us (99%)
    pallas_call x1, Pallas kernels, fused_layer(): pl.pallas_call(fused_kernel, out_shape=(sh((T, D), BF), sh((T, D), F32),...  146 us
    pallas_call x1, Pallas kernels, finish(): pl.pallas_call(finish_kernel, out_shape=[sh(v.shape, v.dtype) for v in bi...  5.39 us

profile of v6, /device:TPU:0, one launch (start us, length us, event | category | flops | bytes accessed | tf_op | source)
XLA Modules:
  0.0 152.1 jit_solution(10201799799410591965)
XLA Ops:
  0.7 145.9 %shard_map.280 = (bf16[768,768]{1,0:T(8,128)(2,1)}, f32[768,768]{1,0:T(8,128)}, f32[48,2304]{1,0:T(8,128)}, f32[48,768]{1,0:T(8,128)}, f32[48,3072]{1,0:T(8,128)...) custom-call(bf16[768,768]{1,0:T(8,128)(2,1)} %bitcast.21, bf16[768,768]{1,0:T(8,128)(2,1)} %bitcast.22, ...), custom_call_target="tpu_custom_call" | custom-call | tf_op jit(solution)/shard_map/pallas_call | solution.py:905
  146.5 5.4 %shard_map.281 = (bf16[768,768]{1,0:T(8,128)(2,1)}, f32[768,768]{1,0:T(8,128)}, f32[48,2304]{1,0:T(8,128)}, f32[48,768]{1,0:T(8,128)}, f32[48,3072]{1,0:T(8,128)...) custom-call(bf16[768,768]{1,0:T(8,128)(2,1)} %get-tuple-element.37.l, ...), custom_call_target="tpu_custom_call" | custom-call | tf_op jit(solution)/shard_map/pallas_call | solution.py:1260
